TPU v7x, 256 devices: a whole 4x4x8 slice. The times are simulated.
256 devices in a mesh: sub: 128 (over x, y, z), blk: 2 (over core).
Axes of the slice: x: 4, y: 4, z: 8, core: 2. Of those that a mesh axis runs over, the one named last changes fastest.
Arguments:
- basis: bfloat16 [65536, 256], P('sub'), may hold values from -6 to 6
- stiffness: bfloat16 [256, 1024, 1024], P('sub', 'blk')
- mass: bfloat16 [256, 1024, 1024], P('sub', 'blk')
- owner_rows: int32 [128, 128, 16], P('sub'), may hold values from 0 to 511
- counts: int32 [256], P('sub'), may hold values from 256 to 1024, as said below
Outputs:
- rotated: float32 [65536, 256], P(('sub', 'blk'))
- projected: float32 [256, 256], replicated
Inputs may be any that keep to these rules, and one draw needn't show every extreme that they name: `counts`: every count lies in 256 to 1024; at least one substructure has all 1024 slots live.
All inputs are finite; a program needn't handle non-finite values.
Results may differ from a plain program's by a relative error of at most 0.002.
Values may be sent and summed in bfloat16 or wider, within the bound.
No kernel may reach another device: no remote copies, remote signals or barrier semaphores. Data moves between devices by JAX's collectives and lax.ppermute only.
A program may use at most 64 MiB of HBM per device.

v0:
```python
import math

import jax
import jax.numpy as jnp
from jax import lax
from jax.sharding import PartitionSpec as P


def split_gram(left, image):
    upper = image.astype(jnp.bfloat16)
    rest = (image - upper.astype(jnp.float32)).astype(jnp.bfloat16)
    first = jnp.dot(left.T, upper, preferred_element_type=jnp.float32)
    return first + jnp.dot(left.T, rest, preferred_element_type=jnp.float32)


def per_device(basis, stiffness, mass, owner_rows, counts):
    n_sub = lax.axis_size("sub")
    me_sub = lax.axis_index("sub")
    me_blk = lax.axis_index("blk")
    rows_dev, width = basis.shape
    sub_dev, half, order = stiffness.shape
    cap = owner_rows.shape[2]
    cap_half = cap // 2
    table = owner_rows[0].T
    my_table = lax.dynamic_slice_in_dim(table, me_blk * cap_half, cap_half, 0)

    def arrange(received):
        rolled = jnp.roll(received, -me_sub, axis=1)
        return rolled.reshape(sub_dev, half, width)

    received = lax.all_to_all(basis[table], "sub", split_axis=1, concat_axis=1, tiled=True)
    local_basis = jnp.concatenate(
        [arrange(received[:cap_half]), arrange(received[cap_half:])], axis=1
    )
    slots = jnp.arange(order, dtype=jnp.int32)
    live = (slots[None, :] < counts[:, None])[:, :, None]
    local_basis = jnp.where(live, local_basis, jnp.zeros((), jnp.bfloat16))
    my_live = lax.dynamic_slice_in_dim(live, me_blk * half, half, 1)
    stiff_part = jnp.where(
        my_live,
        jnp.einsum("sij,sjr->sir", stiffness, local_basis, preferred_element_type=jnp.float32),
        0.0,
    ).astype(jnp.bfloat16)
    mass_part = jnp.where(
        my_live,
        jnp.einsum("sij,sjr->sir", mass, local_basis, preferred_element_type=jnp.float32),
        0.0,
    ).astype(jnp.bfloat16)

    def outgoing(part_rows):
        return jnp.roll(part_rows.reshape(cap_half, n_sub, width), me_sub, axis=1)

    def collect(returned):
        empty = jnp.zeros((rows_dev, width), jnp.float32)
        return empty.at[my_table].add(returned.astype(jnp.float32))

    own_basis = lax.dynamic_slice_in_dim(basis, me_blk * (rows_dev // 2), rows_dev // 2, 0)
    back_k, back_m = (
        lax.all_to_all(outgoing(stiff_part), "sub", split_axis=1, concat_axis=1, tiled=True),
        lax.all_to_all(outgoing(mass_part), "sub", split_axis=1, concat_axis=1, tiled=True),
    )
    image_k, image_m = (
        lax.psum_scatter(collect(back_k), "blk", scatter_dimension=0, tiled=True),
        lax.psum_scatter(collect(back_m), "blk", scatter_dimension=0, tiled=True),
    )
    gram_k = split_gram(own_basis, image_k)
    gram_m = split_gram(own_basis, image_m)
    gram_k, gram_m = lax.psum((gram_k, gram_m), ("sub", "blk"))
    gram_m = 0.5 * (gram_m + gram_m.T)
    lower = jnp.linalg.cholesky(gram_m)
    inverse = lax.linalg.triangular_solve(
        lower, jnp.eye(width, dtype=lower.dtype), left_side=True, lower=True
    )
    scale_rows = math.sqrt(rows_dev * n_sub)
    rotated = scale_rows * jnp.dot(image_k, inverse.T, precision=lax.Precision.HIGH)
    projected = jnp.dot(
        jnp.dot(inverse, gram_k, precision=lax.Precision.HIGHEST),
        inverse.T,
        precision=lax.Precision.HIGHEST,
    )
    return (rotated, projected)


def solution(mesh):
    return jax.shard_map(
        per_device,
        mesh=mesh,
        in_specs=(
            P("sub", None),
            P("sub", "blk", None),
            P("sub", "blk", None),
            P("sub", None, None),
            P("sub"),
        ),
        out_specs=(P(("sub", "blk"), None), P()),
        check_vma=False,
    )
```

profile of v0, /device:TPU:1, one launch (start us, length us, event | category | flops | bytes accessed | tf_op | source)
XLA Modules:
  0.0 478.7 jit_solution(7962032788862668469)
XLA Ops:
  8.0 7.6 %gather_fusion = bf16[2048,256]{1,0:T(8,128)(2,1)S(1)} fusion(bf16[512,256]{1,0:T(8,128)(2,1)} %param.7, s32[2048]{0:T(1024)S(1)} %fusion.38), kind=kCustom, calls=%fused_computation | custom fusion | bytes 2105344 | tf_op jit(solution)/shard_map/gather | solution.py:31
  15.7 1.5 copy.32
  17.2 16.3 %all-to-all-start = ((bf16[16,128,256]{2,0,1:T(8,128)(2,1)}), bf16[16,128,256]{2,0,1:T(8,128)(2,1)S(1)}, u32[]{:S(2)}, u32[]{:S(2)}) async-start(bf16[16,128,256]{2,0,1:T(8,128)(2,1)} %copy.32), calls=%async_computation | async-start | bytes 2097152 | tf_op jit(solution)/shard_map/all_to_all | solution.py:31
  33.7 30.2 %all-to-all-done = bf16[16,128,256]{2,0,1:T(8,128)(2,1)S(1)} async-done(((bf16[16,128,256]{2,0,1:T(8,128)(2,1)}), bf16[16,128,256]{2,0,1:T(8,128)(2,1)S(1)}, u32[]{:S(2)}, u32[]{:S(2)}) %all-to-all-start) | async-done | bytes 1048608 | tf_op jit(solution)/shard_map/all_to_all | solution.py:31
  65.9 1.4 fusion.3
  69.0 6.2 %all-to-all-start.1 = ((bf16[8,128,256]{2,0,1:T(8,128)(2,1)}), bf16[8,128,256]{2,0,1:T(8,128)(2,1)S(1)}, u32[]{:S(2)}, u32[]{:S(2)}) async-start(bf16[8,128,256]{2,0,1:T(8,128)(2,1)} %copy.37), calls=%async_computation.1 | async-start | bytes 1048576 | tf_op jit(solution)/shard_map/all_to_all | solution.py:59
  75.3 3.7 fusion.2
  79.0 1.2 copy.40
  80.2 12.4 %all-to-all-done.1 = bf16[8,128,256]{2,0,1:T(8,128)(2,1)S(1)} async-done(((bf16[8,128,256]{2,0,1:T(8,128)(2,1)}), bf16[8,128,256]{2,0,1:T(8,128)(2,1)S(1)}, u32[]{:S(2)}, u32[]{:S(2)}) %all-to-all-start.1) | async-done | bytes 524320 | tf_op jit(solution)/shard_map/all_to_all | solution.py:59
  93.5 6.7 %scatter_custom_fusion = f32[512,256]{1,0:T(8,128)} fusion(s32[1024]{0:T(1024)S(1)} %fusion.39, bf16[1024,256]{1,0:T(8,128)(2,1)} %bitcast.71, f32[]{:T(128)} %constant.110.clone.1), kind=kCustom, calls=%fused_computation.27 | custom fusion | flops 524288 | bytes 1048580 | tf_op jit(solution)/shard_map/scatter-add | solution.py:55
  101.2 23.4 %all_to_all.15 = bf16[8,128,256]{2,0,1:T(8,128)(2,1)S(1)} all-to-all(bf16[8,128,256]{2,0,1:T(8,128)(2,1)S(1)} %copy.41), channel_id=1, replica_groups=mesh['sub'=128,'blk'=2] {'sub'}, dimensions={1} | all-to-all | bytes 1048576 | tf_op jit(solution)/shard_map/all_to_all | solution.py:60
  124.7 6.9 %scatter_custom_fusion.1 = f32[512,256]{1,0:T(8,128)} fusion(s32[1024]{0:T(1024)S(1)} %fusion.39, bf16[1024,256]{1,0:T(8,128)(2,1)S(1)} %bitcast.69, f32[]{:T(128)} %constant.110.clone.1), kind=kCustom, calls=%fused_computation.25 | custom fusion | flops 524288 | bytes 1048580 | tf_op jit(solution)/shard_map/scatter-add | solution.py:55
  131.7 1.2 fusion.23
  132.9 2.0 convolution_add_fusion
  134.9 8.0 %reduce-scatter.5.cloned.1.call-done = f32[256,256]{1,0:T(8,128)} async-done(((f32[512,256]{1,0:T(8,128)}), f32[256,256]{1,0:T(8,128)}) %reduce-scatter.5.cloned.1.call-update) | async-done | bytes 262160 | tf_op jit(solution)/shard_map/reduce_scatter | solution.py:64
  144.1 2.0 convolution_add_fusion.1
  146.1 257.9 %all-reduce.4.cloned.1.call-done = (f32[256,256]{0,1:T(8,128)}, f32[256,256]{1,0:T(8,128)}) async-done(((f32[256,256]{0,1:T(8,128)}, f32[256,256]{1,0:T(8,128)}), (f32[256,256]{0,1:T(8,128)}, f32[256,256]{1,0:T(8,128)})) %all-reduce.4.cloned.1.call-update) | async-done | bytes 524304 | tf_op jit(solution)/shard_map/psum | solution.py:68
  406.3 11.7 %cholesky.50 = f32[128,128]{1,0:T(8,128)S(1)} custom-call(f32[128,128]{1,0:T(8,128)S(1)} %cholesky.118), custom_call_target="Cholesky" | custom-call | tf_op jit(solution)/shard_map/jit(cholesky)/cholesky | solution.py:70
  418.1 9.8 %custom-call.14 = f32[1,128,128]{1,2,0:T(8,128)S(1)} custom-call(f32[1,128,128]{2,1,0:T(8,128)S(1)} %get-tuple-element.28), custom_call_target="InvertDiagBlocksLowerTriangular" | custom-call | tf_op jit(solution)/shard_map/jit(cholesky)/cholesky | solution.py:70
  428.4 11.7 %cholesky.105 = f32[128,128]{1,0:T(8,128)S(1)} custom-call(f32[128,128]{1,0:T(8,128)S(1)} %convolution_subtract_fusion.1), custom_call_target="Cholesky" | custom-call | tf_op jit(solution)/shard_map/jit(cholesky)/cholesky | solution.py:70
  442.8 5.4 %while.1 = (s32[]{:T(128)}, f32[256,256]{1,0:T(8,128)S(1)}, s32[2,2]{1,0:T(2,128)S(1)}, f32[2,128,128]{2,1,0:T(8,128)}, s32[]{:T(128)}) while((s32[]{:T(128)}, f32[256,256]{1,0:T(8,128)S(1)}, s32[2,2]{1,0:T(2,128)S(1)}, f32[2,128,128]{2,1,0:T(8,128)}, s32[]{:T(128)}) %tuple.29), condition=%wide.while_cond, body=%wide.while_body.sunk | while | flops 2 | bytes 132705 | solution.py:71
  443.6 2.0 bitcast_dynamic-update-slice_fusion.2
  446.2 2.0 bitcast_dynamic-update-slice_fusion.2
  448.2 20.5 %custom-call.15 = f32[2,128,128]{1,2,0:T(8,128)S(1)} custom-call(f32[2,128,128]{2,1,0:T(8,128)} %get-tuple-element.10), custom_call_target="InvertDiagBlocksLowerTriangular" | custom-call | tf_op jit(solution)/shard_map/triangular_solve | solution.py:71
  (68 shorter events, 16.7 us)
Async XLA Ops:
  7.2 58.8 %copy-start = (bf16[2,512,1024]{2,1,0:T(8,128)(2,1)S(1)}, bf16[2,512,1024]{2,1,0:T(8,128)(2,1)}, u32[]{:S(2)}) copy-start(bf16[2,512,1024]{2,1,0:T(8,128)(2,1)} %param.8) | copy-start | bytes 6291460
  15.7 17.9 %copy-start.8 = (s32[2]{0:T(128)S(1)}, s32[2]{0:T(128)}, u32[]{:S(2)}) copy-start(s32[2]{0:T(128)} %param.11) | copy-start | bytes 28
  17.2 46.6 %all-to-all-start = ((bf16[16,128,256]{2,0,1:T(8,128)(2,1)}), bf16[16,128,256]{2,0,1:T(8,128)(2,1)S(1)}, u32[]{:S(2)}, u32[]{:S(2)}) async-start(bf16[16,128,256]{2,0,1:T(8,128)(2,1)} %copy.32), calls=%async_computation | async-start | bytes 2097152 | tf_op jit(solution)/shard_map/all_to_all | solution.py:31
  64.9 0.8 copy-start.3
  65.0 1.0 copy-start.5
  67.3 7.9 %copy-start.7 = (s32[1,128,16]{1,2,0:T(8,128)S(1)}, s32[1,128,16]{1,2,0:T(8,128)}, u32[]{:S(2)}) copy-start(s32[1,128,16]{1,2,0:T(8,128)} %param.10) | copy-start | bytes 24580
  67.9 7.4 %copy-start.4 = (bf16[8,128,256]{2,1,0:T(8,128)(2,1)S(1)}, bf16[8,128,256]{2,1,0:T(8,128)(2,1)}, u32[]{:S(2)}) copy-start(bf16[8,128,256]{2,1,0:T(8,128)(2,1)} %copy-done.3) | copy-start | bytes 1572868
  69.0 23.6 %all-to-all-start.1 = ((bf16[8,128,256]{2,0,1:T(8,128)(2,1)}), bf16[8,128,256]{2,0,1:T(8,128)(2,1)S(1)}, u32[]{:S(2)}, u32[]{:S(2)}) async-start(bf16[8,128,256]{2,0,1:T(8,128)(2,1)} %copy.37), calls=%async_computation.1 | async-start | bytes 1048576 | tf_op jit(solution)/shard_map/all_to_all | solution.py:59
  75.2 56.5 %reduce-scatter.3.cloned.1.call-start = ((), (), s32[]{:S(2)}) async-start(), calls=%async_computation.5 | async-start | bytes 786432 | tf_op jit(solution)/shard_map/reduce_scatter | solution.py:63
  100.3 42.6 %reduce-scatter.5.cloned.1.call-start = ((), (), s32[]{:S(2)}) async-start(), calls=%async_computation.6 | async-start | bytes 786432 | tf_op jit(solution)/shard_map/reduce_scatter | solution.py:64
  101.2 30.5 %copy-start.1 = (bf16[512,256]{1,0:T(8,128)(2,1)S(1)}, bf16[512,256]{1,0:T(8,128)(2,1)}, u32[]{:S(2)}) copy-start(bf16[512,256]{1,0:T(8,128)(2,1)} %param.7) | copy-start | bytes 786436
  131.7 272.4 %all-reduce.4.cloned.1.call-start = ((), (), s32[]{:S(2)}) async-start(), calls=%async_computation.7 | async-start | bytes 1048576 | tf_op jit(solution)/shard_map/psum | solution.py:68
  406.2 63.3 %copy-start.6 = (f32[256,256]{1,0:T(8,128)S(1)}, f32[256,256]{1,0:T(8,128)}, u32[]{:S(2)}) copy-start(f32[256,256]{1,0:T(8,128)} %get-tuple-element.20) | copy-start | bytes 786436
  428.1 43.0 %copy-start.2 = (f32[256,256]{1,0:T(8,128)S(1)}, f32[256,256]{1,0:T(8,128)}, u32[]{:S(2)}) copy-start(f32[256,256]{1,0:T(8,128)} %reduce-scatter.3.cloned.1.call-done) | copy-start | bytes 786436
Sparse Core Ops, SparseCore 0:
  100.4 10.3 reduce-scatter.2
  131.8 11.0 reduce-scatter.4
  149.1 254.8 all-reduce.3
where the time goes:
time: 480 us; the launch traced here: 479 us
  waiting for transfers between devices  309 us (64%)
  other arithmetic  72.2 us (15%)
  blocking collectives  23.4 us (5%)
  starting transfers between devices  22.8 us (5%)
  local copies, waits for them, and re-layouts  20.8 us (4%)
  between operations  15.5 us (3%)
  matrix products  15.2 us (3%)
    psum x1, waiting for transfers between devices, per_device(): gram_k, gram_m = lax.psum((gram_k, gram_m), ('sub', 'blk'))  258 us
    another operation x7, other arithmetic, per_device(): lower = jnp.linalg.cholesky(gram_m)  34.6 us
    all_to_all x1, waiting for transfers between devices, per_device(): lax.all_to_all(basis[table], 'sub', split_axis=1, concat_axis=1, tiled=True)  30.2 us
    all_to_all x1, blocking collectives, per_device(): lax.all_to_all(outgoing(mass_part), 'sub', split_axis=1, concat_axis=1, t...  23.4 us
    another operation x3, other arithmetic, per_device(): lax.linalg.triangular_solve(lower, jnp.eye(width, dtype=lower.dtype), lef...  20.5 us
    all_to_all x1, starting transfers between devices, per_device(): lax.all_to_all(basis[table], 'sub', split_axis=1, concat_axis=1, tiled=True)  16.3 us
    scatter-add x2, other arithmetic, collect(): return empty.at[my_table].add(returned.astype(jnp.float32))  13.6 us
    all_to_all x1, waiting for transfers between devices, per_device(): lax.all_to_all(outgoing(stiff_part), 'sub', split_axis=1, concat_axis=1,...  12.4 us
  transfers between devices with their start and end apart: 5, of which 4 were waited for; matrix products, arithmetic and copies ran while one was open for 3% of the time, Pallas kernels for 0%

commit v1 on v0

v1 whole, which is shorter than its diff:
```python
import math

import jax
import jax.numpy as jnp
from jax import lax
from jax.sharding import PartitionSpec as P

SWAP = ((0, 1), (1, 0))


def select_rows(index, count):
    places = lax.broadcasted_iota(jnp.int32, (index.shape[0], count), 1)
    return (index[:, None] == places).astype(jnp.bfloat16)


def sum_over_devices(parts, me_blk):
    n, rows, width = parts.shape
    n_sub = lax.axis_size("sub")
    halves = parts.reshape(n, 2, rows // 2, width)
    mine = lax.dynamic_index_in_dim(halves, me_blk, 1, keepdims=False)
    theirs = lax.dynamic_index_in_dim(halves, 1 - me_blk, 1, keepdims=False)
    mine = mine + lax.ppermute(theirs, "blk", SWAP)
    pieces = mine.reshape(n_sub, n * rows // 2 // n_sub, width)
    pieces = lax.all_to_all(pieces, "sub", split_axis=0, concat_axis=0, tiled=True)
    total = jnp.sum(pieces, axis=0)
    spread = jnp.broadcast_to(total[None], pieces.shape)
    mine = lax.all_to_all(spread, "sub", split_axis=0, concat_axis=0, tiled=True)
    mine = mine.reshape(n, rows // 2, width)
    other = lax.ppermute(mine, "blk", SWAP)
    low = jnp.where(me_blk == 0, mine, other)
    high = jnp.where(me_blk == 0, other, mine)
    return jnp.concatenate([low, high], axis=1)


def per_device(basis, stiffness, mass, owner_rows, counts):
    n_sub = lax.axis_size("sub")
    me_sub = lax.axis_index("sub")
    me_blk = lax.axis_index("blk")
    rows_dev, width = basis.shape
    sub_dev, half, order = stiffness.shape
    cap = owner_rows.shape[2]
    cap_half = cap // 2
    table = lax.dynamic_slice_in_dim(owner_rows[0], me_blk * cap_half, cap_half, 1)
    picks = select_rows(table.reshape(-1), rows_dev)

    sent = jnp.dot(picks, basis, preferred_element_type=jnp.float32).astype(jnp.bfloat16)
    received = lax.all_to_all(
        sent.reshape(n_sub, cap_half, width), "sub", split_axis=0, concat_axis=0, tiled=True
    )
    mine = jnp.roll(received, -me_sub, axis=0).transpose(1, 0, 2).reshape(sub_dev, half, width)
    slots = me_blk * half + jnp.arange(half, dtype=jnp.int32)
    my_live = (slots[None, :] < counts[:, None])[:, :, None]
    mine = jnp.where(my_live, mine, jnp.zeros((), jnp.bfloat16))
    other = lax.ppermute(mine, "blk", SWAP)
    low = jnp.where(me_blk == 0, mine, other)
    high = jnp.where(me_blk == 0, other, mine)
    local_basis = jnp.concatenate([low, high], axis=1)

    def product(matrix):
        full = jnp.einsum("sij,sjr->sir", matrix, local_basis, preferred_element_type=jnp.float32)
        return jnp.where(my_live, full, 0.0).astype(jnp.bfloat16)

    stiff_part = product(stiffness)
    mass_part = product(mass)

    def gram(part):
        return jnp.einsum("sir,sic->rc", mine, part, preferred_element_type=jnp.float32)

    grams = sum_over_devices(jnp.stack([gram(stiff_part), gram(mass_part)]), me_blk)
    gram_k, gram_m = grams[0], grams[1]

    outgoing = stiff_part.reshape(cap_half, n_sub, width).transpose(1, 0, 2)
    back = lax.all_to_all(
        jnp.roll(outgoing, me_sub, axis=0), "sub", split_axis=0, concat_axis=0, tiled=True
    )
    image = jnp.einsum(
        "tr,tc->rc", picks, back.reshape(-1, width), preferred_element_type=jnp.float32
    ).reshape(2, rows_dev // 2, width)
    image_k = lax.dynamic_index_in_dim(image, me_blk, 0, keepdims=False) + lax.ppermute(
        lax.dynamic_index_in_dim(image, 1 - me_blk, 0, keepdims=False), "blk", SWAP
    )

    gram_m = 0.5 * (gram_m + gram_m.T)
    lower = jnp.linalg.cholesky(gram_m)
    inverse = lax.linalg.triangular_solve(
        lower, jnp.eye(width, dtype=lower.dtype), left_side=True, lower=True
    )
    scale_rows = math.sqrt(rows_dev * n_sub)
    rotated = scale_rows * jnp.dot(image_k, inverse.T, precision=lax.Precision.HIGH)
    projected = jnp.dot(
        jnp.dot(inverse, gram_k, precision=lax.Precision.HIGHEST),
        inverse.T,
        precision=lax.Precision.HIGHEST,
    )
    return (rotated, projected)


def solution(mesh):
    return jax.shard_map(
        per_device,
        mesh=mesh,
        in_specs=(
            P("sub", None),
            P("sub", "blk", None),
            P("sub", "blk", None),
            P("sub", None, None),
            P("sub"),
        ),
        out_specs=(P(("sub", "blk"), None), P()),
        check_vma=False,
    )
```

time: 480 us -> 193 us (0.40)
  waiting for transfers between devices: 309 us -> 47.5 us
  starting transfers between devices: 22.8 us -> 39.5 us
  other arithmetic: 72.2 us -> 58.7 us
  between operations: 15.5 us -> 2.33 us
  local copies, waits for them, and re-layouts: 20.8 us -> 11.5 us
    psum x1 -> x0, waiting for transfers between devices: 258 us -> none  [per_device(): gram_k, gram_m = lax.psum((gram_k, gram_m), ('sub', 'blk'))]
    scatter-add x2 -> x0, other arithmetic: 13.6 us -> none  [collect(): return empty.at[my_table].add(returned.astype(jnp.float32))]
    gather x2 -> x0, local copies, waits for them, and re-layouts: 9.17 us -> none  [per_device(): basis[table]]
    ppermute x0 -> x4, starting transfers between devices: none -> 8.68 us  [the longest x1 3.41 us: per_device(): lax.ppermute(lax.dynamic_index_in_dim(image, 1 - me_blk, 0, keepdims=Fals...]
    all_to_all x2 -> x3, starting transfers between devices: 22.5 us -> 30.8 us  [the longest x1 16.3 us: per_device(): lax.all_to_all(sent.reshape(n_sub, cap_half, width), 'sub', split_axis=0,...]
    reduce_scatter x2 -> x0, waiting for transfers between devices: 8.02 us -> none  [the longest x1 8 us: per_device(): lax.psum_scatter(collect(back_m), 'blk', scatter_dimension=0, tiled=True)]
    dot_general x6 -> x5, matrix products: 11.4 us -> 7.53 us  [the longest x2 4.02 us: gram(): jnp.einsum('sir,sic->rc', mine, part, preferred_element_type=jnp.float32)]
    all_to_all x2 -> x3, waiting for transfers between devices: 42.6 us -> 44.6 us  [the longest x1 19 us: per_device(): lax.all_to_all(sent.reshape(n_sub, cap_half, width), 'sub', split_axis=0,...]
  transfers between devices with their start and end apart: 5 -> 7, of which waited for: 4 -> 5; matrix products, arithmetic and copies ran while one was open for 3% -> 35% of each run, Pallas kernels for 0% -> 0%
where the time goes in v1:
time: 193 us; the launch traced here: 192 us
  other arithmetic  58.7 us (30%)
  waiting for transfers between devices  47.5 us (25%)
  starting transfers between devices  39.5 us (20%)
  blocking collectives  19.9 us (10%)
  matrix products  12.4 us (6%)
  local copies, waits for them, and re-layouts  11.5 us (6%)
  between operations  2.33 us (1%)
    another operation x6, other arithmetic, per_device(): lower = jnp.linalg.cholesky(gram_m)  34 us
    another operation x3, other arithmetic, per_device(): lax.linalg.triangular_solve(lower, jnp.eye(width, dtype=lower.dtype), lef...  20.5 us
    all_to_all x1, blocking collectives, sum_over_devices(): lax.all_to_all(pieces, 'sub', split_axis=0, concat_axis=0, tiled=True)  19.9 us
    all_to_all x1, waiting for transfers between devices, per_device(): lax.all_to_all(sent.reshape(n_sub, cap_half, width), 'sub', split_axis=0,...  19 us
    all_to_all x1, starting transfers between devices, per_device(): lax.all_to_all(sent.reshape(n_sub, cap_half, width), 'sub', split_axis=0,...  16.3 us
    all_to_all x1, waiting for transfers between devices, per_device(): lax.all_to_all(jnp.roll(outgoing, me_sub, axis=0), 'sub', split_axis=0, c...  14.7 us
    all_to_all x1, waiting for transfers between devices, sum_over_devices(): lax.all_to_all(spread, 'sub', split_axis=0, concat_axis=0, tiled=True)  10.9 us
    all_to_all x1, starting transfers between devices, sum_over_devices(): lax.all_to_all(spread, 'sub', split_axis=0, concat_axis=0, tiled=True)  7.29 us
  transfers between devices with their start and end apart: 7, of which 5 were waited for; matrix products, arithmetic and copies ran while one was open for 35% of the time, Pallas kernels for 0%

profile of v1, /device:TPU:1, one launch (start us, length us, event | category | flops | bytes accessed | tf_op | source)
XLA Modules:
  0.0 192.0 jit_solution(18343626215941306401)
XLA Ops:
  1.7 2.3 %fusion.6 = bf16[128,8,256]{2,1,0:T(8,128)(2,1)} fusion(bf16[512,256]{1,0:T(8,128)(2,1)} %param.7, s32[1024]{0:T(1024)S(1)} %eq.33), kind=kOutput, calls=%fused_computation.11 | convolution fusion | flops 269221888 | bytes 790528 | tf_op jit(solution)/shard_map/dot_general | solution.py:46
  4.0 16.3 %all-to-all-start = ((bf16[128,8,256]{2,1,0:T(8,128)(2,1)}), bf16[128,8,256]{2,1,0:T(8,128)(2,1)S(1)}, u32[]{:S(2)}, u32[]{:S(2)}) async-start(bf16[128,8,256]{2,1,0:T(8,128)(2,1)} %fusion.6), calls=%async_computation | async-start | bytes 1048576 | tf_op jit(solution)/shard_map/all_to_all | solution.py:47
  20.4 19.0 %all-to-all-done = bf16[128,8,256]{2,1,0:T(8,128)(2,1)S(1)} async-done(((bf16[128,8,256]{2,1,0:T(8,128)(2,1)}), bf16[128,8,256]{2,1,0:T(8,128)(2,1)S(1)}, u32[]{:S(2)}, u32[]{:S(2)}) %all-to-all-start) | async-done | bytes 524320 | tf_op jit(solution)/shard_map/all_to_all | solution.py:47
  40.2 2.6 %collective-permute-start = (bf16[2,512,256]{1,2,0:T(8,128)(2,1)S(1)}, bf16[2,512,256]{1,2,0:T(8,128)(2,1)}, u32[]{:S(2)}, u32[]{:S(2)}) collective-permute-start(bf16[2,512,256]{1,2,0:T(8,128)(2,1)S(1)} %broadcast_select_fusion), channel_id=1, source_target_pairs={{0,1},{1,0},{2,3},{3,2},{4,5},{5,4},{6,7},{7,6},{8,9},{9,8},{10,11... | collective-permute-start | bytes 1572872 | tf_op jit(solution)/shard_map/ppermute | solution.py:54
  42.8 1.7 collective-permute-done
  46.5 3.7 %convolution_bitcast_fusion = f32[1,2,128,256]{3,2,1,0:T(8,128)} fusion(bf16[2,128,512,2]{2,1,0,3:T(8,128)(2,1)S(1)} %bitcast.96, bf16[2,512,1024]{2,1,0:T(8,128)(2,1)} %param.9, bf16[2,512,256]{1,2,0:T(8,128)(2,1)} %copy-done.3, bf16[2,512,256]{1,2,0:T(8,128)(2,1)} %copy-done.2, pred[2,512]{1,0:T(4,128)(4,1)S(1)} %broadcast_compare_fusion), kind=kOutput, calls=%fused_computation.14 | convolution fusion | flops 673710080 | bytes 3933184 | tf_op jit(solution)/shard_map/sir,sic->rc/dot_general | solution.py:67
  52.0 1.2 collective-permute-done.2
  54.2 19.9 %all_to_all.20 = f32[128,2,256]{2,1,0:T(2,128)S(1)} all-to-all(f32[128,2,256]{2,1,0:T(2,128)S(1)} %reshape.114), channel_id=1, replica_groups=mesh['sub'=128,'blk'=2] {'sub'}, dimensions={0} | all-to-all | bytes 524288 | tf_op jit(solution)/shard_map/all_to_all | solution.py:24
  75.1 7.3 %all-to-all-start.3 = ((f32[128,2,256]{2,1,0:T(2,128)}), f32[128,2,256]{2,1,0:T(2,128)}, u32[]{:S(2)}, u32[]{:S(2)}) async-start(f32[128,2,256]{2,1,0:T(2,128)} %broadcast_in_dim.43), calls=%async_computation.3 | async-start | bytes 524288 | tf_op jit(solution)/shard_map/all_to_all | solution.py:27
  84.1 10.9 %all-to-all-done.3 = f32[128,2,256]{2,1,0:T(2,128)} async-done(((f32[128,2,256]{2,1,0:T(2,128)}), f32[128,2,256]{2,1,0:T(2,128)}, u32[]{:S(2)}, u32[]{:S(2)}) %all-to-all-start.3) | async-done | bytes 262176 | tf_op jit(solution)/shard_map/all_to_all | solution.py:27
  95.0 7.2 %all-to-all-start.1 = ((bf16[128,8,256]{2,1,0:T(8,128)(2,1)}), bf16[128,8,256]{2,1,0:T(8,128)(2,1)S(1)}, u32[]{:S(2)}, u32[]{:S(2)}) async-start(bf16[128,8,256]{2,1,0:T(8,128)(2,1)} %copy.32), calls=%async_computation.1 | async-start | bytes 1048576 | tf_op jit(solution)/shard_map/all_to_all | solution.py:73
  102.3 1.1 reshape.115
  103.5 2.2 %collective-permute-start.3 = (f32[2,128,256]{1,2,0:T(8,128)S(1)}, f32[2,128,256]{1,2,0:T(8,128)S(1)}, u32[]{:S(2)}, u32[]{:S(2)}) collective-permute-start(f32[2,128,256]{1,2,0:T(8,128)S(1)} %copy.36), channel_id=1, source_target_pairs={{0,1},{1,0},{2,3},{3,2},{4,5},{5,4},{6,7},{7,6},{8,9},{9,8},{10,11... | collective-permute-start | bytes 786440 | tf_op jit(solution)/shard_map/ppermute | solution.py:29
  105.8 14.7 %all-to-all-done.1 = bf16[128,8,256]{2,1,0:T(8,128)(2,1)S(1)} async-done(((bf16[128,8,256]{2,1,0:T(8,128)(2,1)}), bf16[128,8,256]{2,1,0:T(8,128)(2,1)S(1)}, u32[]{:S(2)}, u32[]{:S(2)}) %all-to-all-start.1) | async-done | bytes 524320 | tf_op jit(solution)/shard_map/all_to_all | solution.py:73
  121.7 3.4 %collective-permute-start.1 = (f32[256,256]{1,0:T(8,128)}, f32[256,256]{1,0:T(8,128)}, u32[]{:S(2)}, u32[]{:S(2)}) collective-permute-start(f32[256,256]{1,0:T(8,128)} %dynamic-slice_bitcast_fusion), channel_id=1, source_target_pairs={{0,1},{1,0},{2,3},{3,2},{4,5},{5,4},{6,7},{7,6},{8,9},{9,8},{10,11... | collective-permute-start | bytes 786440 | tf_op jit(solution)/shard_map/ppermute | solution.py:79
  125.6 11.7 %cholesky.50 = f32[128,128]{1,0:T(8,128)S(1)} custom-call(f32[128,128]{1,0:T(8,128)S(1)} %cholesky.118), custom_call_target="Cholesky" | custom-call | tf_op jit(solution)/shard_map/jit(cholesky)/cholesky | solution.py:84
  137.4 9.8 %custom-call.14 = f32[1,128,128]{1,2,0:T(8,128)S(1)} custom-call(f32[1,128,128]{2,1,0:T(8,128)S(1)} %get-tuple-element.28), custom_call_target="InvertDiagBlocksLowerTriangular" | custom-call | tf_op jit(solution)/shard_map/jit(cholesky)/cholesky | solution.py:84
  147.7 11.7 %cholesky.105 = f32[128,128]{1,0:T(8,128)S(1)} custom-call(f32[128,128]{1,0:T(8,128)S(1)} %convolution_subtract_fusion.1), custom_call_target="Cholesky" | custom-call | tf_op jit(solution)/shard_map/jit(cholesky)/cholesky | solution.py:84
  161.5 5.5 %while.1 = (s32[]{:T(128)}, f32[256,256]{1,0:T(8,128)S(1)}, s32[2,2]{1,0:T(2,128)S(1)}, f32[2,128,128]{2,1,0:T(8,128)}, s32[]{:T(128)}) while((s32[]{:T(128)}, f32[256,256]{1,0:T(8,128)S(1)}, s32[2,2]{1,0:T(2,128)S(1)}, f32[2,128,128]{2,1,0:T(8,128)}, s32[]{:T(128)}) %tuple.30), condition=%wide.while_cond, body=%wide.while_body.sunk | while | flops 2 | bytes 132705 | solution.py:85
  162.4 2.0 %bitcast_dynamic-update-slice_fusion.2 = f32[2,128,128]{2,1,0:T(8,128)} fusion(f32[2,128,128]{2,1,0:T(8,128)} %get-tuple-element.70, s32[]{:T(128)} %get-tuple-element.67, f32[256,256]{1,0:T(8,128)S(1)} %get-tuple-element.73, s32[]{:T(128)} %bitcast.93, s32[]{:T(128)} %bitcast.94), kind=kLoop, calls=%fused_computation.clone.1 | loop fusion | bytes 132608 | tf_op jit(solution)/shard_map/triangular_solve
  165.0 2.0 %bitcast_dynamic-update-slice_fusion.2 = f32[2,128,128]{2,1,0:T(8,128)} fusion(f32[2,128,128]{2,1,0:T(8,128)} %get-tuple-element.70, s32[]{:T(128)} %get-tuple-element.67, f32[256,256]{1,0:T(8,128)S(1)} %get-tuple-element.73, s32[]{:T(128)} %bitcast.93, s32[]{:T(128)} %bitcast.94), kind=kLoop, calls=%fused_computation.clone.1 | loop fusion | bytes 132608 | tf_op jit(solution)/shard_map/triangular_solve
  167.0 20.5 %custom-call.15 = f32[2,128,128]{1,2,0:T(8,128)S(1)} custom-call(f32[2,128,128]{2,1,0:T(8,128)} %get-tuple-element.10), custom_call_target="InvertDiagBlocksLowerTriangular" | custom-call | tf_op jit(solution)/shard_map/triangular_solve | solution.py:85
  188.8 1.1 fusion.30
  189.9 2.1 %convolution_multiply_fusion = f32[256,256]{1,0:T(8,128)} fusion(f32[256,256]{1,0:T(8,128)} %collective-permute-done.1, f32[2,256,256]{2,1,0:T(8,128)} %copy-done.1, s32[]{:T(128)S(6)} %select_n.70, f32[128,256]{1,0:T(8,128)S(1)} %fusion.34, f32[128,256]{1,0:T(8,128)S(1)} %fusion.31), kind=kOutput, calls=%fused_computation.13 | convolution fusion | flops 100859904 | bytes 1048580 | tf_op jit(solution)/shard_map/dot_general | solution.py:89
  (63 shorter events, 15.0 us)
Async XLA Ops:
  0.6 45.0 %copy-start = (bf16[2,512,1024]{2,1,0:T(8,128)(2,1)S(1)}, bf16[2,512,1024]{2,1,0:T(8,128)(2,1)}, u32[]{:S(2)}) copy-start(bf16[2,512,1024]{2,1,0:T(8,128)(2,1)} %param.8) | copy-start | bytes 6291460
  0.6 19.7 %copy-start.4 = (s32[2]{0:T(128)S(1)}, s32[2]{0:T(128)}, u32[]{:S(2)}) copy-start(s32[2]{0:T(128)} %param.11) | copy-start | bytes 28
  4.0 35.5 %all-to-all-start = ((bf16[128,8,256]{2,1,0:T(8,128)(2,1)}), bf16[128,8,256]{2,1,0:T(8,128)(2,1)S(1)}, u32[]{:S(2)}, u32[]{:S(2)}) async-start(bf16[128,8,256]{2,1,0:T(8,128)(2,1)} %fusion.6), calls=%async_computation | async-start | bytes 1048576 | tf_op jit(solution)/shard_map/all_to_all | solution.py:47
  40.2 4.2 %collective-permute-start = (bf16[2,512,256]{1,2,0:T(8,128)(2,1)S(1)}, bf16[2,512,256]{1,2,0:T(8,128)(2,1)}, u32[]{:S(2)}, u32[]{:S(2)}) collective-permute-start(bf16[2,512,256]{1,2,0:T(8,128)(2,1)S(1)} %broadcast_select_fusion), channel_id=1, source_target_pairs={{0,1},{1,0},{2,3},{3,2},{4,5},{5,4},{6,7},{7,6},{8,9},{9,8},{10,11... | collective-permute-start | bytes 1572872 | tf_op jit(solution)/shard_map/ppermute | solution.py:54
  45.6 0.8 copy-start.2
  45.6 1.0 copy-start.3
  51.5 1.6 collective-permute-start.2
  75.1 19.9 %all-to-all-start.3 = ((f32[128,2,256]{2,1,0:T(2,128)}), f32[128,2,256]{2,1,0:T(2,128)}, u32[]{:S(2)}, u32[]{:S(2)}) async-start(f32[128,2,256]{2,1,0:T(2,128)} %broadcast_in_dim.43), calls=%async_computation.3 | async-start | bytes 524288 | tf_op jit(solution)/shard_map/all_to_all | solution.py:27
  95.0 25.4 %all-to-all-start.1 = ((bf16[128,8,256]{2,1,0:T(8,128)(2,1)}), bf16[128,8,256]{2,1,0:T(8,128)(2,1)S(1)}, u32[]{:S(2)}, u32[]{:S(2)}) async-start(bf16[128,8,256]{2,1,0:T(8,128)(2,1)} %copy.32), calls=%async_computation.1 | async-start | bytes 1048576 | tf_op jit(solution)/shard_map/all_to_all | solution.py:73
  103.5 21.6 %collective-permute-start.3 = (f32[2,128,256]{1,2,0:T(8,128)S(1)}, f32[2,128,256]{1,2,0:T(8,128)S(1)}, u32[]{:S(2)}, u32[]{:S(2)}) collective-permute-start(f32[2,128,256]{1,2,0:T(8,128)S(1)} %copy.36), channel_id=1, source_target_pairs={{0,1},{1,0},{2,3},{3,2},{4,5},{5,4},{6,7},{7,6},{8,9},{9,8},{10,11... | collective-permute-start | bytes 786440 | tf_op jit(solution)/shard_map/ppermute | solution.py:29
  120.9 4.3 %copy-start.1 = (f32[2,256,256]{2,1,0:T(8,128)}, f32[2,256,256]{2,1,0:T(8,128)S(1)}, u32[]{:S(2)}) copy-start(f32[2,256,256]{2,1,0:T(8,128)S(1)} %fusion.1) | copy-start | bytes 1572868
  121.7 68.2 %collective-permute-start.1 = (f32[256,256]{1,0:T(8,128)}, f32[256,256]{1,0:T(8,128)}, u32[]{:S(2)}, u32[]{:S(2)}) collective-permute-start(f32[256,256]{1,0:T(8,128)} %dynamic-slice_bitcast_fusion), channel_id=1, source_target_pairs={{0,1},{1,0},{2,3},{3,2},{4,5},{5,4},{6,7},{7,6},{8,9},{9,8},{10,11... | collective-permute-start | bytes 786440 | tf_op jit(solution)/shard_map/ppermute | solution.py:79

commit v2 on v1

v2 whole, which is shorter than its diff:
```python
import math

import jax
import jax.numpy as jnp
from jax import lax
from jax.experimental import pallas as pl
from jax.experimental.pallas import tpu as pltpu
from jax.sharding import PartitionSpec as P

SWAP = ((0, 1), (1, 0))
MAX_STEPS = 7
RESIDUAL = 2.5e-7
HIGHEST = lax.Precision.HIGHEST


def select_rows(index, count):
    places = lax.broadcasted_iota(jnp.int32, (index.shape[0], count), 1)
    return (index[:, None] == places).astype(jnp.bfloat16)


def two_terms(value):
    upper = lax.reduce_precision(value, exponent_bits=8, mantissa_bits=7)
    return upper.astype(jnp.bfloat16), (value - upper).astype(jnp.bfloat16)


def mat(left, right):
    return lax.dot_general(
        left, right, (((1,), (0,)), ((), ())), precision=HIGHEST, preferred_element_type=jnp.float32
    )


def mat_t(left, right):
    return lax.dot_general(
        left, right, (((1,), (1,)), ((), ())), precision=HIGHEST, preferred_element_type=jnp.float32
    )


def ritz_kernel(gram_m_ref, gram_k_ref, inverse_ref, projected_ref, good_ref, sym_ref):
    n = gram_m_ref.shape[0]
    row = lax.broadcasted_iota(jnp.int32, (n, n), 0)
    col = lax.broadcasted_iota(jnp.int32, (n, n), 1)
    weight = jnp.where(row > col, 1.0, jnp.where(row == col, 0.5, 0.0))
    gram = gram_m_ref[...]
    gram = 0.5 * (gram + gram.T)
    sym_ref[...] = gram
    on_diag = jnp.where(row == col, gram, 0.0)
    down = lax.rsqrt(jnp.sum(on_diag, axis=1, keepdims=True))
    across = lax.rsqrt(jnp.sum(on_diag, axis=0, keepdims=True))
    error = gram * down * across - jnp.where(row == col, 1.0, 0.0)
    inverse_ref[...] = (jnp.where(row == col, 1.0, 0.0) - weight * error) * across

    def going(state):
        step, size = state
        return jnp.logical_and(step < MAX_STEPS, jnp.logical_not(size < RESIDUAL))

    def correct(state):
        step, _ = state
        inverse = inverse_ref[...]
        error = mat_t(mat(inverse, sym_ref[...]), inverse) - jnp.where(row == col, 1.0, 0.0)
        inverse_ref[...] = inverse - mat(weight * error, inverse)
        return step + 1, jnp.sum(error * error)

    _, size = lax.while_loop(going, correct, (jnp.int32(0), jnp.float32(1.0)))
    good_ref[0, 0] = jnp.where(size < RESIDUAL, 1, 0).astype(jnp.int32)
    inverse = inverse_ref[...]
    projected_ref[...] = mat_t(mat(inverse, gram_k_ref[...]), inverse)


def ritz(gram_m, gram_k):
    n = gram_m.shape[0]
    vmem = pl.BlockSpec(memory_space=pltpu.VMEM)
    inverse, projected, good = pl.pallas_call(
        ritz_kernel,
        out_shape=(
            jax.ShapeDtypeStruct((n, n), jnp.float32),
            jax.ShapeDtypeStruct((n, n), jnp.float32),
            jax.ShapeDtypeStruct((1, 1), jnp.int32),
        ),
        in_specs=[vmem, vmem],
        out_specs=(vmem, vmem, pl.BlockSpec(memory_space=pltpu.SMEM)),
        scratch_shapes=[pltpu.VMEM((n, n), jnp.float32)],
        name="ritz",
    )(gram_m, gram_k)

    def direct():
        lower = jnp.linalg.cholesky(0.5 * (gram_m + gram_m.T))
        solved = lax.linalg.triangular_solve(
            lower, jnp.eye(n, dtype=lower.dtype), left_side=True, lower=True
        )
        middle = jnp.dot(solved, gram_k, precision=HIGHEST)
        return solved, jnp.dot(middle, solved.T, precision=HIGHEST)

    return lax.cond(good[0, 0] > 0, lambda: (inverse, projected), direct)


def to_pieces(plane):
    rows, wide = plane.shape
    return plane.reshape(rows // 2, 2, 2, wide // 2).transpose(2, 0, 1, 3).reshape(rows, 2, wide // 2)


def from_pieces(pieces):
    rows, _, lanes = pieces.shape
    return pieces.reshape(2, rows // 2, 2, lanes).transpose(1, 2, 0, 3).reshape(rows, 2 * lanes)


def per_device(basis, stiffness, mass, owner_rows, counts):
    n_sub = lax.axis_size("sub")
    me_sub = lax.axis_index("sub")
    me_blk = lax.axis_index("blk")
    rows_dev, width = basis.shape
    sub_dev, half, order = stiffness.shape
    cap = owner_rows.shape[2]
    cap_half = cap // 2
    lanes = width // 2
    table = lax.dynamic_slice_in_dim(owner_rows[0], me_blk * cap_half, cap_half, 1)
    picks = select_rows(table.reshape(-1), rows_dev)

    sent = jnp.dot(picks, basis, preferred_element_type=jnp.float32).astype(jnp.bfloat16)
    received = lax.all_to_all(
        sent.reshape(n_sub, cap_half, width), "sub", split_axis=0, concat_axis=0, tiled=True
    )
    mine = jnp.roll(received, -me_sub, axis=0).transpose(1, 0, 2).reshape(sub_dev, half, width)
    slots = me_blk * half + jnp.arange(half, dtype=jnp.int32)
    my_live = (slots[None, :] < counts[:, None])[:, :, None]
    mine = jnp.where(my_live, mine, jnp.zeros((), jnp.bfloat16))
    other = lax.ppermute(mine, "blk", SWAP)
    low = jnp.where(me_blk == 0, mine, other)
    high = jnp.where(me_blk == 0, other, mine)
    local_basis = jnp.concatenate([low, high], axis=1)

    def product(matrix):
        full = jnp.einsum("sij,sjr->sir", matrix, local_basis, preferred_element_type=jnp.float32)
        return jnp.where(my_live, full, 0.0).astype(jnp.bfloat16)

    stiff_part = product(stiffness)
    mass_part = product(mass)

    def gram(part):
        return jnp.einsum("sir,sic->rc", mine, part, preferred_element_type=jnp.float32)

    grams = jnp.stack([gram(mass_part), gram(stiff_part)]).reshape(2, 2, width // 2, width)
    grams = lax.dynamic_index_in_dim(grams, me_blk, 1, keepdims=False) + lax.ppermute(
        lax.dynamic_index_in_dim(grams, 1 - me_blk, 1, keepdims=False), "blk", SWAP
    )
    terms = [to_pieces(term) for plane in (grams[0], grams[1]) for term in two_terms(plane)]
    outgoing = stiff_part.reshape(cap_half, n_sub, width).transpose(1, 0, 2)
    outgoing = jnp.roll(outgoing, me_sub, axis=0)
    back = lax.all_to_all(
        jnp.concatenate([outgoing, jnp.concatenate(terms, axis=1)], axis=2),
        "sub",
        split_axis=0,
        concat_axis=0,
        tiled=True,
    )
    total = jnp.sum(back[:, :, width:].astype(jnp.float32), axis=0).reshape(2, 2, 2, lanes)
    total = jnp.sum(total, axis=1).reshape(4, lanes)
    spread = lax.all_to_all(
        jnp.broadcast_to(total[None], (n_sub, 4, lanes)),
        "sub",
        split_axis=0,
        concat_axis=0,
        tiled=True,
    )
    mine_grams = jnp.stack([from_pieces(spread[:, :2]), from_pieces(spread[:, 2:])])
    other_grams = lax.ppermute(mine_grams, "blk", SWAP)
    grams = jnp.concatenate(
        [
            jnp.where(me_blk == 0, mine_grams, other_grams),
            jnp.where(me_blk == 0, other_grams, mine_grams),
        ],
        axis=1,
    )

    image = jnp.einsum(
        "tr,tc->rc",
        picks,
        back[:, :, :width].reshape(-1, width),
        preferred_element_type=jnp.float32,
    ).reshape(2, rows_dev // 2, width)
    image_k = lax.dynamic_index_in_dim(image, me_blk, 0, keepdims=False) + lax.ppermute(
        lax.dynamic_index_in_dim(image, 1 - me_blk, 0, keepdims=False), "blk", SWAP
    )

    inverse, projected = ritz(grams[0], grams[1])
    scale_rows = math.sqrt(rows_dev * n_sub)
    rotated = scale_rows * jnp.dot(image_k, inverse.T, precision=lax.Precision.HIGH)
    return (rotated, projected)


def solution(mesh):
    return jax.shard_map(
        per_device,
        mesh=mesh,
        in_specs=(
            P("sub", None),
            P("sub", "blk", None),
            P("sub", "blk", None),
            P("sub", None, None),
            P("sub"),
        ),
        out_specs=(P(("sub", "blk"), None), P()),
        check_vma=False,
    )
```

time: 193 us -> 192 us (level)
  waiting for transfers between devices: 47.5 us -> 35 us
  blocking collectives: 19.9 us -> 31 us
  Pallas kernels: 0 us -> 11.1 us
  starting transfers between devices: 39.5 us -> 28.8 us
  local copies, waits for them, and re-layouts: 11.5 us -> 8.18 us
  matrix products: 12.4 us -> 14.4 us
    all_to_all x2 -> x1, waiting for transfers between devices: 25.6 us -> 12.8 us  [per_device(): lax.all_to_all(jnp.broadcast_to(total[None], (n_sub, 4, lanes)), 'sub', s...]
    pallas_call x0 -> x1, Pallas kernels: none -> 11.1 us  [ritz(): pl.pallas_call(ritz_kernel, out_shape=(jax.ShapeDtypeStruct((n, n), jnp.f...]
    all_to_all x1, blocking collectives: 19.9 us -> 31 us  [per_device(): lax.all_to_all(jnp.concatenate([outgoing, jnp.concatenate(terms, axis=1)]...]
    all_to_all x2 -> x1, starting transfers between devices: 14.5 us -> 6.36 us  [per_device(): lax.all_to_all(jnp.broadcast_to(total[None], (n_sub, 4, lanes)), 'sub', s...]
    ppermute x1, starting transfers between devices: 3.41 us -> 0.1 us  [per_device(): lax.ppermute(lax.dynamic_index_in_dim(image, 1 - me_blk, 0, keepdims=Fals...]
    another operation x9 -> x13, local copies, waits for them, and re-layouts: 5.43 us -> 4.47 us
    another operation x9 -> x10, other arithmetic: 54.5 us -> 54.5 us  [the longest x6 34 us: direct(): lower = jnp.linalg.cholesky(0.5 * (gram_m + gram_m.T))]
  transfers between devices with their start and end apart: 7 -> 6, of which waited for: 5 -> 5; matrix products, arithmetic and copies ran while one was open for 35% -> 34% of each run, Pallas kernels for 0% -> 6%
where the time goes in v2:
time: 192 us
  other arithmetic  59.6 us (31%)
  waiting for transfers between devices  35 us (18%)
  blocking collectives  31 us (16%)
  starting transfers between devices  28.8 us (15%)
  matrix products  14.4 us (8%)
  Pallas kernels  11.1 us (6%)
  local copies, waits for them, and re-layouts  8.18 us (4%)
    another operation x6, other arithmetic, direct(): lower = jnp.linalg.cholesky(0.5 * (gram_m + gram_m.T))  34 us
    all_to_all x1, blocking collectives, per_device(): lax.all_to_all(jnp.concatenate([outgoing, jnp.concatenate(terms, axis=1)]...  31 us
    another operation x4, other arithmetic, direct(): lax.linalg.triangular_solve(lower, jnp.eye(n, dtype=lower.dtype), left_si...  20.4 us
    all_to_all x1, waiting for transfers between devices, per_device(): lax.all_to_all(sent.reshape(n_sub, cap_half, width), 'sub', split_axis=0,...  19 us
    all_to_all x1, starting transfers between devices, per_device(): lax.all_to_all(sent.reshape(n_sub, cap_half, width), 'sub', split_axis=0,...  16.3 us
    all_to_all x1, waiting for transfers between devices, per_device(): lax.all_to_all(jnp.broadcast_to(total[None], (n_sub, 4, lanes)), 'sub', s...  12.8 us
    pallas_call x1, Pallas kernels, ritz(): pl.pallas_call(ritz_kernel, out_shape=(jax.ShapeDtypeStruct((n, n), jnp.f...  11.1 us
    all_to_all x1, starting transfers between devices, per_device(): lax.all_to_all(jnp.broadcast_to(total[None], (n_sub, 4, lanes)), 'sub', s...  6.36 us
  transfers between devices with their start and end apart: 6, of which 5 were waited for; matrix products, arithmetic and copies ran while one was open for 34% of the time, Pallas kernels for 6%

profile of v2, /device:TPU:1, one launch (start us, length us, event | category | flops | bytes accessed | tf_op | source)
XLA Modules:
  0.0 191.6 jit_solution(390749818766306263)
XLA Ops:
  1.7 2.3 %fusion.15 = bf16[128,8,256]{2,1,0:T(8,128)(2,1)} fusion(bf16[512,256]{1,0:T(8,128)(2,1)} %param.9, s32[1024]{0:T(1024)S(1)} %eq.33), kind=kOutput, calls=%fused_computation.40 | convolution fusion | flops 269221888 | bytes 790528 | tf_op jit(solution)/shard_map/dot_general | solution.py:118
  4.0 16.3 %all-to-all-start = ((bf16[128,8,256]{2,1,0:T(8,128)(2,1)}), bf16[128,8,256]{2,1,0:T(8,128)(2,1)S(1)}, u32[]{:S(2)}, u32[]{:S(2)}) async-start(bf16[128,8,256]{2,1,0:T(8,128)(2,1)} %fusion.15), calls=%async_computation | async-start | bytes 1048576 | tf_op jit(solution)/shard_map/all_to_all | solution.py:119
  20.4 19.0 %all-to-all-done = bf16[128,8,256]{2,1,0:T(8,128)(2,1)S(1)} async-done(((bf16[128,8,256]{2,1,0:T(8,128)(2,1)}), bf16[128,8,256]{2,1,0:T(8,128)(2,1)S(1)}, u32[]{:S(2)}, u32[]{:S(2)}) %all-to-all-start) | async-done | bytes 524320 | tf_op jit(solution)/shard_map/all_to_all | solution.py:119
  40.2 2.6 %collective-permute-start = (bf16[2,512,256]{1,2,0:T(8,128)(2,1)S(1)}, bf16[2,512,256]{1,2,0:T(8,128)(2,1)}, u32[]{:S(2)}, u32[]{:S(2)}) collective-permute-start(bf16[2,512,256]{1,2,0:T(8,128)(2,1)S(1)} %broadcast_select_fusion), channel_id=1, source_target_pairs={{0,1},{1,0},{2,3},{3,2},{4,5},{5,4},{6,7},{7,6},{8,9},{9,8},{10,11... | collective-permute-start | bytes 1572872 | tf_op jit(solution)/shard_map/ppermute | solution.py:126
  42.8 1.7 collective-permute-done
  44.4 1.1 broadcast_select_fusion.2
  46.9 3.7 %convolution_bitcast_fusion.1 = f32[1,2,128,256]{3,2,1,0:T(8,128)} fusion(bf16[2,128,512,2]{2,1,0,3:T(8,128)(2,1)S(1)} %bitcast.120, bf16[2,512,1024]{2,1,0:T(8,128)(2,1)} %param.11, bf16[2,512,256]{1,2,0:T(8,128)(2,1)} %copy-done.3, bf16[2,512,256]{1,2,0:T(8,128)(2,1)} %copy-done.2, pred[2,512]{1,0:T(4,128)(4,1)S(1)} %broadcast_compare_fusion), kind=kOutput, calls=%fused_computation.44 | convolution fusion | flops 673710080 | bytes 3933184 | tf_op jit(solution)/shard_map/sir,sic->rc/dot_general | solution.py:139
  50.6 1.6 fusion.28
  56.1 31.0 %all_to_all.15 = bf16[128,8,384]{2,1,0:T(8,128)(2,1)S(1)} all-to-all(bf16[128,8,384]{2,1,0:T(8,128)(2,1)S(1)} %copy.64), channel_id=1, replica_groups=mesh['sub'=128,'blk'=2] {'sub'}, dimensions={0} | all-to-all | bytes 1572864 | tf_op jit(solution)/shard_map/all_to_all | solution.py:148
  88.0 6.4 %all-to-all-start.2 = ((f32[128,4,128]{2,1,0:T(4,128)}), f32[128,4,128]{2,1,0:T(4,128)S(1)}, u32[]{:S(2)}, u32[]{:S(2)}) async-start(f32[128,4,128]{2,1,0:T(4,128)} %broadcast_in_dim.45), calls=%async_computation.2 | async-start | bytes 524288 | tf_op jit(solution)/shard_map/all_to_all | solution.py:157
  94.4 12.8 %all-to-all-done.2 = f32[128,4,128]{2,1,0:T(4,128)S(1)} async-done(((f32[128,4,128]{2,1,0:T(4,128)}), f32[128,4,128]{2,1,0:T(4,128)S(1)}, u32[]{:S(2)}, u32[]{:S(2)}) %all-to-all-start.2) | async-done | bytes 262176 | tf_op jit(solution)/shard_map/all_to_all | solution.py:157
  107.8 3.1 %collective-permute-start.3 = (f32[2,128,256]{2,1,0:T(8,128)S(1)}, f32[2,128,256]{2,1,0:T(8,128)S(1)}, u32[]{:S(2)}, u32[]{:S(2)}) collective-permute-start(f32[2,128,256]{2,1,0:T(8,128)S(1)} %constant_dynamic-update-slice_fusion.2), channel_id=1, source_target_pairs={{0,1},{1,0},{2,3},{3,2},{4,5},{5,4},{6,7},{7,6},{8,9},{9,8},{10,11... | collective-permute-start | bytes 786440 | tf_op jit(solution)/shard_map/ppermute | solution.py:165
  112.2 11.1 %ritz.1 = (f32[256,256]{1,0:T(8,128)}, f32[256,256]{1,0:T(8,128)}, s32[1,1]{1,0:T(1,128)}) custom-call(f32[256,256]{1,0:T(8,128)S(1)} %get-tuple-element.60.gram_m_ref, f32[256,256]{1,0:T(8,128)S(1)} %get-tuple-element.59.gram_k_ref), custom_call_target="tpu_custom_call" | custom-call | tf_op jit(solution)/shard_map/ritz/pallas_call | solution.py:72
  123.9 65.5 %conditional.1 = ((f32[256,256]{1,0:T(8,128)}, f32[256,256]{1,0:T(8,128)})) conditional(s32[]{:T(128)} %bitcast.44, (f32[256,256]{1,0:T(8,128)S(1)}, f32[256,256]{1,0:T(8,128)S(1)}) %tuple.16, (f32[256,256]{1,0:T(8,128)}, f32[256,256]{1,0:T(8,128)}) %tuple.17), branch_computations={%region_2.8_spmd, %region_7.9_spmd} | conditional | flops 604848384 | bytes 7604447 | solution.py:93
  124.6 11.7 %cholesky.5 = f32[128,128]{1,0:T(8,128)S(1)} custom-call(f32[128,128]{1,0:T(8,128)S(1)} %cholesky.46), custom_call_target="Cholesky" | custom-call | tf_op jit(solution)/shard_map/cond/branch_0_fun/jit(cholesky)/cholesky | solution.py:86
  136.3 9.8 %custom-call.12 = f32[1,128,128]{1,2,0:T(8,128)S(1)} custom-call(f32[1,128,128]{2,1,0:T(8,128)S(1)} %get-tuple-element.52), custom_call_target="InvertDiagBlocksLowerTriangular" | custom-call | tf_op jit(solution)/shard_map/cond/branch_0_fun/jit(cholesky)/cholesky | solution.py:86
  146.6 11.7 %cholesky.29 = f32[128,128]{1,0:T(8,128)S(1)} custom-call(f32[128,128]{1,0:T(8,128)S(1)} %convolution_subtract_fusion.1), custom_call_target="Cholesky" | custom-call | tf_op jit(solution)/shard_map/cond/branch_0_fun/jit(cholesky)/cholesky | solution.py:86
  160.5 4.3 %while.1 = (s32[]{:T(128)}, f32[256,256]{1,0:T(8,128)S(1)}, s32[2,2]{1,0:T(2,128)S(1)}, f32[2,128,128]{2,1,0:T(8,128)S(1)}, s32[]{:T(128)}) while((s32[]{:T(128)}, f32[256,256]{1,0:T(8,128)S(1)}, s32[2,2]{1,0:T(2,128)S(1)}, f32[2,128,128]{2,1,0:T(8,128)S(1)}, s32[]{:T(128)}) %tuple.48), condition=%wide.while_cond, body=%wide.while_body.sunk | while | flops 2 | bytes 131181 | solution.py:87
  161.4 1.3 bitcast_dynamic-update-slice_fusion.2
  163.4 1.3 bitcast_dynamic-update-slice_fusion.2
  164.8 19.7 %custom-call.13 = f32[2,128,128]{1,2,0:T(8,128)S(1)} custom-call(f32[2,128,128]{2,1,0:T(8,128)S(1)} %get-tuple-element.30), custom_call_target="InvertDiagBlocksLowerTriangular" | custom-call | tf_op jit(solution)/shard_map/cond/branch_0_fun/triangular_solve | solution.py:87
  186.1 1.3 fusion.48
  187.4 2.1 %fusion.49 = f32[256,256]{1,0:T(8,128)} fusion(f32[256,256]{1,0:T(8,128)S(1)} %fusion.48, f32[256,256]{1,0:T(8,128)} %pad_maximum_fusion), kind=kOutput, calls=%fused_computation.108 | convolution fusion | flops 201326592 | bytes 786432 | tf_op jit(solution)/shard_map/cond/branch_0_fun/dot_general | solution.py:91
  189.5 2.2 %convolution_multiply_fusion = f32[256,256]{1,0:T(8,128)} fusion(f32[256,256]{1,0:T(8,128)} %get-tuple-element.21, f32[256,256]{1,0:T(8,128)} %collective-permute-done.2, f32[2,256,256]{2,1,0:T(8,128)} %copy-done.1, s32[]{:T(128)S(6)} %select_n.71), kind=kOutput, calls=%fused_computation.42 | convolution fusion | flops 100794368 | bytes 1048580 | tf_op jit(solution)/shard_map/dot_general | solution.py:186
  (81 shorter events, 14.3 us)
Async XLA Ops:
  0.6 45.0 %copy-start = (bf16[2,512,1024]{2,1,0:T(8,128)(2,1)S(1)}, bf16[2,512,1024]{2,1,0:T(8,128)(2,1)}, u32[]{:S(2)}) copy-start(bf16[2,512,1024]{2,1,0:T(8,128)(2,1)} %param.10) | copy-start | bytes 6291460
  0.6 19.7 %copy-start.4 = (s32[2]{0:T(128)S(1)}, s32[2]{0:T(128)}, u32[]{:S(2)}) copy-start(s32[2]{0:T(128)} %param.13) | copy-start | bytes 28
  4.0 35.5 %all-to-all-start = ((bf16[128,8,256]{2,1,0:T(8,128)(2,1)}), bf16[128,8,256]{2,1,0:T(8,128)(2,1)S(1)}, u32[]{:S(2)}, u32[]{:S(2)}) async-start(bf16[128,8,256]{2,1,0:T(8,128)(2,1)} %fusion.15), calls=%async_computation | async-start | bytes 1048576 | tf_op jit(solution)/shard_map/all_to_all | solution.py:119
  40.2 4.2 %collective-permute-start = (bf16[2,512,256]{1,2,0:T(8,128)(2,1)S(1)}, bf16[2,512,256]{1,2,0:T(8,128)(2,1)}, u32[]{:S(2)}, u32[]{:S(2)}) collective-permute-start(bf16[2,512,256]{1,2,0:T(8,128)(2,1)S(1)} %broadcast_select_fusion), channel_id=1, source_target_pairs={{0,1},{1,0},{2,3},{3,2},{4,5},{5,4},{6,7},{7,6},{8,9},{9,8},{10,11... | collective-permute-start | bytes 1572872 | tf_op jit(solution)/shard_map/ppermute | solution.py:126
  45.6 0.8 copy-start.2
  45.6 1.0 copy-start.3
  52.2 1.9 collective-permute-start.1
  88.0 19.2 %all-to-all-start.2 = ((f32[128,4,128]{2,1,0:T(4,128)}), f32[128,4,128]{2,1,0:T(4,128)S(1)}, u32[]{:S(2)}, u32[]{:S(2)}) async-start(f32[128,4,128]{2,1,0:T(4,128)} %broadcast_in_dim.45), calls=%async_computation.2 | async-start | bytes 524288 | tf_op jit(solution)/shard_map/all_to_all | solution.py:157
  107.8 4.3 %collective-permute-start.3 = (f32[2,128,256]{2,1,0:T(8,128)S(1)}, f32[2,128,256]{2,1,0:T(8,128)S(1)}, u32[]{:S(2)}, u32[]{:S(2)}) collective-permute-start(f32[2,128,256]{2,1,0:T(8,128)S(1)} %constant_dynamic-update-slice_fusion.2), channel_id=1, source_target_pairs={{0,1},{1,0},{2,3},{3,2},{4,5},{5,4},{6,7},{7,6},{8,9},{9,8},{10,11... | collective-permute-start | bytes 786440 | tf_op jit(solution)/shard_map/ppermute | solution.py:165
  111.4 0.8 copy-start.1
  111.4 78.0 %collective-permute-start.2 = (f32[256,256]{1,0:T(8,128)S(1)}, f32[256,256]{1,0:T(8,128)}, u32[]{:S(2)}, u32[]{:S(2)}) collective-permute-start(f32[256,256]{1,0:T(8,128)S(1)} %dynamic-slice_bitcast_fusion), channel_id=1, source_target_pairs={{0,1},{1,0},{2,3},{3,2},{4,5},{5,4},{6,7},{7,6},{8,9},{9,8},{10,11... | collective-permute-start | bytes 786440 | tf_op jit(solution)/shard_map/ppermute | solution.py:180

commit v3 on v2

v3 whole, which is shorter than its diff:
```python
import functools
import math

import jax
import jax.numpy as jnp
from jax import lax
from jax.experimental import pallas as pl
from jax.experimental.pallas import tpu as pltpu
from jax.sharding import PartitionSpec as P

SWAP = ((0, 1), (1, 0))
MAX_STEPS = 7
RESIDUAL = 1e-6
HIGHEST = lax.Precision.HIGHEST


def select_rows(index, count):
    places = lax.broadcasted_iota(jnp.int32, (index.shape[0], count), 1)
    return (index[:, None] == places).astype(jnp.bfloat16)


def two_terms(value):
    upper = lax.reduce_precision(value, exponent_bits=8, mantissa_bits=7)
    return upper.astype(jnp.bfloat16), (value - upper).astype(jnp.bfloat16)


def mat(left, right):
    return lax.dot_general(
        left, right, (((1,), (0,)), ((), ())), precision=HIGHEST, preferred_element_type=jnp.float32
    )


def mat_t(left, right):
    return lax.dot_general(
        left, right, (((1,), (1,)), ((), ())), precision=HIGHEST, preferred_element_type=jnp.float32
    )


def short(left, right, side):
    return lax.dot_general(
        left.astype(jnp.bfloat16),
        right.astype(jnp.bfloat16),
        (((1,), (side,)), ((), ())),
        preferred_element_type=jnp.float32,
    )


def product_kernel(counts_ref, mine_ref, other_ref, stiff_ref, mass_ref, part_ref, keep_ref, send_ref):
    sub_dev, half, width = mine_ref.shape
    me_blk = lax.axis_index("blk")
    first = me_blk == 0
    own = pl.ds(pl.multiple_of(me_blk * half, half), half)
    far = pl.ds(pl.multiple_of((1 - me_blk) * half, half), half)
    slot = me_blk * half + lax.broadcasted_iota(jnp.int32, (half, width), 0)
    for place, matrix_ref in enumerate((mass_ref, stiff_ref)):
        gram = None
        for s in range(sub_dev):
            mine = mine_ref[s]
            part = jnp.dot(matrix_ref[s, :, own], mine, preferred_element_type=jnp.float32)
            part += jnp.dot(matrix_ref[s, :, far], other_ref[s], preferred_element_type=jnp.float32)
            part = jnp.where(slot < counts_ref[s], part, 0.0).astype(jnp.bfloat16)
            if place == 1:
                part_ref[s] = part
            term = lax.dot_general(
                mine, part, (((0,), (0,)), ((), ())), preferred_element_type=jnp.float32
            )
            gram = term if gram is None else gram + term
        low, high = gram[: width // 2], gram[width // 2 :]
        keep_ref[place] = jnp.where(first, low, high)
        send_ref[place] = jnp.where(first, high, low)


def products(counts, mine, other, stiffness, mass):
    sub_dev, half, width = mine.shape
    vmem = pl.BlockSpec(memory_space=pltpu.VMEM)
    gram = jax.ShapeDtypeStruct((2, width // 2, width), jnp.float32)
    return pl.pallas_call(
        product_kernel,
        out_shape=(jax.ShapeDtypeStruct(mine.shape, jnp.bfloat16), gram, gram),
        in_specs=[pl.BlockSpec(memory_space=pltpu.SMEM)] + [vmem] * 4,
        out_specs=(vmem, vmem, vmem),
        compiler_params=pltpu.CompilerParams(vmem_limit_bytes=24 << 20),
        cost_estimate=pl.CostEstimate(
            flops=1400000000, bytes_accessed=6 << 20, transcendentals=0
        ),
        name="products",
    )(counts, mine, other, stiffness, mass)


def ritz_kernel(
    scale, mine_ref, other_ref, image_ref, extra_ref, rotated_ref, projected_ref, good_ref, gram_ref, inverse_ref
):
    rows, n = mine_ref.shape[1:]
    me_blk = lax.axis_index("blk")
    gram_ref[0, pl.ds(pl.multiple_of(me_blk * rows, rows), rows), :] = mine_ref[0]
    gram_ref[0, pl.ds(pl.multiple_of((1 - me_blk) * rows, rows), rows), :] = other_ref[0]
    gram_ref[1, pl.ds(pl.multiple_of(me_blk * rows, rows), rows), :] = mine_ref[1]
    gram_ref[1, pl.ds(pl.multiple_of((1 - me_blk) * rows, rows), rows), :] = other_ref[1]
    row = lax.broadcasted_iota(jnp.int32, (n, n), 0)
    col = lax.broadcasted_iota(jnp.int32, (n, n), 1)
    eye = jnp.where(row == col, 1.0, 0.0)
    weight = jnp.where(row > col, 1.0, 0.5 * eye)
    gram = gram_ref[0]
    gram = 0.5 * (gram + gram.T)
    on_diag = eye * gram
    down = lax.rsqrt(jnp.sum(on_diag, axis=1, keepdims=True))
    across = lax.rsqrt(jnp.sum(on_diag, axis=0, keepdims=True))
    scaled = gram * down * across
    gram_ref[0] = scaled
    rest = scaled - eye
    off = -weight * rest
    for _ in range(2):
        left = rest + off + short(off, rest, 0)
        step = weight * (left + off.T + short(left, off, 1))
        off = off - step - short(step, off, 0)
    inverse_ref[...] = eye + off

    def going(state):
        step, size = state
        return jnp.logical_and(step < MAX_STEPS, jnp.logical_not(size < RESIDUAL))

    def correct(state):
        step, _ = state
        inverse = inverse_ref[...]
        error = mat_t(mat(inverse, gram_ref[0]), inverse) - eye
        inverse_ref[...] = inverse - mat(weight * error, inverse)
        return step + 1, jnp.sum(error * error)

    _, size = lax.while_loop(going, correct, (jnp.int32(0), jnp.float32(1.0)))
    good_ref[0, 0] = jnp.where(size < RESIDUAL, 1, 0).astype(jnp.int32)
    inverse = inverse_ref[...] * across
    rotated_ref[...] = scale * mat_t(image_ref[...] + extra_ref[...], inverse)
    projected_ref[...] = mat_t(mat(inverse, gram_ref[1]), inverse)


def ritz(mine, other, image, extra, scale, me_blk):
    rows, n = mine.shape[1:]
    vmem = pl.BlockSpec(memory_space=pltpu.VMEM)
    square = jax.ShapeDtypeStruct((n, n), jnp.float32)
    rotated, projected, good = pl.pallas_call(
        functools.partial(ritz_kernel, scale),
        out_shape=(square, square, jax.ShapeDtypeStruct((1, 1), jnp.int32)),
        in_specs=[vmem] * 4,
        out_specs=(vmem, vmem, pl.BlockSpec(memory_space=pltpu.SMEM)),
        scratch_shapes=[pltpu.VMEM((2, n, n), jnp.float32), pltpu.VMEM((n, n), jnp.float32)],
        name="ritz",
    )(mine, other, image, extra)

    def direct():
        low = jnp.where(me_blk == 0, mine, other)
        high = jnp.where(me_blk == 0, other, mine)
        gram_m, gram_k = jnp.concatenate([low, high], axis=1)
        lower = jnp.linalg.cholesky(0.5 * (gram_m + gram_m.T))
        solved = lax.linalg.triangular_solve(
            lower, jnp.eye(n, dtype=lower.dtype), left_side=True, lower=True
        )
        middle = jnp.dot(solved, gram_k, precision=HIGHEST)
        return (
            scale * jnp.dot(image + extra, solved.T, precision=HIGHEST),
            jnp.dot(middle, solved.T, precision=HIGHEST),
        )

    return lax.cond(good[0, 0] > 0, lambda: (rotated, projected), direct)


def to_pieces(plane):
    rows, wide = plane.shape
    return plane.reshape(rows // 2, 2, 2, wide // 2).transpose(2, 0, 1, 3).reshape(rows, 2, wide // 2)


def from_pieces(pieces):
    rows, _, lanes = pieces.shape
    return pieces.reshape(2, rows // 2, 2, lanes).transpose(1, 2, 0, 3).reshape(rows, 2 * lanes)


def per_device(basis, stiffness, mass, owner_rows, counts):
    n_sub = lax.axis_size("sub")
    me_sub = lax.axis_index("sub")
    me_blk = lax.axis_index("blk")
    rows_dev, width = basis.shape
    sub_dev, half, order = stiffness.shape
    cap = owner_rows.shape[2]
    cap_half = cap // 2
    lanes = width // 2
    table = lax.dynamic_slice_in_dim(owner_rows[0], me_blk * cap_half, cap_half, 1)
    picks = select_rows(table.reshape(-1), rows_dev)

    sent = jnp.dot(picks, basis, preferred_element_type=jnp.float32).astype(jnp.bfloat16)
    received = lax.all_to_all(
        sent.reshape(n_sub, cap_half, width), "sub", split_axis=0, concat_axis=0, tiled=True
    )
    mine = jnp.roll(received, -me_sub, axis=0).transpose(1, 0, 2).reshape(sub_dev, half, width)
    slots = me_blk * half + jnp.arange(half, dtype=jnp.int32)
    my_live = (slots[None, :] < counts[:, None])[:, :, None]
    mine = jnp.where(my_live, mine, jnp.zeros((), jnp.bfloat16))
    other = lax.ppermute(mine, "blk", SWAP)
    stiff_part, keep, send = products(counts, mine, other, stiffness, mass)
    grams = keep + lax.ppermute(send, "blk", SWAP)
    terms = [to_pieces(term) for plane in (grams[0], grams[1]) for term in two_terms(plane)]
    outgoing = stiff_part.reshape(cap_half, n_sub, width).transpose(1, 0, 2)
    outgoing = jnp.roll(outgoing, me_sub, axis=0)
    back = lax.all_to_all(
        jnp.concatenate([outgoing, jnp.concatenate(terms, axis=1)], axis=2),
        "sub",
        split_axis=0,
        concat_axis=0,
        tiled=True,
    )
    total = jnp.sum(back[:, :, width:].astype(jnp.float32), axis=0).reshape(2, 2, 2, lanes)
    total = jnp.sum(total, axis=1).reshape(4, lanes)
    spread = lax.all_to_all(
        jnp.broadcast_to(total[None], (n_sub, 4, lanes)),
        "sub",
        split_axis=0,
        concat_axis=0,
        tiled=True,
    )
    mine_grams = jnp.stack([from_pieces(spread[:, :2]), from_pieces(spread[:, 2:])])
    other_grams = lax.ppermute(mine_grams, "blk", SWAP)
    image = jnp.einsum(
        "tr,tc->rc",
        picks,
        back[:, :, :width].reshape(-1, width),
        preferred_element_type=jnp.float32,
    ).reshape(2, rows_dev // 2, width)
    image_k = lax.dynamic_index_in_dim(image, me_blk, 0, keepdims=False)
    extra_k = lax.ppermute(
        lax.dynamic_index_in_dim(image, 1 - me_blk, 0, keepdims=False), "blk", SWAP
    )
    return ritz(
        mine_grams, other_grams, image_k, extra_k, math.sqrt(rows_dev * n_sub), me_blk
    )


def solution(mesh):
    return jax.shard_map(
        per_device,
        mesh=mesh,
        in_specs=(
            P("sub", None),
            P("sub", "blk", None),
            P("sub", "blk", None),
            P("sub", None, None),
            P("sub"),
        ),
        out_specs=(P(("sub", "blk"), None), P()),
        check_vma=False,
    )
```

time: 192 us -> 182 us (0.948)
  matrix products: 14.4 us -> 4.35 us
  other arithmetic: 59.6 us -> 56.4 us
  Pallas kernels: 11.1 us -> 13.8 us
  waiting for transfers between devices: 35 us -> 32.4 us
    dot_general x5 -> x2, matrix products: 8.99 us -> 0.82 us  [the longest x1 0.41 us: direct(): jnp.dot(image + extra, solved.T, precision=HIGHEST)]
    pallas_call x1 -> x2, Pallas kernels: 11.1 us -> 13.8 us  [the longest x1 11.4 us: ritz(): pl.pallas_call(functools.partial(ritz_kernel, scale), out_shape=(square,...]
    all_to_all x1, waiting for transfers between devices: 12.8 us -> 10.6 us  [per_device(): lax.all_to_all(jnp.broadcast_to(total[None], (n_sub, 4, lanes)), 'sub', s...]
    another operation x4 -> x3, other arithmetic: 20.4 us -> 19.7 us  [direct(): lax.linalg.triangular_solve(lower, jnp.eye(n, dtype=lower.dtype), left_si...]
    another operation x7 -> x9, local copies, waits for them, and re-layouts: 4.15 us -> 4.31 us
  transfers between devices with their start and end apart: 6 -> 6, of which waited for: 5 -> 4; matrix products, arithmetic and copies ran while one was open for 34% -> 1% of each run, Pallas kernels for 6% -> 0%
where the time goes in v3:
time: 182 us
  other arithmetic  56.4 us (31%)
  waiting for transfers between devices  32.4 us (18%)
  blocking collectives  31.1 us (17%)
  starting transfers between devices  30.7 us (17%)
  Pallas kernels  13.8 us (8%)
  local copies, waits for them, and re-layouts  8.97 us (5%)
  matrix products  4.35 us (2%)
  loops' own time  2.24 us (1%)
    another operation x6, other arithmetic, direct(): lower = jnp.linalg.cholesky(0.5 * (gram_m + gram_m.T))  34 us
    all_to_all x1, blocking collectives, per_device(): lax.all_to_all(jnp.concatenate([outgoing, jnp.concatenate(terms, axis=1)]...  31.1 us
    another operation x3, other arithmetic, direct(): lax.linalg.triangular_solve(lower, jnp.eye(n, dtype=lower.dtype), left_si...  19.7 us
    all_to_all x1, waiting for transfers between devices, per_device(): lax.all_to_all(sent.reshape(n_sub, cap_half, width), 'sub', split_axis=0,...  19 us
    all_to_all x1, starting transfers between devices, per_device(): lax.all_to_all(sent.reshape(n_sub, cap_half, width), 'sub', split_axis=0,...  16.5 us
    pallas_call x1, Pallas kernels, ritz(): pl.pallas_call(functools.partial(ritz_kernel, scale), out_shape=(square,...  11.4 us
    all_to_all x1, waiting for transfers between devices, per_device(): lax.all_to_all(jnp.broadcast_to(total[None], (n_sub, 4, lanes)), 'sub', s...  10.6 us
    all_to_all x1, starting transfers between devices, per_device(): lax.all_to_all(jnp.broadcast_to(total[None], (n_sub, 4, lanes)), 'sub', s...  6.36 us
  transfers between devices with their start and end apart: 6, of which 4 were waited for; matrix products, arithmetic and copies ran while one was open for 1% of the time, Pallas kernels for 0%

profile of v3, /device:TPU:1, one launch (start us, length us, event | category | flops | bytes accessed | tf_op | source)
XLA Modules:
  0.0 181.5 jit_solution(6748876758588336960)
XLA Ops:
  1.6 1.3 fusion.24
  2.9 16.5 %all-to-all-start = ((bf16[128,8,256]{2,1,0:T(8,128)(2,1)}), bf16[128,8,256]{2,1,0:T(8,128)(2,1)S(1)}, u32[]{:S(2)}, u32[]{:S(2)}) async-start(bf16[128,8,256]{2,1,0:T(8,128)(2,1)} %fusion.24), calls=%async_computation | async-start | bytes 1048576 | tf_op jit(solution)/shard_map/all_to_all | solution.py:189
  19.5 19.0 %all-to-all-done = bf16[128,8,256]{2,1,0:T(8,128)(2,1)S(1)} async-done(((bf16[128,8,256]{2,1,0:T(8,128)(2,1)}), bf16[128,8,256]{2,1,0:T(8,128)(2,1)S(1)}, u32[]{:S(2)}, u32[]{:S(2)}) %all-to-all-start) | async-done | bytes 524320 | tf_op jit(solution)/shard_map/all_to_all | solution.py:189
  38.5 0.9 fusion.30
  39.8 2.6 %collective-permute-start = (bf16[2,512,256]{2,1,0:T(8,128)(2,1)S(1)}, bf16[2,512,256]{2,1,0:T(8,128)(2,1)S(1)}, u32[]{:S(2)}, u32[]{:S(2)}) collective-permute-start(bf16[2,512,256]{2,1,0:T(8,128)(2,1)S(1)} %bitcast_select_fusion.mine_ref), channel_id=1, source_target_pairs={{0,1},{1,0},{2,3},{3,2},{4,5},{5,4},{6,7},{7,6},{8,9},{9,8},{10,11... | collective-permute-start | bytes 1572872 | tf_op jit(solution)/shard_map/ppermute | solution.py:196
  42.3 1.5 collective-permute-done.other_ref
  43.9 2.4 %products.1 = (bf16[2,512,256]{2,1,0:T(8,128)(2,1)S(1)}, f32[2,128,256]{2,1,0:T(8,128)S(1)}, f32[2,128,256]{2,1,0:T(8,128)S(1)}) custom-call(s32[2]{0:T(128)S(1)} %copy-done.3, bf16[2,512,256]{2,1,0:T(8,128)(2,1)S(1)} %bitcast_select_fusion.mine_ref, bf16[2,512,256]{2,1,0:T(8,128)(2,1)S(1)} %collective-permute-done.other_ref, ...), custom_call_target="tpu_custom_call" | custom-call | flops 1400000000 | bytes 6291456 | tf_op jit(solution)/shard_map/products/pallas_call | solution.py:77
  47.1 0.9 fusion.28
  48.7 31.1 %all_to_all.15 = bf16[128,8,384]{2,1,0:T(8,128)(2,1)S(1)} all-to-all(bf16[128,8,384]{2,1,0:T(8,128)(2,1)S(1)} %pad_maximum_fusion.5), channel_id=1, replica_groups=mesh['sub'=128,'blk'=2] {'sub'}, dimensions={0} | all-to-all | bytes 1572864 | tf_op jit(solution)/shard_map/all_to_all | solution.py:202
  79.9 0.7 broadcast_in_dim.27
  80.6 6.4 %all-to-all-start.2 = ((f32[128,4,128]{2,1,0:T(4,128)}), f32[128,4,128]{2,1,0:T(4,128)S(1)}, u32[]{:S(2)}, u32[]{:S(2)}) async-start(f32[128,4,128]{2,1,0:T(4,128)} %broadcast_in_dim.27), calls=%async_computation.2 | async-start | bytes 524288 | tf_op jit(solution)/shard_map/all_to_all | solution.py:211
  87.5 1.8 collective-permute-start.3
  89.3 10.6 %all-to-all-done.2 = f32[128,4,128]{2,1,0:T(4,128)S(1)} async-done(((f32[128,4,128]{2,1,0:T(4,128)}), f32[128,4,128]{2,1,0:T(4,128)S(1)}, u32[]{:S(2)}, u32[]{:S(2)}) %all-to-all-start.2) | async-done | bytes 262176 | tf_op jit(solution)/shard_map/all_to_all | solution.py:211
  100.6 3.1 %collective-permute-start.2 = (f32[2,128,256]{2,1,0:T(8,128)S(1)}, f32[2,128,256]{2,1,0:T(8,128)S(1)}, u32[]{:S(2)}, u32[]{:S(2)}) collective-permute-start(f32[2,128,256]{2,1,0:T(8,128)S(1)} %constant_dynamic-update-slice_fusion.2.mine_ref), channel_id=1, source_target_pairs={{0,1},{1,0},{2,3},{3,2},{4,5},{5,4},{6,7},{7,6},{8,9},{9,8},{10,11... | collective-permute-start | bytes 786440 | tf_op jit(solution)/shard_map/ppermute | solution.py:219
  103.7 1.2 collective-permute-done.2.other_ref
  104.9 11.4 %ritz.1 = (f32[256,256]{1,0:T(8,128)S(1)}, f32[256,256]{1,0:T(8,128)S(1)}, s32[1,1]{1,0:T(1,128)}) custom-call(f32[2,128,256]{2,1,0:T(8,128)S(1)} %constant_dynamic-update-slice_fusion.2.mine_ref, f32[2,128,256]{2,1,0:T(8,128)S(1)} %collective-permute-done.2.other_ref, f32[256,256]{1,0:T(8,128)S(1)} %get-tuple-element.87.image_ref, ...), custom_call_target="tpu_custom_call" | custom-call | tf_op jit(solution)/shard_map/ritz/pallas_call | solution.py:140
  116.9 63.2 %conditional.1 = ((f32[256,256]{1,0:T(8,128)S(1)}, f32[256,256]{1,0:T(8,128)S(1)})) conditional(s32[]{:T(128)} %bitcast.31, (f32[256,256]{1,0:T(8,128)S(1)}, f32[256,256]{1,0:T(8,128)S(1)}, s32[]{:T(128)}, f32[2,128,256]{2,1,0:T(8,128)S(1)}, f32[2,128,256]{2,1,0:T(8,128)S(1)}) %tuple.15, (f32[256,256]{1,0:T(8,128)S(1)}, ...), branch_computations={%region_2.8_spmd, %region_7.9_spmd} | conditional | flops 806764800 | bytes 11536617 | solution.py:163
  117.9 11.7 %cholesky.5 = f32[128,128]{1,0:T(8,128)S(1)} custom-call(f32[128,128]{1,0:T(8,128)S(1)} %cholesky.46), custom_call_target="Cholesky" | custom-call | tf_op jit(solution)/shard_map/cond/branch_0_fun/jit(cholesky)/cholesky | solution.py:153
  129.6 9.8 %custom-call.12 = f32[1,128,128]{1,2,0:T(8,128)S(1)} custom-call(f32[1,128,128]{2,1,0:T(8,128)S(1)} %get-tuple-element.81), custom_call_target="InvertDiagBlocksLowerTriangular" | custom-call | tf_op jit(solution)/shard_map/cond/branch_0_fun/jit(cholesky)/cholesky | solution.py:153
  139.9 11.7 %cholesky.29 = f32[128,128]{1,0:T(8,128)S(1)} custom-call(f32[128,128]{1,0:T(8,128)S(1)} %convolution_subtract_fusion.1), custom_call_target="Cholesky" | custom-call | tf_op jit(solution)/shard_map/cond/branch_0_fun/jit(cholesky)/cholesky | solution.py:153
  153.8 4.2 %while.1 = (s32[]{:T(128)}, f32[256,256]{1,0:T(8,128)S(1)}, s32[2,2]{1,0:T(2,128)S(1)}, f32[2,128,128]{2,1,0:T(8,128)S(1)}, s32[]{:T(128)}) while((s32[]{:T(128)}, f32[256,256]{1,0:T(8,128)S(1)}, s32[2,2]{1,0:T(2,128)S(1)}, f32[2,128,128]{2,1,0:T(8,128)S(1)}, s32[]{:T(128)}) %tuple.49), condition=%wide.while_cond, body=%wide.while_body.sunk | while | flops 2 | bytes 131181 | solution.py:154
  154.6 1.3 bitcast_dynamic-update-slice_fusion.2
  156.6 1.3 bitcast_dynamic-update-slice_fusion.2
  158.0 19.7 %custom-call.13 = f32[2,128,128]{1,2,0:T(8,128)S(1)} custom-call(f32[2,128,128]{2,1,0:T(8,128)S(1)} %get-tuple-element.45), custom_call_target="InvertDiagBlocksLowerTriangular" | custom-call | tf_op jit(solution)/shard_map/cond/branch_0_fun/triangular_solve | solution.py:154
  (76 shorter events, 10.7 us)
Async XLA Ops:
  0.6 1.0 copy-start
  0.6 18.8 %copy-start.3 = (s32[2]{0:T(128)S(1)}, s32[2]{0:T(128)}, u32[]{:S(2)}) copy-start(s32[2]{0:T(128)} %counts_ref.1) | copy-start | bytes 28
  2.9 41.0 %copy-start.1 = (bf16[2,512,1024]{2,1,0:T(8,128)(2,1)S(1)}, bf16[2,512,1024]{2,1,0:T(8,128)(2,1)}, u32[]{:S(2)}) copy-start(bf16[2,512,1024]{2,1,0:T(8,128)(2,1)} %stiff_ref.1) | copy-start | bytes 6291460
  2.9 35.6 %all-to-all-start = ((bf16[128,8,256]{2,1,0:T(8,128)(2,1)}), bf16[128,8,256]{2,1,0:T(8,128)(2,1)S(1)}, u32[]{:S(2)}, u32[]{:S(2)}) async-start(bf16[128,8,256]{2,1,0:T(8,128)(2,1)} %fusion.24), calls=%async_computation | async-start | bytes 1048576 | tf_op jit(solution)/shard_map/all_to_all | solution.py:189
  38.5 5.3 %copy-start.2 = (bf16[2,512,1024]{2,1,0:T(8,128)(2,1)S(1)}, bf16[2,512,1024]{2,1,0:T(8,128)(2,1)}, u32[]{:S(2)}) copy-start(bf16[2,512,1024]{2,1,0:T(8,128)(2,1)} %mass_ref.1) | copy-start | bytes 6291460
  39.8 4.1 %collective-permute-start = (bf16[2,512,256]{2,1,0:T(8,128)(2,1)S(1)}, bf16[2,512,256]{2,1,0:T(8,128)(2,1)S(1)}, u32[]{:S(2)}, u32[]{:S(2)}) collective-permute-start(bf16[2,512,256]{2,1,0:T(8,128)(2,1)S(1)} %bitcast_select_fusion.mine_ref), channel_id=1, source_target_pairs={{0,1},{1,0},{2,3},{3,2},{4,5},{5,4},{6,7},{7,6},{8,9},{9,8},{10,11... | collective-permute-start | bytes 1572872 | tf_op jit(solution)/shard_map/ppermute | solution.py:196
  46.3 1.7 collective-permute-start.1
  80.6 19.4 %all-to-all-start.2 = ((f32[128,4,128]{2,1,0:T(4,128)}), f32[128,4,128]{2,1,0:T(4,128)S(1)}, u32[]{:S(2)}, u32[]{:S(2)}) async-start(f32[128,4,128]{2,1,0:T(4,128)} %broadcast_in_dim.27), calls=%async_computation.2 | async-start | bytes 524288 | tf_op jit(solution)/shard_map/all_to_all | solution.py:211
  87.5 16.2 %collective-permute-start.3 = (f32[256,256]{1,0:T(8,128)S(1)}, f32[256,256]{1,0:T(8,128)S(1)}, u32[]{:S(2)}, u32[]{:S(2)}) collective-permute-start(f32[256,256]{1,0:T(8,128)S(1)} %get-tuple-element.86), channel_id=1, source_target_pairs={{0,1},{1,0},{2,3},{3,2},{4,5},{5,4},{6,7},{7,6},{8,9},{9,8},{10,11... | collective-permute-start | bytes 786440 | tf_op jit(solution)/shard_map/ppermute | solution.py:227
  100.6 4.3 %collective-permute-start.2 = (f32[2,128,256]{2,1,0:T(8,128)S(1)}, f32[2,128,256]{2,1,0:T(8,128)S(1)}, u32[]{:S(2)}, u32[]{:S(2)}) collective-permute-start(f32[2,128,256]{2,1,0:T(8,128)S(1)} %constant_dynamic-update-slice_fusion.2.mine_ref), channel_id=1, source_target_pairs={{0,1},{1,0},{2,3},{3,2},{4,5},{5,4},{6,7},{7,6},{8,9},{9,8},{10,11... | collective-permute-start | bytes 786440 | tf_op jit(solution)/shard_map/ppermute | solution.py:219
  180.1 0.7 copy-start.4
  180.8 0.7 copy-start.5

commit v4 on v3

--- a/solution.py
+++ b/solution.py
@@ -87,22 +87,58 @@
     )(counts, mine, other, stiffness, mass)
 
 
+def eliminate(work_ref, inverse_ref):
+    n = work_ref.shape[0]
+    row = lax.broadcasted_iota(jnp.int32, (n, n), 0)
+    col = lax.broadcasted_iota(jnp.int32, (n, n), 1)
+    lane = lax.broadcasted_iota(jnp.int32, (1, n), 1)
+    inverse_ref[...] = jnp.where(row == col, 1.0, 0.0)
+
+    def column(k, _):
+        pivot_row = work_ref[pl.ds(k, 1), :]
+        pivot = jnp.sum(jnp.where(lane == k, pivot_row, 0.0), axis=1, keepdims=True)
+        work = work_ref[...]
+        inverse = inverse_ref[...]
+        below = jnp.sum(jnp.where(col == k, work, 0.0), axis=1, keepdims=True) / pivot
+        below = jnp.where(row[:, :1] > k, below, 0.0)
+        inverse_row = inverse_ref[pl.ds(k, 1), :]
+        work_ref[...] = work - below * pivot_row
+        inverse = inverse - below * inverse_row
+        inverse_ref[...] = jnp.where(row == k, inverse * lax.rsqrt(pivot), inverse)
+        return 0
+
+    lax.fori_loop(0, n, column, 0)
+
+
 def ritz_kernel(
-    scale, mine_ref, other_ref, image_ref, extra_ref, rotated_ref, projected_ref, good_ref, gram_ref, inverse_ref
+    scale,
+    mine_ref,
+    other_ref,
+    image_ref,
+    extra_ref,
+    rotated_hbm,
+    projected_hbm,
+    gram_ref,
+    inverse_ref,
+    rotated_ref,
+    projected_ref,
+    sems,
 ):
     rows, n = mine_ref.shape[1:]
     me_blk = lax.axis_index("blk")
-    gram_ref[0, pl.ds(pl.multiple_of(me_blk * rows, rows), rows), :] = mine_ref[0]
-    gram_ref[0, pl.ds(pl.multiple_of((1 - me_blk) * rows, rows), rows), :] = other_ref[0]
-    gram_ref[1, pl.ds(pl.multiple_of(me_blk * rows, rows), rows), :] = mine_ref[1]
-    gram_ref[1, pl.ds(pl.multiple_of((1 - me_blk) * rows, rows), rows), :] = other_ref[1]
+    own = pl.ds(pl.multiple_of(me_blk * rows, rows), rows)
+    far = pl.ds(pl.multiple_of((1 - me_blk) * rows, rows), rows)
+    for plane in range(2):
+        gram_ref[plane, own, :] = mine_ref[plane]
+        gram_ref[plane, far, :] = other_ref[plane]
     row = lax.broadcasted_iota(jnp.int32, (n, n), 0)
     col = lax.broadcasted_iota(jnp.int32, (n, n), 1)
     eye = jnp.where(row == col, 1.0, 0.0)
     weight = jnp.where(row > col, 1.0, 0.5 * eye)
     gram = gram_ref[0]
     gram = 0.5 * (gram + gram.T)
-    on_diag = eye * gram
+    projected_ref[...] = gram
+    on_diag = jnp.where(row == col, gram, 0.0)
     down = lax.rsqrt(jnp.sum(on_diag, axis=1, keepdims=True))
     across = lax.rsqrt(jnp.sum(on_diag, axis=0, keepdims=True))
     scaled = gram * down * across
@@ -127,40 +163,43 @@
         return step + 1, jnp.sum(error * error)
 
     _, size = lax.while_loop(going, correct, (jnp.int32(0), jnp.float32(1.0)))
-    good_ref[0, 0] = jnp.where(size < RESIDUAL, 1, 0).astype(jnp.int32)
-    inverse = inverse_ref[...] * across
+
+    inverse_ref[...] = inverse_ref[...] * across
+
+    @pl.when(jnp.logical_not(size < RESIDUAL))
+    def _():
+        eliminate(projected_ref, inverse_ref)
+
+    inverse = inverse_ref[...]
     rotated_ref[...] = scale * mat_t(image_ref[...] + extra_ref[...], inverse)
+    first = pltpu.make_async_copy(rotated_ref, rotated_hbm, sems.at[0])
+    first.start()
     projected_ref[...] = mat_t(mat(inverse, gram_ref[1]), inverse)
-
-
-def ritz(mine, other, image, extra, scale, me_blk):
-    rows, n = mine.shape[1:]
+    second = pltpu.make_async_copy(projected_ref, projected_hbm, sems.at[1])
+    second.start()
+    first.wait()
+    second.wait()
+
+
+def ritz(mine, other, image, extra, scale):
+    n = mine.shape[2]
     vmem = pl.BlockSpec(memory_space=pltpu.VMEM)
+    hbm = pl.BlockSpec(memory_space=pltpu.HBM)
     square = jax.ShapeDtypeStruct((n, n), jnp.float32)
-    rotated, projected, good = pl.pallas_call(
+    return pl.pallas_call(
         functools.partial(ritz_kernel, scale),
-        out_shape=(square, square, jax.ShapeDtypeStruct((1, 1), jnp.int32)),
+        out_shape=(square, square),
         in_specs=[vmem] * 4,
-        out_specs=(vmem, vmem, pl.BlockSpec(memory_space=pltpu.SMEM)),
-        scratch_shapes=[pltpu.VMEM((2, n, n), jnp.float32), pltpu.VMEM((n, n), jnp.float32)],
+        out_specs=(hbm, hbm),
+        scratch_shapes=[
+            pltpu.VMEM((2, n, n), jnp.float32),
+            pltpu.VMEM((n, n), jnp.float32),
+            pltpu.VMEM((n, n), jnp.float32),
+            pltpu.VMEM((n, n), jnp.float32),
+            pltpu.SemaphoreType.DMA((2,)),
+        ],
         name="ritz",
     )(mine, other, image, extra)
-
-    def direct():
-        low = jnp.where(me_blk == 0, mine, other)
-        high = jnp.where(me_blk == 0, other, mine)
-        gram_m, gram_k = jnp.concatenate([low, high], axis=1)
-        lower = jnp.linalg.cholesky(0.5 * (gram_m + gram_m.T))
-        solved = lax.linalg.triangular_solve(
-            lower, jnp.eye(n, dtype=lower.dtype), left_side=True, lower=True
-        )
-        middle = jnp.dot(solved, gram_k, precision=HIGHEST)
-        return (
-            scale * jnp.dot(image + extra, solved.T, precision=HIGHEST),
-            jnp.dot(middle, solved.T, precision=HIGHEST),
-        )
-
-    return lax.cond(good[0, 0] > 0, lambda: (rotated, projected), direct)
 
 
 def to_pieces(plane):
@@ -227,9 +266,7 @@
     extra_k = lax.ppermute(
         lax.dynamic_index_in_dim(image, 1 - me_blk, 0, keepdims=False), "blk", SWAP
     )
-    return ritz(
-        mine_grams, other_grams, image_k, extra_k, math.sqrt(rows_dev * n_sub), me_blk
-    )
+    return ritz(mine_grams, other_grams, image_k, extra_k, math.sqrt(rows_dev * n_sub))
 
 
 def solution(mesh):

time: 182 us -> 163 us (0.90)
  other arithmetic: 56.4 us -> 2.48 us
  Pallas kernels: 13.8 us -> 59 us
  local copies, waits for them, and re-layouts: 8.97 us -> 4.45 us
  matrix products: 4.35 us -> 1.8 us
  loops' own time: 2.24 us -> 0 us
    another operation x10 -> x0, other arithmetic: 53.7 us -> none  [the longest x6 34 us: direct(): lower = jnp.linalg.cholesky(0.5 * (gram_m + gram_m.T))]
    pallas_call x1, Pallas kernels: 11.4 us -> 56.6 us  [ritz(): pl.pallas_call(functools.partial(ritz_kernel, scale), out_shape=(square,...]
    another operation x12 -> x0, local copies, waits for them, and re-layouts: 4.4 us -> none
    another operation x2 -> x0, loops' own time: 2.24 us -> none  [the longest x1 1.98 us: ritz(): return lax.cond(good[0, 0] > 0, lambda: (rotated, projected), direct)]
  transfers between devices with their start and end apart: 6 -> 6, of which waited for: 4 -> 4; matrix products, arithmetic and copies ran while one was open for 1% -> 2% of each run, Pallas kernels for 0% -> 0%
where the time goes in v4:
time: 163 us; the launch traced here: 162 us
  Pallas kernels  59 us (36%)
  waiting for transfers between devices  31.8 us (20%)
  blocking collectives  31.1 us (19%)
  starting transfers between devices  30.7 us (19%)
  local copies, waits for them, and re-layouts  4.45 us (3%)
  other arithmetic  2.48 us (2%)
  matrix products  1.8 us (1%)
    pallas_call x1, Pallas kernels, ritz(): pl.pallas_call(functools.partial(ritz_kernel, scale), out_shape=(square,...  56.6 us
    all_to_all x1, blocking collectives, per_device(): lax.all_to_all(jnp.concatenate([outgoing, jnp.concatenate(terms, axis=1)]...  31.1 us
    all_to_all x1, waiting for transfers between devices, per_device(): lax.all_to_all(sent.reshape(n_sub, cap_half, width), 'sub', split_axis=0,...  19 us
    all_to_all x1, starting transfers between devices, per_device(): lax.all_to_all(sent.reshape(n_sub, cap_half, width), 'sub', split_axis=0,...  16.5 us
    all_to_all x1, waiting for transfers between devices, per_device(): lax.all_to_all(jnp.broadcast_to(total[None], (n_sub, 4, lanes)), 'sub', s...  10 us
    all_to_all x1, starting transfers between devices, per_device(): lax.all_to_all(jnp.broadcast_to(total[None], (n_sub, 4, lanes)), 'sub', s...  6.36 us
  transfers between devices with their start and end apart: 6, of which 4 were waited for; matrix products, arithmetic and copies ran while one was open for 2% of the time, Pallas kernels for 0%

profile of v4, /device:TPU:1, one launch (start us, length us, event | category | flops | bytes accessed | tf_op | source)
XLA Modules:
  0.0 162.3 jit_solution(8468979993444346578)
XLA Ops:
  0.7 0.7 constant_dynamic-slice_fusion
  1.6 1.3 fusion.4
  2.9 16.5 %all-to-all-start = ((bf16[128,8,256]{2,1,0:T(8,128)(2,1)}), bf16[128,8,256]{2,1,0:T(8,128)(2,1)S(1)}, u32[]{:S(2)}, u32[]{:S(2)}) async-start(bf16[128,8,256]{2,1,0:T(8,128)(2,1)} %fusion.4), calls=%async_computation | async-start | bytes 1048576 | tf_op jit(solution)/shard_map/all_to_all | solution.py:228
  19.5 19.0 %all-to-all-done = bf16[128,8,256]{2,1,0:T(8,128)(2,1)S(1)} async-done(((bf16[128,8,256]{2,1,0:T(8,128)(2,1)}), bf16[128,8,256]{2,1,0:T(8,128)(2,1)S(1)}, u32[]{:S(2)}, u32[]{:S(2)}) %all-to-all-start) | async-done | bytes 524320 | tf_op jit(solution)/shard_map/all_to_all | solution.py:228
  38.5 0.9 fusion.10
  39.6 0.2 bitcast_select_fusion.mine_ref
  39.8 2.6 %collective-permute-start = (bf16[2,512,256]{2,1,0:T(8,128)(2,1)S(1)}, bf16[2,512,256]{2,1,0:T(8,128)(2,1)S(1)}, u32[]{:S(2)}, u32[]{:S(2)}) collective-permute-start(bf16[2,512,256]{2,1,0:T(8,128)(2,1)S(1)} %bitcast_select_fusion.mine_ref), channel_id=1, source_target_pairs={{0,1},{1,0},{2,3},{3,2},{4,5},{5,4},{6,7},{7,6},{8,9},{9,8},{10,11... | collective-permute-start | bytes 1572872 | tf_op jit(solution)/shard_map/ppermute | solution.py:235
  42.3 1.5 collective-permute-done.other_ref
  43.9 2.5 %products.1 = (bf16[2,512,256]{2,1,0:T(8,128)(2,1)S(1)}, f32[2,128,256]{2,1,0:T(8,128)S(1)}, f32[2,128,256]{2,1,0:T(8,128)S(1)}) custom-call(s32[2]{0:T(128)S(1)} %copy-done.3, bf16[2,512,256]{2,1,0:T(8,128)(2,1)S(1)} %bitcast_select_fusion.mine_ref, bf16[2,512,256]{2,1,0:T(8,128)(2,1)S(1)} %collective-permute-done.other_ref, ...), custom_call_target="tpu_custom_call" | custom-call | flops 1400000000 | bytes 6291456 | tf_op jit(solution)/shard_map/products/pallas_call | solution.py:77
  46.3 0.5 collective-permute-start.1
  46.8 0.3 copy.49
  47.1 0.9 fusion.8
  48.4 0.2 copy.37
  48.6 31.1 %all_to_all.15 = bf16[128,8,384]{2,1,0:T(8,128)(2,1)S(1)} all-to-all(bf16[128,8,384]{2,1,0:T(8,128)(2,1)S(1)} %pad_maximum_fusion), channel_id=1, replica_groups=mesh['sub'=128,'blk'=2] {'sub'}, dimensions={0} | all-to-all | bytes 1572864 | tf_op jit(solution)/shard_map/all_to_all | solution.py:241
  79.9 0.7 broadcast_in_dim.25
  80.6 6.4 %all-to-all-start.2 = ((f32[128,4,128]{2,1,0:T(4,128)}), f32[128,4,128]{2,1,0:T(4,128)S(1)}, u32[]{:S(2)}, u32[]{:S(2)}) async-start(f32[128,4,128]{2,1,0:T(4,128)} %broadcast_in_dim.25), calls=%async_computation.2 | async-start | bytes 524288 | tf_op jit(solution)/shard_map/all_to_all | solution.py:250
  87.0 0.5 fusion.1
  87.5 0.8 dynamic-slice_bitcast_fusion
  88.2 1.7 %collective-permute-start.3 = (f32[256,256]{1,0:T(8,128)S(1)}, f32[256,256]{1,0:T(8,128)S(1)}, u32[]{:S(2)}, u32[]{:S(2)}) collective-permute-start(f32[256,256]{1,0:T(8,128)S(1)} %get-tuple-element.9), channel_id=1, source_target_pairs={{0,1},{1,0},{2,3},{3,2},{4,5},{5,4},{6,7},{7,6},{8,9},{9,8},{10,11... | collective-permute-start | bytes 786440 | tf_op jit(solution)/shard_map/ppermute | solution.py:266
  90.0 10.0 %all-to-all-done.2 = f32[128,4,128]{2,1,0:T(4,128)S(1)} async-done(((f32[128,4,128]{2,1,0:T(4,128)}), f32[128,4,128]{2,1,0:T(4,128)S(1)}, u32[]{:S(2)}, u32[]{:S(2)}) %all-to-all-start.2) | async-done | bytes 262176 | tf_op jit(solution)/shard_map/all_to_all | solution.py:250
  100.6 3.1 %collective-permute-start.2 = (f32[2,128,256]{2,1,0:T(8,128)S(1)}, f32[2,128,256]{2,1,0:T(8,128)S(1)}, u32[]{:S(2)}, u32[]{:S(2)}) collective-permute-start(f32[2,128,256]{2,1,0:T(8,128)S(1)} %constant_dynamic-update-slice_fusion.mine_ref), channel_id=1, source_target_pairs={{0,1},{1,0},{2,3},{3,2},{4,5},{5,4},{6,7},{7,6},{8,9},{9,8},{10,11... | collective-permute-start | bytes 786440 | tf_op jit(solution)/shard_map/ppermute | solution.py:258
  103.7 1.2 collective-permute-done.2.other_ref
  104.9 0.7 copy-done.6
  105.6 56.6 %ritz.1 = (f32[256,256]{1,0:T(8,128)}, f32[256,256]{1,0:T(8,128)}) custom-call(f32[2,128,256]{2,1,0:T(8,128)} %copy-done.4, f32[2,128,256]{2,1,0:T(8,128)} %copy-done.6, f32[256,256]{1,0:T(8,128)} %get-tuple-element.10.image_ref, f32[256,256]{1,0:T(8,128)} %copy-done.5), custom_call_target="tpu_custom_call" | custom-call | tf_op jit(solution)/shard_map/ritz/pallas_call | solution.py:189
  (40 shorter events, 1.5 us)
Async XLA Ops:
  0.6 1.0 copy-start
  0.6 18.8 %copy-start.3 = (s32[2]{0:T(128)S(1)}, s32[2]{0:T(128)}, u32[]{:S(2)}) copy-start(s32[2]{0:T(128)} %counts_ref.1) | copy-start | bytes 28
  2.9 41.0 %copy-start.1 = (bf16[2,512,1024]{2,1,0:T(8,128)(2,1)S(1)}, bf16[2,512,1024]{2,1,0:T(8,128)(2,1)}, u32[]{:S(2)}) copy-start(bf16[2,512,1024]{2,1,0:T(8,128)(2,1)} %stiff_ref.1) | copy-start | bytes 6291460
  2.9 35.6 %all-to-all-start = ((bf16[128,8,256]{2,1,0:T(8,128)(2,1)}), bf16[128,8,256]{2,1,0:T(8,128)(2,1)S(1)}, u32[]{:S(2)}, u32[]{:S(2)}) async-start(bf16[128,8,256]{2,1,0:T(8,128)(2,1)} %fusion.4), calls=%async_computation | async-start | bytes 1048576 | tf_op jit(solution)/shard_map/all_to_all | solution.py:228
  38.5 5.3 %copy-start.2 = (bf16[2,512,1024]{2,1,0:T(8,128)(2,1)S(1)}, bf16[2,512,1024]{2,1,0:T(8,128)(2,1)}, u32[]{:S(2)}) copy-start(bf16[2,512,1024]{2,1,0:T(8,128)(2,1)} %mass_ref.1) | copy-start | bytes 6291460
  39.8 4.1 %collective-permute-start = (bf16[2,512,256]{2,1,0:T(8,128)(2,1)S(1)}, bf16[2,512,256]{2,1,0:T(8,128)(2,1)S(1)}, u32[]{:S(2)}, u32[]{:S(2)}) collective-permute-start(bf16[2,512,256]{2,1,0:T(8,128)(2,1)S(1)} %bitcast_select_fusion.mine_ref), channel_id=1, source_target_pairs={{0,1},{1,0},{2,3},{3,2},{4,5},{5,4},{6,7},{7,6},{8,9},{9,8},{10,11... | collective-permute-start | bytes 1572872 | tf_op jit(solution)/shard_map/ppermute | solution.py:235
  46.3 1.7 %collective-permute-start.1 = (f32[2,128,256]{2,1,0:T(8,128)S(1)}, f32[2,128,256]{2,1,0:T(8,128)S(1)}, u32[]{:S(2)}, u32[]{:S(2)}) collective-permute-start(f32[2,128,256]{2,1,0:T(8,128)S(1)} %get-tuple-element.8), channel_id=1, source_target_pairs={{0,1},{1,0},{2,3},{3,2},{4,5},{5,4},{6,7},{7,6},{8,9},{9,8},{10,11... | collective-permute-start | bytes 786440 | tf_op jit(solution)/shard_map/ppermute | solution.py:237
  80.6 19.4 %all-to-all-start.2 = ((f32[128,4,128]{2,1,0:T(4,128)}), f32[128,4,128]{2,1,0:T(4,128)S(1)}, u32[]{:S(2)}, u32[]{:S(2)}) async-start(f32[128,4,128]{2,1,0:T(4,128)} %broadcast_in_dim.25), calls=%async_computation.2 | async-start | bytes 524288 | tf_op jit(solution)/shard_map/all_to_all | solution.py:250
  88.2 15.5 %collective-permute-start.3 = (f32[256,256]{1,0:T(8,128)S(1)}, f32[256,256]{1,0:T(8,128)S(1)}, u32[]{:S(2)}, u32[]{:S(2)}) collective-permute-start(f32[256,256]{1,0:T(8,128)S(1)} %get-tuple-element.9), channel_id=1, source_target_pairs={{0,1},{1,0},{2,3},{3,2},{4,5},{5,4},{6,7},{7,6},{8,9},{9,8},{10,11... | collective-permute-start | bytes 786440 | tf_op jit(solution)/shard_map/ppermute | solution.py:266
  100.6 4.3 %copy-start.4 = (f32[2,128,256]{2,1,0:T(8,128)}, f32[2,128,256]{2,1,0:T(8,128)S(1)}, u32[]{:S(2)}) copy-start(f32[2,128,256]{2,1,0:T(8,128)S(1)} %constant_dynamic-update-slice_fusion.mine_ref) | copy-start | bytes 786436
  100.6 4.3 %collective-permute-start.2 = (f32[2,128,256]{2,1,0:T(8,128)S(1)}, f32[2,128,256]{2,1,0:T(8,128)S(1)}, u32[]{:S(2)}, u32[]{:S(2)}) collective-permute-start(f32[2,128,256]{2,1,0:T(8,128)S(1)} %constant_dynamic-update-slice_fusion.mine_ref), channel_id=1, source_target_pairs={{0,1},{1,0},{2,3},{3,2},{4,5},{5,4},{6,7},{7,6},{8,9},{9,8},{10,11... | collective-permute-start | bytes 786440 | tf_op jit(solution)/shard_map/ppermute | solution.py:258
  103.7 1.2 copy-start.5
  104.9 0.7 copy-start.6

commit v5 on v4

--- a/solution.py
+++ b/solution.py
@@ -11,7 +11,6 @@
 SWAP = ((0, 1), (1, 0))
 MAX_STEPS = 7
 RESIDUAL = 1e-6
-HIGHEST = lax.Precision.HIGHEST
 
 
 def select_rows(index, count):
@@ -22,18 +21,6 @@
 def two_terms(value):
     upper = lax.reduce_precision(value, exponent_bits=8, mantissa_bits=7)
     return upper.astype(jnp.bfloat16), (value - upper).astype(jnp.bfloat16)
-
-
-def mat(left, right):
-    return lax.dot_general(
-        left, right, (((1,), (0,)), ((), ())), precision=HIGHEST, preferred_element_type=jnp.float32
-    )
-
-
-def mat_t(left, right):
-    return lax.dot_general(
-        left, right, (((1,), (1,)), ((), ())), precision=HIGHEST, preferred_element_type=jnp.float32
-    )
 
 
 def short(left, right, side):
@@ -45,24 +32,50 @@
     )
 
 
-def product_kernel(counts_ref, mine_ref, other_ref, stiff_ref, mass_ref, part_ref, keep_ref, send_ref):
-    sub_dev, half, width = mine_ref.shape
+def long(left, right, side):
+    left_top = left.astype(jnp.bfloat16)
+    left_rest = left - left_top.astype(jnp.float32)
+    right_top = right.astype(jnp.bfloat16)
+    right_rest = right - right_top.astype(jnp.float32)
+    small = short(left_top, right_rest, side) + short(left_rest, right_top, side)
+    return small + short(left_top, right_top, side)
+
+
+def halves(half):
     me_blk = lax.axis_index("blk")
-    first = me_blk == 0
     own = pl.ds(pl.multiple_of(me_blk * half, half), half)
     far = pl.ds(pl.multiple_of((1 - me_blk) * half, half), half)
+    return me_blk, own, far
+
+
+def own_kernel(mine_ref, stiff_ref, mass_ref, partial_ref):
+    sub_dev, half, _ = mine_ref.shape
+    _, own, _ = halves(half)
+    for place, matrix_ref in enumerate((mass_ref, stiff_ref)):
+        for s in range(sub_dev):
+            partial_ref[place, s] = jnp.dot(
+                matrix_ref[s, :, own], mine_ref[s], preferred_element_type=jnp.float32
+            )
+
+
+def far_kernel(
+    counts_ref, partial_ref, mine_ref, other_ref, stiff_ref, mass_ref, part_ref, keep_ref, send_ref
+):
+    sub_dev, half, width = mine_ref.shape
+    me_blk, _, far = halves(half)
+    first = me_blk == 0
     slot = me_blk * half + lax.broadcasted_iota(jnp.int32, (half, width), 0)
     for place, matrix_ref in enumerate((mass_ref, stiff_ref)):
         gram = None
         for s in range(sub_dev):
-            mine = mine_ref[s]
-            part = jnp.dot(matrix_ref[s, :, own], mine, preferred_element_type=jnp.float32)
-            part += jnp.dot(matrix_ref[s, :, far], other_ref[s], preferred_element_type=jnp.float32)
+            part = partial_ref[place, s] + jnp.dot(
+                matrix_ref[s, :, far], other_ref[s], preferred_element_type=jnp.float32
+            )
             part = jnp.where(slot < counts_ref[s], part, 0.0).astype(jnp.bfloat16)
             if place == 1:
                 part_ref[s] = part
             term = lax.dot_general(
-                mine, part, (((0,), (0,)), ((), ())), preferred_element_type=jnp.float32
+                mine_ref[s], part, (((0,), (0,)), ((), ())), preferred_element_type=jnp.float32
             )
             gram = term if gram is None else gram + term
         low, high = gram[: width // 2], gram[width // 2 :]
@@ -73,18 +86,26 @@
 def products(counts, mine, other, stiffness, mass):
     sub_dev, half, width = mine.shape
     vmem = pl.BlockSpec(memory_space=pltpu.VMEM)
+    params = pltpu.CompilerParams(vmem_limit_bytes=20 << 20)
+    partial = pl.pallas_call(
+        own_kernel,
+        out_shape=jax.ShapeDtypeStruct((2, sub_dev, half, width), jnp.float32),
+        in_specs=[vmem] * 3,
+        out_specs=vmem,
+        compiler_params=params,
+        cost_estimate=pl.CostEstimate(flops=540000000, bytes_accessed=4 << 20, transcendentals=0),
+        name="own_half",
+    )(mine, stiffness, mass)
     gram = jax.ShapeDtypeStruct((2, width // 2, width), jnp.float32)
     return pl.pallas_call(
-        product_kernel,
+        far_kernel,
         out_shape=(jax.ShapeDtypeStruct(mine.shape, jnp.bfloat16), gram, gram),
-        in_specs=[pl.BlockSpec(memory_space=pltpu.SMEM)] + [vmem] * 4,
+        in_specs=[pl.BlockSpec(memory_space=pltpu.SMEM)] + [vmem] * 5,
         out_specs=(vmem, vmem, vmem),
-        compiler_params=pltpu.CompilerParams(vmem_limit_bytes=24 << 20),
-        cost_estimate=pl.CostEstimate(
-            flops=1400000000, bytes_accessed=6 << 20, transcendentals=0
-        ),
-        name="products",
-    )(counts, mine, other, stiffness, mass)
+        compiler_params=params,
+        cost_estimate=pl.CostEstimate(flops=810000000, bytes_accessed=4 << 20, transcendentals=0),
+        name="far_half",
+    )(counts, partial, mine, other, stiffness, mass)
 
 
 def eliminate(work_ref, inverse_ref):
@@ -141,15 +162,14 @@
     on_diag = jnp.where(row == col, gram, 0.0)
     down = lax.rsqrt(jnp.sum(on_diag, axis=1, keepdims=True))
     across = lax.rsqrt(jnp.sum(on_diag, axis=0, keepdims=True))
-    scaled = gram * down * across
-    gram_ref[0] = scaled
-    rest = scaled - eye
+    rest = jnp.where(row == col, 0.0, gram * down * across)
+    gram_ref[0] = rest
     off = -weight * rest
     for _ in range(2):
         left = rest + off + short(off, rest, 0)
         step = weight * (left + off.T + short(left, off, 1))
         off = off - step - short(step, off, 0)
-    inverse_ref[...] = eye + off
+    inverse_ref[...] = off
 
     def going(state):
         step, size = state
@@ -157,24 +177,26 @@
 
     def correct(state):
         step, _ = state
-        inverse = inverse_ref[...]
-        error = mat_t(mat(inverse, gram_ref[0]), inverse) - eye
-        inverse_ref[...] = inverse - mat(weight * error, inverse)
+        off = inverse_ref[...]
+        rest = gram_ref[0]
+        left = rest + off + long(off, rest, 0)
+        error = left + off.T + long(left, off, 1)
+        change = weight * error
+        inverse_ref[...] = off - change - long(change, off, 0)
         return step + 1, jnp.sum(error * error)
 
     _, size = lax.while_loop(going, correct, (jnp.int32(0), jnp.float32(1.0)))
-
-    inverse_ref[...] = inverse_ref[...] * across
+    inverse_ref[...] = (eye + inverse_ref[...]) * across
 
     @pl.when(jnp.logical_not(size < RESIDUAL))
     def _():
         eliminate(projected_ref, inverse_ref)
 
     inverse = inverse_ref[...]
-    rotated_ref[...] = scale * mat_t(image_ref[...] + extra_ref[...], inverse)
+    rotated_ref[...] = scale * long(image_ref[...] + extra_ref[...], inverse, 1)
     first = pltpu.make_async_copy(rotated_ref, rotated_hbm, sems.at[0])
     first.start()
-    projected_ref[...] = mat_t(mat(inverse, gram_ref[1]), inverse)
+    projected_ref[...] = long(long(inverse, gram_ref[1], 0), inverse, 1)
     second = pltpu.make_async_copy(projected_ref, projected_hbm, sems.at[1])
     second.start()
     first.wait()
@@ -198,6 +220,7 @@
             pltpu.VMEM((n, n), jnp.float32),
             pltpu.SemaphoreType.DMA((2,)),
         ],
+        compiler_params=pltpu.CompilerParams(vmem_limit_bytes=16 << 20),
         name="ritz",
     )(mine, other, image, extra)
 
@@ -228,7 +251,8 @@
     received = lax.all_to_all(
         sent.reshape(n_sub, cap_half, width), "sub", split_axis=0, concat_axis=0, tiled=True
     )
-    mine = jnp.roll(received, -me_sub, axis=0).transpose(1, 0, 2).reshape(sub_dev, half, width)
+    received = lax.optimization_barrier(jnp.roll(received, -me_sub, axis=0))
+    mine = received.transpose(1, 0, 2).reshape(sub_dev, half, width)
     slots = me_blk * half + jnp.arange(half, dtype=jnp.int32)
     my_live = (slots[None, :] < counts[:, None])[:, :, None]
     mine = jnp.where(my_live, mine, jnp.zeros((), jnp.bfloat16))

time: 163 us -> 156 us (0.957)
  Pallas kernels: 59 us -> 54.2 us
    pallas_call x1, Pallas kernels: 56.6 us -> 51.6 us  [ritz(): pl.pallas_call(functools.partial(ritz_kernel, scale), out_shape=(square,...]
where the time goes in v5:
time: 156 us
  Pallas kernels  54.2 us (35%)
  waiting for transfers between devices  31.6 us (20%)
  blocking collectives  31.1 us (20%)
  starting transfers between devices  30.7 us (20%)
  local copies, waits for them, and re-layouts  3.04 us (2%)
  other arithmetic  2.48 us (2%)
  matrix products  1.81 us (1%)
    pallas_call x1, Pallas kernels, ritz(): pl.pallas_call(functools.partial(ritz_kernel, scale), out_shape=(square,...  51.6 us
    all_to_all x1, blocking collectives, per_device(): lax.all_to_all(jnp.concatenate([outgoing, jnp.concatenate(terms, axis=1)]...  31.1 us
    all_to_all x1, waiting for transfers between devices, per_device(): lax.all_to_all(sent.reshape(n_sub, cap_half, width), 'sub', split_axis=0,...  19 us
    all_to_all x1, starting transfers between devices, per_device(): lax.all_to_all(sent.reshape(n_sub, cap_half, width), 'sub', split_axis=0,...  16.5 us
    all_to_all x1, waiting for transfers between devices, per_device(): lax.all_to_all(jnp.broadcast_to(total[None], (n_sub, 4, lanes)), 'sub', s...  10.6 us
    all_to_all x1, starting transfers between devices, per_device(): lax.all_to_all(jnp.broadcast_to(total[None], (n_sub, 4, lanes)), 'sub', s...  6.36 us
  transfers between devices with their start and end apart: 6, of which 4 were waited for; matrix products, arithmetic and copies ran while one was open for 2% of the time, Pallas kernels for 0%

profile of v5, /device:TPU:1, one launch (start us, length us, event | category | flops | bytes accessed | tf_op | source)
XLA Modules:
  0.0 156.1 jit_solution(8343725872003942964)
XLA Ops:
  0.7 0.7 constant_dynamic-slice_fusion
  1.6 1.3 fusion.4
  2.9 16.5 %all-to-all-start = ((bf16[128,8,256]{2,1,0:T(8,128)(2,1)}), bf16[128,8,256]{2,1,0:T(8,128)(2,1)S(1)}, u32[]{:S(2)}, u32[]{:S(2)}) async-start(bf16[128,8,256]{2,1,0:T(8,128)(2,1)} %fusion.4), calls=%async_computation | async-start | bytes 1048576 | tf_op jit(solution)/shard_map/all_to_all | solution.py:251
  19.5 19.0 %all-to-all-done = bf16[128,8,256]{2,1,0:T(8,128)(2,1)S(1)} async-done(((bf16[128,8,256]{2,1,0:T(8,128)(2,1)}), bf16[128,8,256]{2,1,0:T(8,128)(2,1)S(1)}, u32[]{:S(2)}, u32[]{:S(2)}) %all-to-all-start) | async-done | bytes 524320 | tf_op jit(solution)/shard_map/all_to_all | solution.py:251
  38.6 0.9 fusion.9
  39.6 0.2 bitcast_select_fusion.mine_ref
  39.8 2.6 %collective-permute-start = (bf16[2,512,256]{2,1,0:T(8,128)(2,1)S(1)}, bf16[2,512,256]{2,1,0:T(8,128)(2,1)S(1)}, u32[]{:S(2)}, u32[]{:S(2)}) collective-permute-start(bf16[2,512,256]{2,1,0:T(8,128)(2,1)S(1)} %bitcast_select_fusion.mine_ref), channel_id=1, source_target_pairs={{0,1},{1,0},{2,3},{3,2},{4,5},{5,4},{6,7},{7,6},{8,9},{9,8},{10,11... | collective-permute-start | bytes 1572872 | tf_op jit(solution)/shard_map/ppermute | solution.py:259
  42.4 0.7 own_half.1.partial_ref
  43.1 0.8 collective-permute-done.other_ref
  43.9 1.9 %far_half.1 = (bf16[2,512,256]{2,1,0:T(8,128)(2,1)S(1)}, f32[2,128,256]{2,1,0:T(8,128)S(1)}, f32[2,128,256]{2,1,0:T(8,128)S(1)}) custom-call(s32[2]{0:T(128)S(1)} %copy-done.3, f32[2,2,512,256]{3,2,1,0:T(8,128)S(1)} %own_half.1.partial_ref, bf16[2,512,256]{2,1,0:T(8,128)(2,1)S(1)} %bitcast_select_fusion.mine_ref, ...), custom_call_target="tpu_custom_call" | custom-call | flops 810000000 | bytes 4194304 | tf_op jit(solution)/shard_map/far_half/pallas_call | solution.py:100
  45.8 0.5 collective-permute-start.1
  46.3 0.3 copy.49
  46.6 0.9 fusion.8
  47.8 0.2 copy.37
  48.1 31.1 %all_to_all.15 = bf16[128,8,384]{2,1,0:T(8,128)(2,1)S(1)} all-to-all(bf16[128,8,384]{2,1,0:T(8,128)(2,1)S(1)} %pad_maximum_fusion), channel_id=1, replica_groups=mesh['sub'=128,'blk'=2] {'sub'}, dimensions={0} | all-to-all | bytes 1572864 | tf_op jit(solution)/shard_map/all_to_all | solution.py:265
  79.2 0.1 convert_reduce_fusion
  79.3 0.7 broadcast_in_dim.25
  80.1 6.4 %all-to-all-start.2 = ((f32[128,4,128]{2,1,0:T(4,128)}), f32[128,4,128]{2,1,0:T(4,128)S(1)}, u32[]{:S(2)}, u32[]{:S(2)}) async-start(f32[128,4,128]{2,1,0:T(4,128)} %broadcast_in_dim.25), calls=%async_computation.2 | async-start | bytes 524288 | tf_op jit(solution)/shard_map/all_to_all | solution.py:274
  86.5 0.5 fusion.1
  87.0 1.8 %collective-permute-start.3 = (f32[256,256]{1,0:T(8,128)S(1)}, f32[256,256]{1,0:T(8,128)S(1)}, u32[]{:S(2)}, u32[]{:S(2)}) collective-permute-start(f32[256,256]{1,0:T(8,128)S(1)} %get-tuple-element.9), channel_id=1, source_target_pairs={{0,1},{1,0},{2,3},{3,2},{4,5},{5,4},{6,7},{7,6},{8,9},{9,8},{10,11... | collective-permute-start | bytes 786440 | tf_op jit(solution)/shard_map/ppermute | solution.py:290
  88.8 10.6 %all-to-all-done.2 = f32[128,4,128]{2,1,0:T(4,128)S(1)} async-done(((f32[128,4,128]{2,1,0:T(4,128)}), f32[128,4,128]{2,1,0:T(4,128)S(1)}, u32[]{:S(2)}, u32[]{:S(2)}) %all-to-all-start.2) | async-done | bytes 262176 | tf_op jit(solution)/shard_map/all_to_all | solution.py:274
  100.1 3.1 %collective-permute-start.2 = (f32[2,128,256]{2,1,0:T(8,128)S(1)}, f32[2,128,256]{2,1,0:T(8,128)S(1)}, u32[]{:S(2)}, u32[]{:S(2)}) collective-permute-start(f32[2,128,256]{2,1,0:T(8,128)S(1)} %constant_dynamic-update-slice_fusion.mine_ref), channel_id=1, source_target_pairs={{0,1},{1,0},{2,3},{3,2},{4,5},{5,4},{6,7},{7,6},{8,9},{9,8},{10,11... | collective-permute-start | bytes 786440 | tf_op jit(solution)/shard_map/ppermute | solution.py:282
  103.2 1.2 collective-permute-done.2.other_ref
  104.3 51.6 %ritz.1 = (f32[256,256]{1,0:T(8,128)}, f32[256,256]{1,0:T(8,128)}) custom-call(f32[2,128,256]{2,1,0:T(8,128)S(1)} %constant_dynamic-update-slice_fusion.mine_ref, f32[2,128,256]{2,1,0:T(8,128)S(1)} %collective-permute-done.2.other_ref, f32[256,256]{1,0:T(8,128)S(1)} %get-tuple-element.10.image_ref, f32[256,256]{1,0:T(8,128)S(1)} %collective-permute-done.3.extra_ref), custom_call_target="tpu_custom_call" | custom-call | tf_op jit(solution)/shard_map/ritz/pallas_call | solution.py:211
  (35 shorter events, 1.4 us)
Async XLA Ops:
  0.6 1.0 copy-start
  0.6 18.8 %copy-start.3 = (s32[2]{0:T(128)S(1)}, s32[2]{0:T(128)}, u32[]{:S(2)}) copy-start(s32[2]{0:T(128)} %counts_ref.1) | copy-start | bytes 28
  2.9 39.4 %copy-start.1 = (bf16[2,512,1024]{2,1,0:T(8,128)(2,1)S(1)}, bf16[2,512,1024]{2,1,0:T(8,128)(2,1)}, u32[]{:S(2)}) copy-start(bf16[2,512,1024]{2,1,0:T(8,128)(2,1)} %stiff_ref.3) | copy-start | bytes 6291460
  2.9 35.6 %all-to-all-start = ((bf16[128,8,256]{2,1,0:T(8,128)(2,1)}), bf16[128,8,256]{2,1,0:T(8,128)(2,1)S(1)}, u32[]{:S(2)}, u32[]{:S(2)}) async-start(bf16[128,8,256]{2,1,0:T(8,128)(2,1)} %fusion.4), calls=%async_computation | async-start | bytes 1048576 | tf_op jit(solution)/shard_map/all_to_all | solution.py:251
  38.6 3.8 %copy-start.2 = (bf16[2,512,1024]{2,1,0:T(8,128)(2,1)S(1)}, bf16[2,512,1024]{2,1,0:T(8,128)(2,1)}, u32[]{:S(2)}) copy-start(bf16[2,512,1024]{2,1,0:T(8,128)(2,1)} %mass_ref.3) | copy-start | bytes 6291460
  39.8 4.1 %collective-permute-start = (bf16[2,512,256]{2,1,0:T(8,128)(2,1)S(1)}, bf16[2,512,256]{2,1,0:T(8,128)(2,1)S(1)}, u32[]{:S(2)}, u32[]{:S(2)}) collective-permute-start(bf16[2,512,256]{2,1,0:T(8,128)(2,1)S(1)} %bitcast_select_fusion.mine_ref), channel_id=1, source_target_pairs={{0,1},{1,0},{2,3},{3,2},{4,5},{5,4},{6,7},{7,6},{8,9},{9,8},{10,11... | collective-permute-start | bytes 1572872 | tf_op jit(solution)/shard_map/ppermute | solution.py:259
  45.8 1.7 %collective-permute-start.1 = (f32[2,128,256]{2,1,0:T(8,128)S(1)}, f32[2,128,256]{2,1,0:T(8,128)S(1)}, u32[]{:S(2)}, u32[]{:S(2)}) collective-permute-start(f32[2,128,256]{2,1,0:T(8,128)S(1)} %get-tuple-element.8), channel_id=1, source_target_pairs={{0,1},{1,0},{2,3},{3,2},{4,5},{5,4},{6,7},{7,6},{8,9},{9,8},{10,11... | collective-permute-start | bytes 786440 | tf_op jit(solution)/shard_map/ppermute | solution.py:261
  80.1 19.4 %all-to-all-start.2 = ((f32[128,4,128]{2,1,0:T(4,128)}), f32[128,4,128]{2,1,0:T(4,128)S(1)}, u32[]{:S(2)}, u32[]{:S(2)}) async-start(f32[128,4,128]{2,1,0:T(4,128)} %broadcast_in_dim.25), calls=%async_computation.2 | async-start | bytes 524288 | tf_op jit(solution)/shard_map/all_to_all | solution.py:274
  87.0 16.2 %collective-permute-start.3 = (f32[256,256]{1,0:T(8,128)S(1)}, f32[256,256]{1,0:T(8,128)S(1)}, u32[]{:S(2)}, u32[]{:S(2)}) collective-permute-start(f32[256,256]{1,0:T(8,128)S(1)} %get-tuple-element.9), channel_id=1, source_target_pairs={{0,1},{1,0},{2,3},{3,2},{4,5},{5,4},{6,7},{7,6},{8,9},{9,8},{10,11... | collective-permute-start | bytes 786440 | tf_op jit(solution)/shard_map/ppermute | solution.py:290
  100.1 4.3 %collective-permute-start.2 = (f32[2,128,256]{2,1,0:T(8,128)S(1)}, f32[2,128,256]{2,1,0:T(8,128)S(1)}, u32[]{:S(2)}, u32[]{:S(2)}) collective-permute-start(f32[2,128,256]{2,1,0:T(8,128)S(1)} %constant_dynamic-update-slice_fusion.mine_ref), channel_id=1, source_target_pairs={{0,1},{1,0},{2,3},{3,2},{4,5},{5,4},{6,7},{7,6},{8,9},{9,8},{10,11... | collective-permute-start | bytes 786440 | tf_op jit(solution)/shard_map/ppermute | solution.py:282

commit v6 on v5

--- a/solution.py
+++ b/solution.py
@@ -4,6 +4,7 @@
 import jax
 import jax.numpy as jnp
 from jax import lax
+from jax.experimental.layout import Layout, with_layout_constraint
 from jax.experimental import pallas as pl
 from jax.experimental.pallas import tpu as pltpu
 from jax.sharding import PartitionSpec as P
@@ -48,9 +49,11 @@
     return me_blk, own, far
 
 
-def own_kernel(mine_ref, stiff_ref, mass_ref, partial_ref):
+def own_kernel(mine_ref, stiff_ref, mass_ref, partial_ref, turned_ref):
     sub_dev, half, _ = mine_ref.shape
     _, own, _ = halves(half)
+    for s in range(sub_dev):
+        turned_ref[s] = mine_ref[s].T
     for place, matrix_ref in enumerate((mass_ref, stiff_ref)):
         for s in range(sub_dev):
             partial_ref[place, s] = jnp.dot(
@@ -59,9 +62,9 @@
 
 
 def far_kernel(
-    counts_ref, partial_ref, mine_ref, other_ref, stiff_ref, mass_ref, part_ref, keep_ref, send_ref
+    counts_ref, partial_ref, turned_ref, other_ref, stiff_ref, mass_ref, part_ref, keep_ref, send_ref
 ):
-    sub_dev, half, width = mine_ref.shape
+    sub_dev, half, width = other_ref.shape
     me_blk, _, far = halves(half)
     first = me_blk == 0
     slot = me_blk * half + lax.broadcasted_iota(jnp.int32, (half, width), 0)
@@ -74,9 +77,7 @@
             part = jnp.where(slot < counts_ref[s], part, 0.0).astype(jnp.bfloat16)
             if place == 1:
                 part_ref[s] = part
-            term = lax.dot_general(
-                mine_ref[s], part, (((0,), (0,)), ((), ())), preferred_element_type=jnp.float32
-            )
+            term = jnp.dot(turned_ref[s], part, preferred_element_type=jnp.float32)
             gram = term if gram is None else gram + term
         low, high = gram[: width // 2], gram[width // 2 :]
         keep_ref[place] = jnp.where(first, low, high)
@@ -87,11 +88,14 @@
     sub_dev, half, width = mine.shape
     vmem = pl.BlockSpec(memory_space=pltpu.VMEM)
     params = pltpu.CompilerParams(vmem_limit_bytes=20 << 20)
-    partial = pl.pallas_call(
+    partial, turned = pl.pallas_call(
         own_kernel,
-        out_shape=jax.ShapeDtypeStruct((2, sub_dev, half, width), jnp.float32),
+        out_shape=(
+            jax.ShapeDtypeStruct((2, sub_dev, half, width), jnp.float32),
+            jax.ShapeDtypeStruct((sub_dev, width, half), jnp.bfloat16),
+        ),
         in_specs=[vmem] * 3,
-        out_specs=vmem,
+        out_specs=(vmem, vmem),
         compiler_params=params,
         cost_estimate=pl.CostEstimate(flops=540000000, bytes_accessed=4 << 20, transcendentals=0),
         name="own_half",
@@ -105,7 +109,7 @@
         compiler_params=params,
         cost_estimate=pl.CostEstimate(flops=810000000, bytes_accessed=4 << 20, transcendentals=0),
         name="far_half",
-    )(counts, partial, mine, other, stiffness, mass)
+    )(counts, partial, turned, other, stiffness, mass)
 
 
 def eliminate(work_ref, inverse_ref):
@@ -225,14 +229,16 @@
     )(mine, other, image, extra)
 
 
-def to_pieces(plane):
-    rows, wide = plane.shape
-    return plane.reshape(rows // 2, 2, 2, wide // 2).transpose(2, 0, 1, 3).reshape(rows, 2, wide // 2)
+def to_pieces(planes):
+    n, rows, wide = planes.shape
+    pieces = planes.reshape(n, 2, rows // 2, 2, wide // 2).transpose(3, 2, 0, 1, 4)
+    return pieces.reshape(rows, 2 * n, wide // 2)
 
 
 def from_pieces(pieces):
-    rows, _, lanes = pieces.shape
-    return pieces.reshape(2, rows // 2, 2, lanes).transpose(1, 2, 0, 3).reshape(rows, 2 * lanes)
+    rows, double, lanes = pieces.shape
+    planes = pieces.reshape(2, rows // 2, double // 2, 2, lanes).transpose(2, 3, 1, 0, 4)
+    return planes.reshape(double // 2, rows, 2 * lanes)
 
 
 def per_device(basis, stiffness, mass, owner_rows, counts):
@@ -251,26 +257,26 @@
     received = lax.all_to_all(
         sent.reshape(n_sub, cap_half, width), "sub", split_axis=0, concat_axis=0, tiled=True
     )
-    received = lax.optimization_barrier(jnp.roll(received, -me_sub, axis=0))
-    mine = received.transpose(1, 0, 2).reshape(sub_dev, half, width)
+    received = with_layout_constraint(received.transpose(1, 0, 2), Layout((0, 1, 2)))
+    mine = jnp.roll(received, -me_sub, axis=1).reshape(sub_dev, half, width)
     slots = me_blk * half + jnp.arange(half, dtype=jnp.int32)
     my_live = (slots[None, :] < counts[:, None])[:, :, None]
     mine = jnp.where(my_live, mine, jnp.zeros((), jnp.bfloat16))
     other = lax.ppermute(mine, "blk", SWAP)
     stiff_part, keep, send = products(counts, mine, other, stiffness, mass)
     grams = keep + lax.ppermute(send, "blk", SWAP)
-    terms = [to_pieces(term) for plane in (grams[0], grams[1]) for term in two_terms(plane)]
+    terms = to_pieces(jnp.concatenate(two_terms(grams)))
     outgoing = stiff_part.reshape(cap_half, n_sub, width).transpose(1, 0, 2)
     outgoing = jnp.roll(outgoing, me_sub, axis=0)
     back = lax.all_to_all(
-        jnp.concatenate([outgoing, jnp.concatenate(terms, axis=1)], axis=2),
+        jnp.concatenate([outgoing, terms], axis=2),
         "sub",
         split_axis=0,
         concat_axis=0,
         tiled=True,
     )
-    total = jnp.sum(back[:, :, width:].astype(jnp.float32), axis=0).reshape(2, 2, 2, lanes)
-    total = jnp.sum(total, axis=1).reshape(4, lanes)
+    total = jnp.sum(back[:, :, width:].astype(jnp.float32), axis=0)
+    total = total[:4] + total[4:]
     spread = lax.all_to_all(
         jnp.broadcast_to(total[None], (n_sub, 4, lanes)),
         "sub",
@@ -278,7 +284,7 @@
         concat_axis=0,
         tiled=True,
     )
-    mine_grams = jnp.stack([from_pieces(spread[:, :2]), from_pieces(spread[:, 2:])])
+    mine_grams = from_pieces(spread)
     other_grams = lax.ppermute(mine_grams, "blk", SWAP)
     image = jnp.einsum(
         "tr,tc->rc",

time: 156 us -> 155 us (level)
  transfers between devices with their start and end apart: 6 -> 6, of which waited for: 4 -> 4; matrix products, arithmetic and copies ran while one was open for 2% -> 1% of each run, Pallas kernels for 0% -> 0%
where the time goes in v6:
time: 155 us
  Pallas kernels  54.2 us (35%)
  waiting for transfers between devices  31.5 us (20%)
  blocking collectives  31.1 us (20%)
  starting transfers between devices  30.7 us (20%)
  local copies, waits for them, and re-layouts  2.86 us (2%)
  other arithmetic  1.87 us (1%)
  matrix products  1.8 us (1%)
    pallas_call x1, Pallas kernels, ritz(): pl.pallas_call(functools.partial(ritz_kernel, scale), out_shape=(square,...  51.6 us
    all_to_all x1, blocking collectives, per_device(): lax.all_to_all(jnp.concatenate([outgoing, terms], axis=2), 'sub', split_a...  31.1 us
    all_to_all x1, waiting for transfers between devices, per_device(): lax.all_to_all(sent.reshape(n_sub, cap_half, width), 'sub', split_axis=0,...  19 us
    all_to_all x1, starting transfers between devices, per_device(): lax.all_to_all(sent.reshape(n_sub, cap_half, width), 'sub', split_axis=0,...  16.5 us
    all_to_all x1, waiting for transfers between devices, per_device(): lax.all_to_all(jnp.broadcast_to(total[None], (n_sub, 4, lanes)), 'sub', s...  10.5 us
    all_to_all x1, starting transfers between devices, per_device(): lax.all_to_all(jnp.broadcast_to(total[None], (n_sub, 4, lanes)), 'sub', s...  6.35 us
  transfers between devices with their start and end apart: 6, of which 4 were waited for; matrix products, arithmetic and copies ran while one was open for 1% of the time, Pallas kernels for 0%

profile of v6, /device:TPU:1, one launch (start us, length us, event | category | flops | bytes accessed | tf_op | source)
XLA Modules:
  0.0 155.0 jit_solution(16144075691638600642)
XLA Ops:
  0.7 0.7 constant_dynamic-slice_fusion
  1.6 1.3 fusion.4
  2.9 16.5 %all-to-all-start = ((bf16[128,8,256]{2,1,0:T(8,128)(2,1)}), bf16[128,8,256]{2,1,0:T(8,128)(2,1)S(1)}, u32[]{:S(2)}, u32[]{:S(2)}) async-start(bf16[128,8,256]{2,1,0:T(8,128)(2,1)} %fusion.4), calls=%async_computation | async-start | bytes 1048576 | tf_op jit(solution)/shard_map/all_to_all | solution.py:257
  19.5 19.0 %all-to-all-done = bf16[128,8,256]{2,1,0:T(8,128)(2,1)S(1)} async-done(((bf16[128,8,256]{2,1,0:T(8,128)(2,1)}), bf16[128,8,256]{2,1,0:T(8,128)(2,1)S(1)}, u32[]{:S(2)}, u32[]{:S(2)}) %all-to-all-start) | async-done | bytes 524320 | tf_op jit(solution)/shard_map/all_to_all | solution.py:257
  38.7 0.4 fusion.9
  39.0 0.2 bitcast_select_fusion.mine_ref
  39.2 2.6 %collective-permute-start = (bf16[2,512,256]{2,1,0:T(8,128)(2,1)S(1)}, bf16[2,512,256]{2,1,0:T(8,128)(2,1)S(1)}, u32[]{:S(2)}, u32[]{:S(2)}) collective-permute-start(bf16[2,512,256]{2,1,0:T(8,128)(2,1)S(1)} %bitcast_select_fusion.mine_ref), channel_id=1, source_target_pairs={{0,1},{1,0},{2,3},{3,2},{4,5},{5,4},{6,7},{7,6},{8,9},{9,8},{10,11... | collective-permute-start | bytes 1572872 | tf_op jit(solution)/shard_map/ppermute | solution.py:265
  41.8 0.7 own_half.1
  42.5 0.8 collective-permute-done.other_ref
  43.3 1.9 %far_half.1 = (bf16[2,512,256]{2,1,0:T(8,128)(2,1)S(1)}, f32[2,128,256]{2,1,0:T(8,128)S(1)}, f32[2,128,256]{2,1,0:T(8,128)S(1)}) custom-call(s32[2]{0:T(128)S(1)} %copy-done.3, f32[2,2,512,256]{3,2,1,0:T(8,128)S(1)} %get-tuple-element.7.partial_ref, bf16[2,256,512]{2,1,0:T(8,128)(2,1)S(1)} %get-tuple-element.8.turned_ref, ...), custom_call_target="tpu_custom_call" | custom-call | flops 810000000 | bytes 4194304 | tf_op jit(solution)/shard_map/far_half/pallas_call | solution.py:104
  45.3 0.5 collective-permute-start.1
  45.7 0.3 copy.22
  46.0 0.9 fusion.8
  47.4 31.1 %all_to_all.15 = bf16[128,8,384]{2,1,0:T(8,128)(2,1)S(1)} all-to-all(bf16[128,8,384]{2,1,0:T(8,128)(2,1)S(1)} %pad_maximum_fusion), channel_id=1, replica_groups=mesh['sub'=128,'blk'=2] {'sub'}, dimensions={0} | all-to-all | bytes 1572864 | tf_op jit(solution)/shard_map/all_to_all | solution.py:271
  78.7 0.7 broadcast_in_dim.23
  79.4 6.4 %all-to-all-start.2 = ((f32[128,4,128]{2,1,0:T(4,128)}), f32[128,4,128]{2,1,0:T(4,128)S(1)}, u32[]{:S(2)}, u32[]{:S(2)}) async-start(f32[128,4,128]{2,1,0:T(4,128)} %broadcast_in_dim.23), calls=%async_computation.2 | async-start | bytes 524288 | tf_op jit(solution)/shard_map/all_to_all | solution.py:280
  85.8 0.5 fusion.1
  86.3 1.8 %collective-permute-start.3 = (f32[256,256]{1,0:T(8,128)S(1)}, f32[256,256]{1,0:T(8,128)S(1)}, u32[]{:S(2)}, u32[]{:S(2)}) collective-permute-start(f32[256,256]{1,0:T(8,128)S(1)} %get-tuple-element.12), channel_id=1, source_target_pairs={{0,1},{1,0},{2,3},{3,2},{4,5},{5,4},{6,7},{7,6},{8,9},{9,8},{10,11... | collective-permute-start | bytes 786440 | tf_op jit(solution)/shard_map/ppermute | solution.py:296
  88.1 10.5 %all-to-all-done.2 = f32[128,4,128]{2,1,0:T(4,128)S(1)} async-done(((f32[128,4,128]{2,1,0:T(4,128)}), f32[128,4,128]{2,1,0:T(4,128)S(1)}, u32[]{:S(2)}, u32[]{:S(2)}) %all-to-all-start.2) | async-done | bytes 262176 | tf_op jit(solution)/shard_map/all_to_all | solution.py:280
  98.6 0.2 copy.19
  98.8 0.2 reshape.89.mine_ref
  99.0 3.1 %collective-permute-start.2 = (f32[2,128,256]{2,1,0:T(8,128)S(1)}, f32[2,128,256]{2,1,0:T(8,128)S(1)}, u32[]{:S(2)}, u32[]{:S(2)}) collective-permute-start(f32[2,128,256]{2,1,0:T(8,128)S(1)} %reshape.89.mine_ref), channel_id=1, source_target_pairs={{0,1},{1,0},{2,3},{3,2},{4,5},{5,4},{6,7},{7,6},{8,9},{9,8},{10,11... | collective-permute-start | bytes 786440 | tf_op jit(solution)/shard_map/ppermute | solution.py:288
  102.2 1.2 collective-permute-done.2.other_ref
  103.3 51.6 %ritz.1 = (f32[256,256]{1,0:T(8,128)}, f32[256,256]{1,0:T(8,128)}) custom-call(f32[2,128,256]{2,1,0:T(8,128)S(1)} %reshape.89.mine_ref, f32[2,128,256]{2,1,0:T(8,128)S(1)} %collective-permute-done.2.other_ref, f32[256,256]{1,0:T(8,128)S(1)} %get-tuple-element.13.image_ref, f32[256,256]{1,0:T(8,128)S(1)} %collective-permute-done.3.extra_ref), custom_call_target="tpu_custom_call" | custom-call | tf_op jit(solution)/shard_map/ritz/pallas_call | solution.py:215
  (26 shorter events, 1.1 us)
Async XLA Ops:
  0.6 1.0 copy-start
  0.6 18.8 %copy-start.3 = (s32[2]{0:T(128)S(1)}, s32[2]{0:T(128)}, u32[]{:S(2)}) copy-start(s32[2]{0:T(128)} %counts_ref.1) | copy-start | bytes 28
  2.9 38.9 %copy-start.1 = (bf16[2,512,1024]{2,1,0:T(8,128)(2,1)S(1)}, bf16[2,512,1024]{2,1,0:T(8,128)(2,1)}, u32[]{:S(2)}) copy-start(bf16[2,512,1024]{2,1,0:T(8,128)(2,1)} %stiff_ref.3) | copy-start | bytes 6291460
  2.9 35.6 %all-to-all-start = ((bf16[128,8,256]{2,1,0:T(8,128)(2,1)}), bf16[128,8,256]{2,1,0:T(8,128)(2,1)S(1)}, u32[]{:S(2)}, u32[]{:S(2)}) async-start(bf16[128,8,256]{2,1,0:T(8,128)(2,1)} %fusion.4), calls=%async_computation | async-start | bytes 1048576 | tf_op jit(solution)/shard_map/all_to_all | solution.py:257
  38.5 3.3 %copy-start.2 = (bf16[2,512,1024]{2,1,0:T(8,128)(2,1)S(1)}, bf16[2,512,1024]{2,1,0:T(8,128)(2,1)}, u32[]{:S(2)}) copy-start(bf16[2,512,1024]{2,1,0:T(8,128)(2,1)} %mass_ref.3) | copy-start | bytes 6291460
  39.2 4.1 %collective-permute-start = (bf16[2,512,256]{2,1,0:T(8,128)(2,1)S(1)}, bf16[2,512,256]{2,1,0:T(8,128)(2,1)S(1)}, u32[]{:S(2)}, u32[]{:S(2)}) collective-permute-start(bf16[2,512,256]{2,1,0:T(8,128)(2,1)S(1)} %bitcast_select_fusion.mine_ref), channel_id=1, source_target_pairs={{0,1},{1,0},{2,3},{3,2},{4,5},{5,4},{6,7},{7,6},{8,9},{9,8},{10,11... | collective-permute-start | bytes 1572872 | tf_op jit(solution)/shard_map/ppermute | solution.py:265
  45.3 1.7 %collective-permute-start.1 = (f32[2,128,256]{2,1,0:T(8,128)S(1)}, f32[2,128,256]{2,1,0:T(8,128)S(1)}, u32[]{:S(2)}, u32[]{:S(2)}) collective-permute-start(f32[2,128,256]{2,1,0:T(8,128)S(1)} %get-tuple-element.11), channel_id=1, source_target_pairs={{0,1},{1,0},{2,3},{3,2},{4,5},{5,4},{6,7},{7,6},{8,9},{9,8},{10,11... | collective-permute-start | bytes 786440 | tf_op jit(solution)/shard_map/ppermute | solution.py:267
  79.4 19.2 %all-to-all-start.2 = ((f32[128,4,128]{2,1,0:T(4,128)}), f32[128,4,128]{2,1,0:T(4,128)S(1)}, u32[]{:S(2)}, u32[]{:S(2)}) async-start(f32[128,4,128]{2,1,0:T(4,128)} %broadcast_in_dim.23), calls=%async_computation.2 | async-start | bytes 524288 | tf_op jit(solution)/shard_map/all_to_all | solution.py:280
  86.3 15.8 %collective-permute-start.3 = (f32[256,256]{1,0:T(8,128)S(1)}, f32[256,256]{1,0:T(8,128)S(1)}, u32[]{:S(2)}, u32[]{:S(2)}) collective-permute-start(f32[256,256]{1,0:T(8,128)S(1)} %get-tuple-element.12), channel_id=1, source_target_pairs={{0,1},{1,0},{2,3},{3,2},{4,5},{5,4},{6,7},{7,6},{8,9},{9,8},{10,11... | collective-permute-start | bytes 786440 | tf_op jit(solution)/shard_map/ppermute | solution.py:296
  99.0 4.3 %collective-permute-start.2 = (f32[2,128,256]{2,1,0:T(8,128)S(1)}, f32[2,128,256]{2,1,0:T(8,128)S(1)}, u32[]{:S(2)}, u32[]{:S(2)}) collective-permute-start(f32[2,128,256]{2,1,0:T(8,128)S(1)} %reshape.89.mine_ref), channel_id=1, source_target_pairs={{0,1},{1,0},{2,3},{3,2},{4,5},{5,4},{6,7},{7,6},{8,9},{9,8},{10,11... | collective-permute-start | bytes 786440 | tf_op jit(solution)/shard_map/ppermute | solution.py:288

commit v7 on v6

--- a/solution.py
+++ b/solution.py
@@ -49,36 +49,47 @@
     return me_blk, own, far
 
 
-def own_kernel(mine_ref, stiff_ref, mass_ref, partial_ref, turned_ref):
+def own_kernel(mine_ref, matrix_ref, partial_ref, turned_ref=None):
     sub_dev, half, _ = mine_ref.shape
     _, own, _ = halves(half)
     for s in range(sub_dev):
-        turned_ref[s] = mine_ref[s].T
-    for place, matrix_ref in enumerate((mass_ref, stiff_ref)):
-        for s in range(sub_dev):
-            partial_ref[place, s] = jnp.dot(
-                matrix_ref[s, :, own], mine_ref[s], preferred_element_type=jnp.float32
-            )
+        partial_ref[s] = jnp.dot(
+            matrix_ref[s, :, own], mine_ref[s], preferred_element_type=jnp.float32
+        )
+        if turned_ref is not None:
+            turned_ref[:, s * half : (s + 1) * half] = mine_ref[s].T
 
 
 def far_kernel(
-    counts_ref, partial_ref, turned_ref, other_ref, stiff_ref, mass_ref, part_ref, keep_ref, send_ref
+    counts_ref,
+    stiff_own_ref,
+    mass_own_ref,
+    turned_ref,
+    other_ref,
+    stiff_ref,
+    mass_ref,
+    part_ref,
+    keep_ref,
+    send_ref,
+    mass_part_ref,
 ):
     sub_dev, half, width = other_ref.shape
     me_blk, _, far = halves(half)
     first = me_blk == 0
-    slot = me_blk * half + lax.broadcasted_iota(jnp.int32, (half, width), 0)
-    for place, matrix_ref in enumerate((mass_ref, stiff_ref)):
-        gram = None
-        for s in range(sub_dev):
-            part = partial_ref[place, s] + jnp.dot(
-                matrix_ref[s, :, far], other_ref[s], preferred_element_type=jnp.float32
-            )
-            part = jnp.where(slot < counts_ref[s], part, 0.0).astype(jnp.bfloat16)
-            if place == 1:
-                part_ref[s] = part
-            term = jnp.dot(turned_ref[s], part, preferred_element_type=jnp.float32)
-            gram = term if gram is None else gram + term
+    slot = me_blk * half + lax.broadcasted_iota(jnp.int32, (half, 1), 0)
+    for s in range(sub_dev):
+        part = mass_own_ref[s] + jnp.dot(
+            mass_ref[s, :, far], other_ref[s], preferred_element_type=jnp.float32
+        )
+        mass_part_ref[s] = jnp.where(slot < counts_ref[s], part, 0.0).astype(jnp.bfloat16)
+    for s in range(sub_dev):
+        part = stiff_own_ref[s] + jnp.dot(
+            stiff_ref[s, :, far], other_ref[s], preferred_element_type=jnp.float32
+        )
+        part_ref[s] = jnp.where(slot < counts_ref[s], part, 0.0).astype(jnp.bfloat16)
+    for place, parts_ref in enumerate((mass_part_ref, part_ref)):
+        parts = parts_ref[...].reshape(sub_dev * half, width)
+        gram = jnp.dot(turned_ref[...], parts, preferred_element_type=jnp.float32)
         low, high = gram[: width // 2], gram[width // 2 :]
         keep_ref[place] = jnp.where(first, low, high)
         send_ref[place] = jnp.where(first, high, low)
@@ -88,28 +99,37 @@
     sub_dev, half, width = mine.shape
     vmem = pl.BlockSpec(memory_space=pltpu.VMEM)
     params = pltpu.CompilerParams(vmem_limit_bytes=20 << 20)
-    partial, turned = pl.pallas_call(
+    partial = jax.ShapeDtypeStruct((sub_dev, half, width), jnp.float32)
+    cost = pl.CostEstimate(flops=270000000, bytes_accessed=2 << 20, transcendentals=0)
+    stiff_own, turned = pl.pallas_call(
         own_kernel,
-        out_shape=(
-            jax.ShapeDtypeStruct((2, sub_dev, half, width), jnp.float32),
-            jax.ShapeDtypeStruct((sub_dev, width, half), jnp.bfloat16),
-        ),
-        in_specs=[vmem] * 3,
+        out_shape=(partial, jax.ShapeDtypeStruct((width, sub_dev * half), jnp.bfloat16)),
+        in_specs=[vmem] * 2,
         out_specs=(vmem, vmem),
         compiler_params=params,
-        cost_estimate=pl.CostEstimate(flops=540000000, bytes_accessed=4 << 20, transcendentals=0),
-        name="own_half",
-    )(mine, stiffness, mass)
+        cost_estimate=cost,
+        name="own_stiff",
+    )(mine, stiffness)
+    mass_own = pl.pallas_call(
+        own_kernel,
+        out_shape=partial,
+        in_specs=[vmem] * 2,
+        out_specs=vmem,
+        compiler_params=params,
+        cost_estimate=cost,
+        name="own_mass",
+    )(mine, mass)
     gram = jax.ShapeDtypeStruct((2, width // 2, width), jnp.float32)
     return pl.pallas_call(
         far_kernel,
         out_shape=(jax.ShapeDtypeStruct(mine.shape, jnp.bfloat16), gram, gram),
-        in_specs=[pl.BlockSpec(memory_space=pltpu.SMEM)] + [vmem] * 5,
+        in_specs=[pl.BlockSpec(memory_space=pltpu.SMEM)] + [vmem] * 6,
         out_specs=(vmem, vmem, vmem),
+        scratch_shapes=[pltpu.VMEM((sub_dev, half, width), jnp.bfloat16)],
         compiler_params=params,
         cost_estimate=pl.CostEstimate(flops=810000000, bytes_accessed=4 << 20, transcendentals=0),
         name="far_half",
-    )(counts, partial, turned, other, stiffness, mass)
+    )(counts, stiff_own, mass_own, turned, other, stiffness, mass)
 
 
 def eliminate(work_ref, inverse_ref):
@@ -186,7 +206,7 @@
         left = rest + off + long(off, rest, 0)
         error = left + off.T + long(left, off, 1)
         change = weight * error
-        inverse_ref[...] = off - change - long(change, off, 0)
+        inverse_ref[...] = off - change - short(change, off, 0)
         return step + 1, jnp.sum(error * error)
 
     _, size = lax.while_loop(going, correct, (jnp.int32(0), jnp.float32(1.0)))

time: 155 us -> 155 us (level)
  transfers between devices with their start and end apart: 6 -> 6, of which waited for: 4 -> 4; matrix products, arithmetic and copies ran while one was open for 1% -> 1% of each run, Pallas kernels for 0% -> 1%
where the time goes in v7:
time: 155 us; the launch traced here: 154 us
  Pallas kernels  53.6 us (35%)
  waiting for transfers between devices  31.3 us (20%)
  blocking collectives  31.1 us (20%)
  starting transfers between devices  30.8 us (20%)
  local copies, waits for them, and re-layouts  2.86 us (2%)
  other arithmetic  1.87 us (1%)
  matrix products  1.81 us (1%)
    pallas_call x1, Pallas kernels, ritz(): pl.pallas_call(functools.partial(ritz_kernel, scale), out_shape=(square,...  51.1 us
    all_to_all x1, blocking collectives, per_device(): lax.all_to_all(jnp.concatenate([outgoing, terms], axis=2), 'sub', split_a...  31.1 us
    all_to_all x1, waiting for transfers between devices, per_device(): lax.all_to_all(sent.reshape(n_sub, cap_half, width), 'sub', split_axis=0,...  19 us
    all_to_all x1, starting transfers between devices, per_device(): lax.all_to_all(sent.reshape(n_sub, cap_half, width), 'sub', split_axis=0,...  16.5 us
    all_to_all x1, waiting for transfers between devices, per_device(): lax.all_to_all(jnp.broadcast_to(total[None], (n_sub, 4, lanes)), 'sub', s...  10.5 us
    all_to_all x1, starting transfers between devices, per_device(): lax.all_to_all(jnp.broadcast_to(total[None], (n_sub, 4, lanes)), 'sub', s...  6.35 us
  transfers between devices with their start and end apart: 6, of which 4 were waited for; matrix products, arithmetic and copies ran while one was open for 1% of the time, Pallas kernels for 1%

profile of v7, /device:TPU:1, one launch (start us, length us, event | category | flops | bytes accessed | tf_op | source)
XLA Modules:
  0.0 154.3 jit_solution(15757272092830297151)
XLA Ops:
  0.7 0.7 constant_dynamic-slice_fusion
  1.6 1.3 fusion.4
  2.9 16.5 %all-to-all-start = ((bf16[128,8,256]{2,1,0:T(8,128)(2,1)}), bf16[128,8,256]{2,1,0:T(8,128)(2,1)S(1)}, u32[]{:S(2)}, u32[]{:S(2)}) async-start(bf16[128,8,256]{2,1,0:T(8,128)(2,1)} %fusion.4), calls=%async_computation | async-start | bytes 1048576 | tf_op jit(solution)/shard_map/all_to_all | solution.py:277
  19.5 19.0 %all-to-all-done = bf16[128,8,256]{2,1,0:T(8,128)(2,1)S(1)} async-done(((bf16[128,8,256]{2,1,0:T(8,128)(2,1)}), bf16[128,8,256]{2,1,0:T(8,128)(2,1)S(1)}, u32[]{:S(2)}, u32[]{:S(2)}) %all-to-all-start) | async-done | bytes 524320 | tf_op jit(solution)/shard_map/all_to_all | solution.py:277
  38.7 0.4 fusion.9
  39.2 2.6 %collective-permute-start = (bf16[2,512,256]{2,1,0:T(8,128)(2,1)S(1)}, bf16[2,512,256]{2,1,0:T(8,128)(2,1)S(1)}, u32[]{:S(2)}, u32[]{:S(2)}) collective-permute-start(bf16[2,512,256]{2,1,0:T(8,128)(2,1)S(1)} %bitcast_select_fusion.mine_ref), channel_id=1, source_target_pairs={{0,1},{1,0},{2,3},{3,2},{4,5},{5,4},{6,7},{7,6},{8,9},{9,8},{10,11... | collective-permute-start | bytes 1572872 | tf_op jit(solution)/shard_map/ppermute | solution.py:285
  41.8 0.5 own_stiff.1
  42.3 0.5 own_mass.1.mass_own_ref
  42.7 0.6 collective-permute-done.other_ref
  43.4 1.6 %far_half.1 = (bf16[2,512,256]{2,1,0:T(8,128)(2,1)S(1)}, f32[2,128,256]{2,1,0:T(8,128)S(1)}, f32[2,128,256]{2,1,0:T(8,128)S(1)}) custom-call(s32[2]{0:T(128)S(1)} %copy-done.3, f32[2,512,256]{2,1,0:T(8,128)S(1)} %get-tuple-element.7.stiff_own_ref, f32[2,512,256]{2,1,0:T(8,128)S(1)} %own_mass.1.mass_own_ref, ...), custom_call_target="tpu_custom_call" | custom-call | flops 810000000 | bytes 4194304 | tf_op jit(solution)/shard_map/far_half/pallas_call | solution.py:123
  45.0 0.5 collective-permute-start.1
  45.5 0.3 copy.22
  45.8 0.9 fusion.8
  47.2 31.1 %all_to_all.15 = bf16[128,8,384]{2,1,0:T(8,128)(2,1)S(1)} all-to-all(bf16[128,8,384]{2,1,0:T(8,128)(2,1)S(1)} %pad_maximum_fusion), channel_id=1, replica_groups=mesh['sub'=128,'blk'=2] {'sub'}, dimensions={0} | all-to-all | bytes 1572864 | tf_op jit(solution)/shard_map/all_to_all | solution.py:291
  78.4 0.7 broadcast_in_dim.23
  79.1 6.4 %all-to-all-start.2 = ((f32[128,4,128]{2,1,0:T(4,128)}), f32[128,4,128]{2,1,0:T(4,128)S(1)}, u32[]{:S(2)}, u32[]{:S(2)}) async-start(f32[128,4,128]{2,1,0:T(4,128)} %broadcast_in_dim.23), calls=%async_computation.2 | async-start | bytes 524288 | tf_op jit(solution)/shard_map/all_to_all | solution.py:300
  85.5 0.5 fusion.1
  86.1 1.8 %collective-permute-start.3 = (f32[256,256]{1,0:T(8,128)S(1)}, f32[256,256]{1,0:T(8,128)S(1)}, u32[]{:S(2)}, u32[]{:S(2)}) collective-permute-start(f32[256,256]{1,0:T(8,128)S(1)} %get-tuple-element.12), channel_id=1, source_target_pairs={{0,1},{1,0},{2,3},{3,2},{4,5},{5,4},{6,7},{7,6},{8,9},{9,8},{10,11... | collective-permute-start | bytes 786440 | tf_op jit(solution)/shard_map/ppermute | solution.py:316
  87.9 10.5 %all-to-all-done.2 = f32[128,4,128]{2,1,0:T(4,128)S(1)} async-done(((f32[128,4,128]{2,1,0:T(4,128)}), f32[128,4,128]{2,1,0:T(4,128)S(1)}, u32[]{:S(2)}, u32[]{:S(2)}) %all-to-all-start.2) | async-done | bytes 262176 | tf_op jit(solution)/shard_map/all_to_all | solution.py:300
  98.4 0.2 copy.19
  98.6 0.2 reshape.89.mine_ref
  98.8 3.1 %collective-permute-start.2 = (f32[2,128,256]{2,1,0:T(8,128)S(1)}, f32[2,128,256]{2,1,0:T(8,128)S(1)}, u32[]{:S(2)}, u32[]{:S(2)}) collective-permute-start(f32[2,128,256]{2,1,0:T(8,128)S(1)} %reshape.89.mine_ref), channel_id=1, source_target_pairs={{0,1},{1,0},{2,3},{3,2},{4,5},{5,4},{6,7},{7,6},{8,9},{9,8},{10,11... | collective-permute-start | bytes 786440 | tf_op jit(solution)/shard_map/ppermute | solution.py:308
  101.9 1.2 collective-permute-done.2.other_ref
  103.0 51.1 %ritz.1 = (f32[256,256]{1,0:T(8,128)}, f32[256,256]{1,0:T(8,128)}) custom-call(f32[2,128,256]{2,1,0:T(8,128)S(1)} %reshape.89.mine_ref, f32[2,128,256]{2,1,0:T(8,128)S(1)} %collective-permute-done.2.other_ref, f32[256,256]{1,0:T(8,128)S(1)} %get-tuple-element.13.image_ref, f32[256,256]{1,0:T(8,128)S(1)} %collective-permute-done.3.extra_ref), custom_call_target="tpu_custom_call" | custom-call | tf_op jit(solution)/shard_map/ritz/pallas_call | solution.py:235
  (27 shorter events, 1.3 us)
Async XLA Ops:
  0.6 1.0 copy-start
  0.6 18.8 %copy-start.3 = (s32[2]{0:T(128)S(1)}, s32[2]{0:T(128)}, u32[]{:S(2)}) copy-start(s32[2]{0:T(128)} %counts_ref.1) | copy-start | bytes 28
  2.9 38.9 %copy-start.1 = (bf16[2,512,1024]{2,1,0:T(8,128)(2,1)S(1)}, bf16[2,512,1024]{2,1,0:T(8,128)(2,1)}, u32[]{:S(2)}) copy-start(bf16[2,512,1024]{2,1,0:T(8,128)(2,1)} %stiff_ref.1) | copy-start | bytes 6291460
  2.9 35.6 %all-to-all-start = ((bf16[128,8,256]{2,1,0:T(8,128)(2,1)}), bf16[128,8,256]{2,1,0:T(8,128)(2,1)S(1)}, u32[]{:S(2)}, u32[]{:S(2)}) async-start(bf16[128,8,256]{2,1,0:T(8,128)(2,1)} %fusion.4), calls=%async_computation | async-start | bytes 1048576 | tf_op jit(solution)/shard_map/all_to_all | solution.py:277
  39.0 3.3 %copy-start.2 = (bf16[2,512,1024]{2,1,0:T(8,128)(2,1)S(1)}, bf16[2,512,1024]{2,1,0:T(8,128)(2,1)}, u32[]{:S(2)}) copy-start(bf16[2,512,1024]{2,1,0:T(8,128)(2,1)} %mass_ref.1) | copy-start | bytes 6291460
  39.2 4.1 %collective-permute-start = (bf16[2,512,256]{2,1,0:T(8,128)(2,1)S(1)}, bf16[2,512,256]{2,1,0:T(8,128)(2,1)S(1)}, u32[]{:S(2)}, u32[]{:S(2)}) collective-permute-start(bf16[2,512,256]{2,1,0:T(8,128)(2,1)S(1)} %bitcast_select_fusion.mine_ref), channel_id=1, source_target_pairs={{0,1},{1,0},{2,3},{3,2},{4,5},{5,4},{6,7},{7,6},{8,9},{9,8},{10,11... | collective-permute-start | bytes 1572872 | tf_op jit(solution)/shard_map/ppermute | solution.py:285
  45.0 1.7 %collective-permute-start.1 = (f32[2,128,256]{2,1,0:T(8,128)S(1)}, f32[2,128,256]{2,1,0:T(8,128)S(1)}, u32[]{:S(2)}, u32[]{:S(2)}) collective-permute-start(f32[2,128,256]{2,1,0:T(8,128)S(1)} %get-tuple-element.11), channel_id=1, source_target_pairs={{0,1},{1,0},{2,3},{3,2},{4,5},{5,4},{6,7},{7,6},{8,9},{9,8},{10,11... | collective-permute-start | bytes 786440 | tf_op jit(solution)/shard_map/ppermute | solution.py:287
  79.1 19.2 %all-to-all-start.2 = ((f32[128,4,128]{2,1,0:T(4,128)}), f32[128,4,128]{2,1,0:T(4,128)S(1)}, u32[]{:S(2)}, u32[]{:S(2)}) async-start(f32[128,4,128]{2,1,0:T(4,128)} %broadcast_in_dim.23), calls=%async_computation.2 | async-start | bytes 524288 | tf_op jit(solution)/shard_map/all_to_all | solution.py:300
  86.1 15.8 %collective-permute-start.3 = (f32[256,256]{1,0:T(8,128)S(1)}, f32[256,256]{1,0:T(8,128)S(1)}, u32[]{:S(2)}, u32[]{:S(2)}) collective-permute-start(f32[256,256]{1,0:T(8,128)S(1)} %get-tuple-element.12), channel_id=1, source_target_pairs={{0,1},{1,0},{2,3},{3,2},{4,5},{5,4},{6,7},{7,6},{8,9},{9,8},{10,11... | collective-permute-start | bytes 786440 | tf_op jit(solution)/shard_map/ppermute | solution.py:316
  98.8 4.3 %collective-permute-start.2 = (f32[2,128,256]{2,1,0:T(8,128)S(1)}, f32[2,128,256]{2,1,0:T(8,128)S(1)}, u32[]{:S(2)}, u32[]{:S(2)}) collective-permute-start(f32[2,128,256]{2,1,0:T(8,128)S(1)} %reshape.89.mine_ref), channel_id=1, source_target_pairs={{0,1},{1,0},{2,3},{3,2},{4,5},{5,4},{6,7},{7,6},{8,9},{9,8},{10,11... | collective-permute-start | bytes 786440 | tf_op jit(solution)/shard_map/ppermute | solution.py:308

commit v8 on v7

--- a/solution.py
+++ b/solution.py
@@ -274,13 +274,15 @@
     picks = select_rows(table.reshape(-1), rows_dev)
 
     sent = jnp.dot(picks, basis, preferred_element_type=jnp.float32).astype(jnp.bfloat16)
+    sent, me_sub, me_blk = lax.optimization_barrier((sent, me_sub, me_blk))
     received = lax.all_to_all(
         sent.reshape(n_sub, cap_half, width), "sub", split_axis=0, concat_axis=0, tiled=True
     )
+    received, counts, me_sub, me_blk = lax.optimization_barrier((received, counts, me_sub, me_blk))
     received = with_layout_constraint(received.transpose(1, 0, 2), Layout((0, 1, 2)))
     mine = jnp.roll(received, -me_sub, axis=1).reshape(sub_dev, half, width)
-    slots = me_blk * half + jnp.arange(half, dtype=jnp.int32)
-    my_live = (slots[None, :] < counts[:, None])[:, :, None]
+    slots = jnp.arange(half, dtype=jnp.int32)
+    my_live = (slots[None, :] < (counts - me_blk * half)[:, None])[:, :, None]
     mine = jnp.where(my_live, mine, jnp.zeros((), jnp.bfloat16))
     other = lax.ppermute(mine, "blk", SWAP)
     stiff_part, keep, send = products(counts, mine, other, stiffness, mass)

time: 155 us -> 154 us (level)
  blocking collectives: 31.1 us -> 66.5 us
  waiting for transfers between devices: 31.3 us -> 12.2 us
  starting transfers between devices: 30.8 us -> 14.3 us
    all_to_all x0 -> x1, blocking collectives: none -> 35.4 us  [per_device(): lax.all_to_all(sent.reshape(n_sub, cap_half, width), 'sub', split_axis=0,...]
    all_to_all x1 -> x0, waiting for transfers between devices: 19 us -> none  [per_device(): lax.all_to_all(sent.reshape(n_sub, cap_half, width), 'sub', split_axis=0,...]
    all_to_all x1 -> x0, starting transfers between devices: 16.5 us -> none  [per_device(): lax.all_to_all(sent.reshape(n_sub, cap_half, width), 'sub', split_axis=0,...]
  transfers between devices with their start and end apart: 6 -> 5, of which waited for: 4 -> 3; matrix products, arithmetic and copies ran while one was open for 1% -> 1% of each run, Pallas kernels for 1% -> 1%
where the time goes in v8:
time: 154 us; the launch traced here: 153 us
  blocking collectives  66.5 us (43%)
  Pallas kernels  53.6 us (35%)
  starting transfers between devices  14.3 us (9%)
  waiting for transfers between devices  12.2 us (8%)
  local copies, waits for them, and re-layouts  2.86 us (2%)
  other arithmetic  1.87 us (1%)
    pallas_call x1, Pallas kernels, ritz(): pl.pallas_call(functools.partial(ritz_kernel, scale), out_shape=(square,...  51.1 us
    all_to_all x1, blocking collectives, per_device(): lax.all_to_all(sent.reshape(n_sub, cap_half, width), 'sub', split_axis=0,...  35.4 us
    all_to_all x1, blocking collectives, per_device(): lax.all_to_all(jnp.concatenate([outgoing, terms], axis=2), 'sub', split_a...  31.1 us
    all_to_all x1, waiting for transfers between devices, per_device(): lax.all_to_all(jnp.broadcast_to(total[None], (n_sub, 4, lanes)), 'sub', s...  10.5 us
    all_to_all x1, starting transfers between devices, per_device(): lax.all_to_all(jnp.broadcast_to(total[None], (n_sub, 4, lanes)), 'sub', s...  6.36 us
    ppermute x1, starting transfers between devices, per_device(): other_grams = lax.ppermute(mine_grams, 'blk', SWAP)  3.1 us
  transfers between devices with their start and end apart: 5, of which 3 were waited for; matrix products, arithmetic and copies ran while one was open for 1% of the time, Pallas kernels for 1%

profile of v8, /device:TPU:1, one launch (start us, length us, event | category | flops | bytes accessed | tf_op | source)
XLA Modules:
  0.0 153.4 jit_solution(15781077648253152370)
XLA Ops:
  0.7 0.7 constant_dynamic-slice_fusion
  1.6 0.5 fusion.3
  2.1 35.4 %all_to_all.15 = bf16[128,8,256]{2,1,0:T(8,128)(2,1)S(1)} all-to-all(bf16[128,8,256]{2,1,0:T(8,128)(2,1)S(1)} %bitcast.33), channel_id=1, replica_groups=mesh['sub'=128,'blk'=2] {'sub'}, dimensions={0} | all-to-all | bytes 1048576 | tf_op jit(solution)/shard_map/all_to_all | solution.py:278
  37.8 0.4 fusion.8
  38.1 0.2 bitcast_select_fusion.mine_ref
  38.3 2.6 %collective-permute-start = (bf16[2,512,256]{2,1,0:T(8,128)(2,1)S(1)}, bf16[2,512,256]{2,1,0:T(8,128)(2,1)S(1)}, u32[]{:S(2)}, u32[]{:S(2)}) collective-permute-start(bf16[2,512,256]{2,1,0:T(8,128)(2,1)S(1)} %bitcast_select_fusion.mine_ref), channel_id=1, source_target_pairs={{0,1},{1,0},{2,3},{3,2},{4,5},{5,4},{6,7},{7,6},{8,9},{9,8},{10,11... | collective-permute-start | bytes 1572872 | tf_op jit(solution)/shard_map/ppermute | solution.py:287
  40.9 0.5 own_stiff.1
  41.4 0.5 own_mass.1.mass_own_ref
  41.8 0.6 collective-permute-done.other_ref
  42.4 1.6 %far_half.1 = (bf16[2,512,256]{2,1,0:T(8,128)(2,1)S(1)}, f32[2,128,256]{2,1,0:T(8,128)S(1)}, f32[2,128,256]{2,1,0:T(8,128)S(1)}) custom-call(s32[2]{0:T(128)S(1)} %copy-done.3, f32[2,512,256]{2,1,0:T(8,128)S(1)} %get-tuple-element.21.stiff_own_ref, f32[2,512,256]{2,1,0:T(8,128)S(1)} %own_mass.1.mass_own_ref, ...), custom_call_target="tpu_custom_call" | custom-call | flops 810000000 | bytes 4194304 | tf_op jit(solution)/shard_map/far_half/pallas_call | solution.py:123
  44.1 0.5 collective-permute-start.1
  44.6 0.3 copy.22
  44.8 0.9 fusion.7
  46.3 31.1 %all_to_all.16 = bf16[128,8,384]{2,1,0:T(8,128)(2,1)S(1)} all-to-all(bf16[128,8,384]{2,1,0:T(8,128)(2,1)S(1)} %pad_maximum_fusion), channel_id=1, replica_groups=mesh['sub'=128,'blk'=2] {'sub'}, dimensions={0} | all-to-all | bytes 1572864 | tf_op jit(solution)/shard_map/all_to_all | solution.py:293
  77.5 0.7 broadcast_in_dim.23
  78.2 6.4 %all-to-all-start.2 = ((f32[128,4,128]{2,1,0:T(4,128)}), f32[128,4,128]{2,1,0:T(4,128)S(1)}, u32[]{:S(2)}, u32[]{:S(2)}) async-start(f32[128,4,128]{2,1,0:T(4,128)} %broadcast_in_dim.23), calls=%async_computation.2 | async-start | bytes 524288 | tf_op jit(solution)/shard_map/all_to_all | solution.py:302
  84.6 0.5 fusion.1
  85.2 1.8 %collective-permute-start.3 = (f32[256,256]{1,0:T(8,128)S(1)}, f32[256,256]{1,0:T(8,128)S(1)}, u32[]{:S(2)}, u32[]{:S(2)}) collective-permute-start(f32[256,256]{1,0:T(8,128)S(1)} %get-tuple-element.26), channel_id=1, source_target_pairs={{0,1},{1,0},{2,3},{3,2},{4,5},{5,4},{6,7},{7,6},{8,9},{9,8},{10,11... | collective-permute-start | bytes 786440 | tf_op jit(solution)/shard_map/ppermute | solution.py:318
  87.0 10.5 %all-to-all-done.2 = f32[128,4,128]{2,1,0:T(4,128)S(1)} async-done(((f32[128,4,128]{2,1,0:T(4,128)}), f32[128,4,128]{2,1,0:T(4,128)S(1)}, u32[]{:S(2)}, u32[]{:S(2)}) %all-to-all-start.2) | async-done | bytes 262176 | tf_op jit(solution)/shard_map/all_to_all | solution.py:302
  97.4 0.2 copy.19
  97.7 0.2 reshape.78.mine_ref
  97.9 3.1 %collective-permute-start.2 = (f32[2,128,256]{2,1,0:T(8,128)S(1)}, f32[2,128,256]{2,1,0:T(8,128)S(1)}, u32[]{:S(2)}, u32[]{:S(2)}) collective-permute-start(f32[2,128,256]{2,1,0:T(8,128)S(1)} %reshape.78.mine_ref), channel_id=1, source_target_pairs={{0,1},{1,0},{2,3},{3,2},{4,5},{5,4},{6,7},{7,6},{8,9},{9,8},{10,11... | collective-permute-start | bytes 786440 | tf_op jit(solution)/shard_map/ppermute | solution.py:310
  101.0 1.2 collective-permute-done.2.other_ref
  102.1 51.1 %ritz.1 = (f32[256,256]{1,0:T(8,128)}, f32[256,256]{1,0:T(8,128)}) custom-call(f32[2,128,256]{2,1,0:T(8,128)S(1)} %reshape.78.mine_ref, f32[2,128,256]{2,1,0:T(8,128)S(1)} %collective-permute-done.2.other_ref, f32[256,256]{1,0:T(8,128)S(1)} %get-tuple-element.27.image_ref, f32[256,256]{1,0:T(8,128)S(1)} %collective-permute-done.3.extra_ref), custom_call_target="tpu_custom_call" | custom-call | tf_op jit(solution)/shard_map/ritz/pallas_call | solution.py:235
  (26 shorter events, 1.1 us)
Async XLA Ops:
  0.6 1.0 copy-start
  0.6 37.0 %copy-start.3 = (s32[2]{0:T(128)S(1)}, s32[2]{0:T(128)}, u32[]{:S(2)}) copy-start(s32[2]{0:T(128)} %counts_ref) | copy-start | bytes 28
  2.1 38.8 %copy-start.1 = (bf16[2,512,1024]{2,1,0:T(8,128)(2,1)S(1)}, bf16[2,512,1024]{2,1,0:T(8,128)(2,1)}, u32[]{:S(2)}) copy-start(bf16[2,512,1024]{2,1,0:T(8,128)(2,1)} %stiff_ref.1) | copy-start | bytes 6291460
  38.1 3.3 %copy-start.2 = (bf16[2,512,1024]{2,1,0:T(8,128)(2,1)S(1)}, bf16[2,512,1024]{2,1,0:T(8,128)(2,1)}, u32[]{:S(2)}) copy-start(bf16[2,512,1024]{2,1,0:T(8,128)(2,1)} %mass_ref.1) | copy-start | bytes 6291460
  38.3 4.1 %collective-permute-start = (bf16[2,512,256]{2,1,0:T(8,128)(2,1)S(1)}, bf16[2,512,256]{2,1,0:T(8,128)(2,1)S(1)}, u32[]{:S(2)}, u32[]{:S(2)}) collective-permute-start(bf16[2,512,256]{2,1,0:T(8,128)(2,1)S(1)} %bitcast_select_fusion.mine_ref), channel_id=1, source_target_pairs={{0,1},{1,0},{2,3},{3,2},{4,5},{5,4},{6,7},{7,6},{8,9},{9,8},{10,11... | collective-permute-start | bytes 1572872 | tf_op jit(solution)/shard_map/ppermute | solution.py:287
  44.1 1.7 %collective-permute-start.1 = (f32[2,128,256]{2,1,0:T(8,128)S(1)}, f32[2,128,256]{2,1,0:T(8,128)S(1)}, u32[]{:S(2)}, u32[]{:S(2)}) collective-permute-start(f32[2,128,256]{2,1,0:T(8,128)S(1)} %get-tuple-element.25), channel_id=1, source_target_pairs={{0,1},{1,0},{2,3},{3,2},{4,5},{5,4},{6,7},{7,6},{8,9},{9,8},{10,11... | collective-permute-start | bytes 786440 | tf_op jit(solution)/shard_map/ppermute | solution.py:289
  78.2 19.2 %all-to-all-start.2 = ((f32[128,4,128]{2,1,0:T(4,128)}), f32[128,4,128]{2,1,0:T(4,128)S(1)}, u32[]{:S(2)}, u32[]{:S(2)}) async-start(f32[128,4,128]{2,1,0:T(4,128)} %broadcast_in_dim.23), calls=%async_computation.2 | async-start | bytes 524288 | tf_op jit(solution)/shard_map/all_to_all | solution.py:302
  85.2 15.8 %collective-permute-start.3 = (f32[256,256]{1,0:T(8,128)S(1)}, f32[256,256]{1,0:T(8,128)S(1)}, u32[]{:S(2)}, u32[]{:S(2)}) collective-permute-start(f32[256,256]{1,0:T(8,128)S(1)} %get-tuple-element.26), channel_id=1, source_target_pairs={{0,1},{1,0},{2,3},{3,2},{4,5},{5,4},{6,7},{7,6},{8,9},{9,8},{10,11... | collective-permute-start | bytes 786440 | tf_op jit(solution)/shard_map/ppermute | solution.py:318
  97.9 4.3 %collective-permute-start.2 = (f32[2,128,256]{2,1,0:T(8,128)S(1)}, f32[2,128,256]{2,1,0:T(8,128)S(1)}, u32[]{:S(2)}, u32[]{:S(2)}) collective-permute-start(f32[2,128,256]{2,1,0:T(8,128)S(1)} %reshape.78.mine_ref), channel_id=1, source_target_pairs={{0,1},{1,0},{2,3},{3,2},{4,5},{5,4},{6,7},{7,6},{8,9},{9,8},{10,11... | collective-permute-start | bytes 786440 | tf_op jit(solution)/shard_map/ppermute | solution.py:310

commit v9 on v8

--- a/solution.py
+++ b/solution.py
@@ -155,8 +155,60 @@
     lax.fori_loop(0, n, column, 0)
 
 
-def ritz_kernel(
+def join(target_ref, mine_ref, other_ref, plane):
+    rows = mine_ref.shape[1]
+    me_blk = lax.axis_index("blk")
+    target_ref[pl.ds(pl.multiple_of(me_blk * rows, rows), rows), :] = mine_ref[plane]
+    target_ref[pl.ds(pl.multiple_of((1 - me_blk) * rows, rows), rows), :] = other_ref[plane]
+
+
+def inverse_kernel(mine_ref, other_ref, inverse_ref, gram_ref, rest_ref):
+    n = mine_ref.shape[2]
+    join(gram_ref, mine_ref, other_ref, 0)
+    row = lax.broadcasted_iota(jnp.int32, (n, n), 0)
+    col = lax.broadcasted_iota(jnp.int32, (n, n), 1)
+    eye = jnp.where(row == col, 1.0, 0.0)
+    weight = jnp.where(row > col, 1.0, 0.5 * eye)
+    gram = gram_ref[...]
+    gram = 0.5 * (gram + gram.T)
+    gram_ref[...] = gram
+    on_diag = jnp.where(row == col, gram, 0.0)
+    down = lax.rsqrt(jnp.sum(on_diag, axis=1, keepdims=True))
+    across = lax.rsqrt(jnp.sum(on_diag, axis=0, keepdims=True))
+    rest = jnp.where(row == col, 0.0, gram * down * across)
+    rest_ref[...] = rest
+    lead = weight * rest
+    off = weight * short(lead, lead, 1) + short(lead, lead, 0) - lead
+    left = rest + off + short(off, rest, 0)
+    step = weight * (left + off.T + short(left, off, 1))
+    off = off - step - short(step, off, 0)
+    inverse_ref[...] = off
+
+    def going(state):
+        step, size = state
+        return jnp.logical_and(step < MAX_STEPS, jnp.logical_not(size < RESIDUAL))
+
+    def correct(state):
+        step, _ = state
+        off = inverse_ref[...]
+        rest = rest_ref[...]
+        left = rest + off + long(off, rest, 0)
+        error = left + off.T + long(left, off, 1)
+        change = weight * error
+        inverse_ref[...] = off - change - short(change, off, 0)
+        return step + 1, jnp.sum(error * error)
+
+    _, size = lax.while_loop(going, correct, (jnp.int32(0), jnp.float32(1.0)))
+    inverse_ref[...] = (eye + inverse_ref[...]) * across
+
+    @pl.when(jnp.logical_not(size < RESIDUAL))
+    def _():
+        eliminate(gram_ref, inverse_ref)
+
+
+def rotate_kernel(
     scale,
+    inverse_ref,
     mine_ref,
     other_ref,
     image_ref,
@@ -164,63 +216,16 @@
     rotated_hbm,
     projected_hbm,
     gram_ref,
-    inverse_ref,
     rotated_ref,
     projected_ref,
     sems,
 ):
-    rows, n = mine_ref.shape[1:]
-    me_blk = lax.axis_index("blk")
-    own = pl.ds(pl.multiple_of(me_blk * rows, rows), rows)
-    far = pl.ds(pl.multiple_of((1 - me_blk) * rows, rows), rows)
-    for plane in range(2):
-        gram_ref[plane, own, :] = mine_ref[plane]
-        gram_ref[plane, far, :] = other_ref[plane]
-    row = lax.broadcasted_iota(jnp.int32, (n, n), 0)
-    col = lax.broadcasted_iota(jnp.int32, (n, n), 1)
-    eye = jnp.where(row == col, 1.0, 0.0)
-    weight = jnp.where(row > col, 1.0, 0.5 * eye)
-    gram = gram_ref[0]
-    gram = 0.5 * (gram + gram.T)
-    projected_ref[...] = gram
-    on_diag = jnp.where(row == col, gram, 0.0)
-    down = lax.rsqrt(jnp.sum(on_diag, axis=1, keepdims=True))
-    across = lax.rsqrt(jnp.sum(on_diag, axis=0, keepdims=True))
-    rest = jnp.where(row == col, 0.0, gram * down * across)
-    gram_ref[0] = rest
-    off = -weight * rest
-    for _ in range(2):
-        left = rest + off + short(off, rest, 0)
-        step = weight * (left + off.T + short(left, off, 1))
-        off = off - step - short(step, off, 0)
-    inverse_ref[...] = off
-
-    def going(state):
-        step, size = state
-        return jnp.logical_and(step < MAX_STEPS, jnp.logical_not(size < RESIDUAL))
-
-    def correct(state):
-        step, _ = state
-        off = inverse_ref[...]
-        rest = gram_ref[0]
-        left = rest + off + long(off, rest, 0)
-        error = left + off.T + long(left, off, 1)
-        change = weight * error
-        inverse_ref[...] = off - change - short(change, off, 0)
-        return step + 1, jnp.sum(error * error)
-
-    _, size = lax.while_loop(going, correct, (jnp.int32(0), jnp.float32(1.0)))
-    inverse_ref[...] = (eye + inverse_ref[...]) * across
-
-    @pl.when(jnp.logical_not(size < RESIDUAL))
-    def _():
-        eliminate(projected_ref, inverse_ref)
-
+    join(gram_ref, mine_ref, other_ref, 1)
     inverse = inverse_ref[...]
     rotated_ref[...] = scale * long(image_ref[...] + extra_ref[...], inverse, 1)
     first = pltpu.make_async_copy(rotated_ref, rotated_hbm, sems.at[0])
     first.start()
-    projected_ref[...] = long(long(inverse, gram_ref[1], 0), inverse, 1)
+    projected_ref[...] = long(long(inverse, gram_ref[...], 0), inverse, 1)
     second = pltpu.make_async_copy(projected_ref, projected_hbm, sems.at[1])
     second.start()
     first.wait()
@@ -232,21 +237,27 @@
     vmem = pl.BlockSpec(memory_space=pltpu.VMEM)
     hbm = pl.BlockSpec(memory_space=pltpu.HBM)
     square = jax.ShapeDtypeStruct((n, n), jnp.float32)
+    params = pltpu.CompilerParams(vmem_limit_bytes=16 << 20)
+    spare = pltpu.VMEM((n, n), jnp.float32)
+    inverse = pl.pallas_call(
+        inverse_kernel,
+        out_shape=square,
+        in_specs=[vmem] * 2,
+        out_specs=vmem,
+        scratch_shapes=[spare, spare],
+        compiler_params=params,
+        cost_estimate=pl.CostEstimate(flops=3000000000, bytes_accessed=1 << 20, transcendentals=512),
+        name="inverse",
+    )(mine, other)
     return pl.pallas_call(
-        functools.partial(ritz_kernel, scale),
+        functools.partial(rotate_kernel, scale),
         out_shape=(square, square),
-        in_specs=[vmem] * 4,
+        in_specs=[vmem] * 5,
         out_specs=(hbm, hbm),
-        scratch_shapes=[
-            pltpu.VMEM((2, n, n), jnp.float32),
-            pltpu.VMEM((n, n), jnp.float32),
-            pltpu.VMEM((n, n), jnp.float32),
-            pltpu.VMEM((n, n), jnp.float32),
-            pltpu.SemaphoreType.DMA((2,)),
-        ],
-        compiler_params=pltpu.CompilerParams(vmem_limit_bytes=16 << 20),
-        name="ritz",
-    )(mine, other, image, extra)
+        scratch_shapes=[spare, spare, spare, pltpu.SemaphoreType.DMA((2,))],
+        compiler_params=params,
+        name="rotate",
+    )(inverse, mine, other, image, extra)
 
 
 def to_pieces(planes):
@@ -306,6 +317,7 @@
         concat_axis=0,
         tiled=True,
     )
+    spread, back, me_blk = lax.optimization_barrier((spread, back, me_blk))
     mine_grams = from_pieces(spread)
     other_grams = lax.ppermute(mine_grams, "blk", SWAP)
     image = jnp.einsum(
@@ -313,11 +325,11 @@
         picks,
         back[:, :, :width].reshape(-1, width),
         preferred_element_type=jnp.float32,
-    ).reshape(2, rows_dev // 2, width)
-    image_k = lax.dynamic_index_in_dim(image, me_blk, 0, keepdims=False)
-    extra_k = lax.ppermute(
-        lax.dynamic_index_in_dim(image, 1 - me_blk, 0, keepdims=False), "blk", SWAP
-    )
+    )
+    rows_core = rows_dev // 2
+    image_k = lax.dynamic_slice_in_dim(image, me_blk * rows_core, rows_core, 0)
+    extra_k = lax.dynamic_slice_in_dim(image, (1 - me_blk) * rows_core, rows_core, 0)
+    extra_k = lax.ppermute(extra_k, "blk", SWAP)
     return ritz(mine_grams, other_grams, image_k, extra_k, math.sqrt(rows_dev * n_sub))
 
 

time: 154 us -> 152 us (0.987)
  blocking collectives: 66.5 us -> 85 us
  waiting for transfers between devices: 12.2 us -> 0.72 us
  starting transfers between devices: 14.3 us -> 6.31 us
    all_to_all x0 -> x1, blocking collectives: none -> 18.5 us  [per_device(): lax.all_to_all(jnp.broadcast_to(total[None], (n_sub, 4, lanes)), 'sub', s...]
    all_to_all x1 -> x0, waiting for transfers between devices: 10.5 us -> none  [per_device(): lax.all_to_all(jnp.broadcast_to(total[None], (n_sub, 4, lanes)), 'sub', s...]
    all_to_all x1 -> x0, starting transfers between devices: 6.36 us -> none  [per_device(): lax.all_to_all(jnp.broadcast_to(total[None], (n_sub, 4, lanes)), 'sub', s...]
    ppermute x1, starting transfers between devices: 1.8 us -> 0.1 us  [per_device(): extra_k = lax.ppermute(extra_k, 'blk', SWAP)]
    pallas_call x1 -> x2, Pallas kernels: 51.1 us -> 51 us  [the longest x1 49.5 us: ritz(): pl.pallas_call(inverse_kernel, out_shape=square, in_specs=[vmem] * 2, out...]
  transfers between devices with their start and end apart: 5 -> 4, of which waited for: 3 -> 2; matrix products, arithmetic and copies ran while one was open for 1% -> 1% of each run, Pallas kernels for 1% -> 33%
where the time goes in v9:
time: 152 us
  blocking collectives  85 us (56%)
  Pallas kernels  53.6 us (35%)
  starting transfers between devices  6.31 us (4%)
  local copies, waits for them, and re-layouts  2.16 us (1%)
  other arithmetic  1.86 us (1%)
    pallas_call x1, Pallas kernels, ritz(): pl.pallas_call(inverse_kernel, out_shape=square, in_specs=[vmem] * 2, out...  49.5 us
    all_to_all x1, blocking collectives, per_device(): lax.all_to_all(sent.reshape(n_sub, cap_half, width), 'sub', split_axis=0,...  35.4 us
    all_to_all x1, blocking collectives, per_device(): lax.all_to_all(jnp.concatenate([outgoing, terms], axis=2), 'sub', split_a...  31.1 us
    all_to_all x1, blocking collectives, per_device(): lax.all_to_all(jnp.broadcast_to(total[None], (n_sub, 4, lanes)), 'sub', s...  18.5 us
    ppermute x1, starting transfers between devices, per_device(): other_grams = lax.ppermute(mine_grams, 'blk', SWAP)  3.1 us
  transfers between devices with their start and end apart: 4, of which 2 were waited for; matrix products, arithmetic and copies ran while one was open for 1% of the time, Pallas kernels for 33%

profile of v9, /device:TPU:1, one launch (start us, length us, event | category | flops | bytes accessed | tf_op | source)
XLA Modules:
  0.0 152.0 jit_solution(17604273845394838041)
XLA Ops:
  0.7 0.7 constant_dynamic-slice_fusion.2
  1.6 0.5 fusion.2
  2.1 35.4 %all_to_all.15 = bf16[128,8,256]{2,1,0:T(8,128)(2,1)S(1)} all-to-all(bf16[128,8,256]{2,1,0:T(8,128)(2,1)S(1)} %bitcast.27), channel_id=1, replica_groups=mesh['sub'=128,'blk'=2] {'sub'}, dimensions={0} | all-to-all | bytes 1048576 | tf_op jit(solution)/shard_map/all_to_all | solution.py:289
  37.8 0.4 fusion.6
  38.1 0.2 bitcast_select_fusion.mine_ref
  38.3 2.6 %collective-permute-start = (bf16[2,512,256]{2,1,0:T(8,128)(2,1)S(1)}, bf16[2,512,256]{2,1,0:T(8,128)(2,1)S(1)}, u32[]{:S(2)}, u32[]{:S(2)}) collective-permute-start(bf16[2,512,256]{2,1,0:T(8,128)(2,1)S(1)} %bitcast_select_fusion.mine_ref), channel_id=1, source_target_pairs={{0,1},{1,0},{2,3},{3,2},{4,5},{5,4},{6,7},{7,6},{8,9},{9,8},{10,11... | collective-permute-start | bytes 1572872 | tf_op jit(solution)/shard_map/ppermute | solution.py:298
  40.9 0.5 own_mass.1.mass_own_ref
  41.4 0.5 own_stiff.1
  41.8 0.6 collective-permute-done.other_ref
  42.4 1.6 %far_half.1 = (bf16[2,512,256]{2,1,0:T(8,128)(2,1)S(1)}, f32[2,128,256]{2,1,0:T(8,128)S(1)}, f32[2,128,256]{2,1,0:T(8,128)S(1)}) custom-call(s32[2]{0:T(128)S(1)} %copy-done.3, f32[2,512,256]{2,1,0:T(8,128)S(1)} %get-tuple-element.24.stiff_own_ref, f32[2,512,256]{2,1,0:T(8,128)S(1)} %own_mass.1.mass_own_ref, ...), custom_call_target="tpu_custom_call" | custom-call | flops 810000000 | bytes 4194304 | tf_op jit(solution)/shard_map/far_half/pallas_call | solution.py:123
  44.0 0.5 collective-permute-start.1
  44.6 0.3 copy.22
  44.9 0.9 fusion.5
  46.0 0.2 copy.17
  46.3 31.1 %all_to_all.16 = bf16[128,8,384]{2,1,0:T(8,128)(2,1)S(1)} all-to-all(bf16[128,8,384]{2,1,0:T(8,128)(2,1)S(1)} %pad_maximum_fusion), channel_id=1, replica_groups=mesh['sub'=128,'blk'=2] {'sub'}, dimensions={0} | all-to-all | bytes 1572864 | tf_op jit(solution)/shard_map/all_to_all | solution.py:304
  77.4 0.1 convert_reduce_fusion
  77.6 18.5 %all_to_all.17 = f32[128,4,128]{2,1,0:T(4,128)S(1)} all-to-all(f32[128,4,128]{2,1,0:T(4,128)S(1)} %broadcast_in_dim.23), channel_id=1, replica_groups=mesh['sub'=128,'blk'=2] {'sub'}, dimensions={0} | all-to-all | bytes 524288 | tf_op jit(solution)/shard_map/all_to_all | solution.py:313
  96.1 0.2 copy.19
  96.3 0.2 reshape.59.mine_ref
  96.6 3.1 %collective-permute-start.2 = (f32[2,128,256]{2,1,0:T(8,128)S(1)}, f32[2,128,256]{2,1,0:T(8,128)S(1)}, u32[]{:S(2)}, u32[]{:S(2)}) collective-permute-start(f32[2,128,256]{2,1,0:T(8,128)S(1)} %reshape.59.mine_ref), channel_id=1, source_target_pairs={{0,1},{1,0},{2,3},{3,2},{4,5},{5,4},{6,7},{7,6},{8,9},{9,8},{10,11... | collective-permute-start | bytes 786440 | tf_op jit(solution)/shard_map/ppermute | solution.py:322
  99.7 0.9 fusion
  100.7 0.1 collective-permute-done.2.other_ref
  100.8 49.5 %inverse.1.inverse_ref = f32[256,256]{1,0:T(8,128)S(1)} custom-call(f32[2,128,256]{2,1,0:T(8,128)S(1)} %reshape.59.mine_ref, f32[2,128,256]{2,1,0:T(8,128)S(1)} %collective-permute-done.2.other_ref), custom_call_target="tpu_custom_call" | custom-call | flops 3000000000 | bytes 1048576 | tf_op jit(solution)/shard_map/inverse/pallas_call | solution.py:242
  150.3 1.6 %rotate.1 = (f32[256,256]{1,0:T(8,128)}, f32[256,256]{1,0:T(8,128)}) custom-call(f32[256,256]{1,0:T(8,128)S(1)} %inverse.1.inverse_ref, f32[2,128,256]{2,1,0:T(8,128)S(1)} %reshape.59.mine_ref, f32[2,128,256]{2,1,0:T(8,128)S(1)} %collective-permute-done.2.other_ref, f32[256,256]{1,0:T(8,128)S(1)} %get-tuple-element.33.image_ref, ...), custom_call_target="tpu_custom_call" | custom-call | tf_op jit(solution)/shard_map/rotate/pallas_call | solution.py:252
  (25 shorter events, 0.9 us)
Async XLA Ops:
  0.6 1.0 copy-start
  0.6 37.0 %copy-start.3 = (s32[2]{0:T(128)S(1)}, s32[2]{0:T(128)}, u32[]{:S(2)}) copy-start(s32[2]{0:T(128)} %counts_ref) | copy-start | bytes 28
  2.1 38.8 %copy-start.2 = (bf16[2,512,1024]{2,1,0:T(8,128)(2,1)S(1)}, bf16[2,512,1024]{2,1,0:T(8,128)(2,1)}, u32[]{:S(2)}) copy-start(bf16[2,512,1024]{2,1,0:T(8,128)(2,1)} %mass_ref.1) | copy-start | bytes 6291460
  38.3 3.0 %copy-start.1 = (bf16[2,512,1024]{2,1,0:T(8,128)(2,1)S(1)}, bf16[2,512,1024]{2,1,0:T(8,128)(2,1)}, u32[]{:S(2)}) copy-start(bf16[2,512,1024]{2,1,0:T(8,128)(2,1)} %stiff_ref.1) | copy-start | bytes 6291460
  38.3 4.1 %collective-permute-start = (bf16[2,512,256]{2,1,0:T(8,128)(2,1)S(1)}, bf16[2,512,256]{2,1,0:T(8,128)(2,1)S(1)}, u32[]{:S(2)}, u32[]{:S(2)}) collective-permute-start(bf16[2,512,256]{2,1,0:T(8,128)(2,1)S(1)} %bitcast_select_fusion.mine_ref), channel_id=1, source_target_pairs={{0,1},{1,0},{2,3},{3,2},{4,5},{5,4},{6,7},{7,6},{8,9},{9,8},{10,11... | collective-permute-start | bytes 1572872 | tf_op jit(solution)/shard_map/ppermute | solution.py:298
  44.0 1.8 %collective-permute-start.1 = (f32[2,128,256]{2,1,0:T(8,128)S(1)}, f32[2,128,256]{2,1,0:T(8,128)S(1)}, u32[]{:S(2)}, u32[]{:S(2)}) collective-permute-start(f32[2,128,256]{2,1,0:T(8,128)S(1)} %get-tuple-element.28), channel_id=1, source_target_pairs={{0,1},{1,0},{2,3},{3,2},{4,5},{5,4},{6,7},{7,6},{8,9},{9,8},{10,11... | collective-permute-start | bytes 786440 | tf_op jit(solution)/shard_map/ppermute | solution.py:300
  96.6 4.3 %collective-permute-start.2 = (f32[2,128,256]{2,1,0:T(8,128)S(1)}, f32[2,128,256]{2,1,0:T(8,128)S(1)}, u32[]{:S(2)}, u32[]{:S(2)}) collective-permute-start(f32[2,128,256]{2,1,0:T(8,128)S(1)} %reshape.59.mine_ref), channel_id=1, source_target_pairs={{0,1},{1,0},{2,3},{3,2},{4,5},{5,4},{6,7},{7,6},{8,9},{9,8},{10,11... | collective-permute-start | bytes 786440 | tf_op jit(solution)/shard_map/ppermute | solution.py:322
  100.6 49.7 %collective-permute-start.3 = (f32[256,256]{1,0:T(8,128)S(1)}, f32[256,256]{1,0:T(8,128)S(1)}, u32[]{:S(2)}, u32[]{:S(2)}) collective-permute-start(f32[256,256]{1,0:T(8,128)S(1)} %get-tuple-element.32), channel_id=1, source_target_pairs={{0,1},{1,0},{2,3},{3,2},{4,5},{5,4},{6,7},{7,6},{8,9},{9,8},{10,11... | collective-permute-start | bytes 786440 | tf_op jit(solution)/shard_map/ppermute | solution.py:332

commit v10 on v9

--- a/solution.py
+++ b/solution.py
@@ -156,14 +156,20 @@
 
 
 def join(target_ref, mine_ref, other_ref, plane):
-    rows = mine_ref.shape[1]
+    pieces, _, lanes = mine_ref.shape
+    rows = pieces // 2
     me_blk = lax.axis_index("blk")
-    target_ref[pl.ds(pl.multiple_of(me_blk * rows, rows), rows), :] = mine_ref[plane]
-    target_ref[pl.ds(pl.multiple_of((1 - me_blk) * rows, rows), rows), :] = other_ref[plane]
+    for side, ref in ((me_blk, mine_ref), (1 - me_blk, other_ref)):
+        for r in range(2):
+            start = pl.multiple_of(side * pieces + r * rows, rows)
+            for part in range(2):
+                target_ref[pl.ds(start, rows), part * lanes : (part + 1) * lanes] = ref[
+                    part * rows : (part + 1) * rows, 2 * plane + r, :
+                ]
 
 
 def inverse_kernel(mine_ref, other_ref, inverse_ref, gram_ref, rest_ref):
-    n = mine_ref.shape[2]
+    n = gram_ref.shape[0]
     join(gram_ref, mine_ref, other_ref, 0)
     row = lax.broadcasted_iota(jnp.int32, (n, n), 0)
     col = lax.broadcasted_iota(jnp.int32, (n, n), 1)
@@ -233,7 +239,7 @@
 
 
 def ritz(mine, other, image, extra, scale):
-    n = mine.shape[2]
+    n = image.shape[1]
     vmem = pl.BlockSpec(memory_space=pltpu.VMEM)
     hbm = pl.BlockSpec(memory_space=pltpu.HBM)
     square = jax.ShapeDtypeStruct((n, n), jnp.float32)
@@ -264,12 +270,6 @@
     n, rows, wide = planes.shape
     pieces = planes.reshape(n, 2, rows // 2, 2, wide // 2).transpose(3, 2, 0, 1, 4)
     return pieces.reshape(rows, 2 * n, wide // 2)
-
-
-def from_pieces(pieces):
-    rows, double, lanes = pieces.shape
-    planes = pieces.reshape(2, rows // 2, double // 2, 2, lanes).transpose(2, 3, 1, 0, 4)
-    return planes.reshape(double // 2, rows, 2 * lanes)
 
 
 def per_device(basis, stiffness, mass, owner_rows, counts):
@@ -318,8 +318,8 @@
         tiled=True,
     )
     spread, back, me_blk = lax.optimization_barrier((spread, back, me_blk))
-    mine_grams = from_pieces(spread)
-    other_grams = lax.ppermute(mine_grams, "blk", SWAP)
+    other_grams = lax.ppermute(spread, "blk", SWAP)
+
     image = jnp.einsum(
         "tr,tc->rc",
         picks,
@@ -330,7 +330,7 @@
     image_k = lax.dynamic_slice_in_dim(image, me_blk * rows_core, rows_core, 0)
     extra_k = lax.dynamic_slice_in_dim(image, (1 - me_blk) * rows_core, rows_core, 0)
     extra_k = lax.ppermute(extra_k, "blk", SWAP)
-    return ritz(mine_grams, other_grams, image_k, extra_k, math.sqrt(rows_dev * n_sub))
+    return ritz(spread, other_grams, image_k, extra_k, math.sqrt(rows_dev * n_sub))
 
 
 def solution(mesh):

time: 152 us -> 152 us (level)
  no operation moved by 1% of the time
where the time goes in v10:
time: 152 us
  blocking collectives  85 us (56%)
  Pallas kernels  53.6 us (35%)
  starting transfers between devices  6.21 us (4%)
  other arithmetic  1.86 us (1%)
  local copies, waits for them, and re-layouts  1.73 us (1%)
    pallas_call x1, Pallas kernels, ritz(): pl.pallas_call(inverse_kernel, out_shape=square, in_specs=[vmem] * 2, out...  49.6 us
    all_to_all x1, blocking collectives, per_device(): lax.all_to_all(sent.reshape(n_sub, cap_half, width), 'sub', split_axis=0,...  35.4 us
    all_to_all x1, blocking collectives, per_device(): lax.all_to_all(jnp.concatenate([outgoing, terms], axis=2), 'sub', split_a...  31.1 us
    all_to_all x1, blocking collectives, per_device(): lax.all_to_all(jnp.broadcast_to(total[None], (n_sub, 4, lanes)), 'sub', s...  18.5 us
  transfers between devices with their start and end apart: 4, of which 2 were waited for; matrix products, arithmetic and copies ran while one was open for 1% of the time, Pallas kernels for 33%

profile of v10, /device:TPU:1, one launch (start us, length us, event | category | flops | bytes accessed | tf_op | source)
XLA Modules:
  0.0 151.6 jit_solution(11662637552344644359)
XLA Ops:
  0.7 0.7 constant_dynamic-slice_fusion.2
  1.4 0.1 copy.12
  1.6 0.5 fusion.2
  2.1 35.4 %all_to_all.15 = bf16[128,8,256]{2,1,0:T(8,128)(2,1)S(1)} all-to-all(bf16[128,8,256]{2,1,0:T(8,128)(2,1)S(1)} %bitcast.23), channel_id=1, replica_groups=mesh['sub'=128,'blk'=2] {'sub'}, dimensions={0} | all-to-all | bytes 1048576 | tf_op jit(solution)/shard_map/all_to_all | solution.py:289
  37.6 0.1 copy.20
  37.8 0.4 fusion.6
  38.1 0.2 bitcast_select_fusion.mine_ref
  38.3 2.6 %collective-permute-start = (bf16[2,512,256]{2,1,0:T(8,128)(2,1)S(1)}, bf16[2,512,256]{2,1,0:T(8,128)(2,1)S(1)}, u32[]{:S(2)}, u32[]{:S(2)}) collective-permute-start(bf16[2,512,256]{2,1,0:T(8,128)(2,1)S(1)} %bitcast_select_fusion.mine_ref), channel_id=1, source_target_pairs={{0,1},{1,0},{2,3},{3,2},{4,5},{5,4},{6,7},{7,6},{8,9},{9,8},{10,11... | collective-permute-start | bytes 1572872 | tf_op jit(solution)/shard_map/ppermute | solution.py:298
  40.9 0.5 own_mass.1.mass_own_ref
  41.4 0.5 own_stiff.1
  41.8 0.6 collective-permute-done.other_ref
  42.4 1.6 %far_half.1 = (bf16[2,512,256]{2,1,0:T(8,128)(2,1)S(1)}, f32[2,128,256]{2,1,0:T(8,128)S(1)}, f32[2,128,256]{2,1,0:T(8,128)S(1)}) custom-call(s32[2]{0:T(128)S(1)} %copy-done.3, f32[2,512,256]{2,1,0:T(8,128)S(1)} %get-tuple-element.24.stiff_own_ref, f32[2,512,256]{2,1,0:T(8,128)S(1)} %own_mass.1.mass_own_ref, ...), custom_call_target="tpu_custom_call" | custom-call | flops 810000000 | bytes 4194304 | tf_op jit(solution)/shard_map/far_half/pallas_call | solution.py:123
  44.0 0.5 collective-permute-start.1
  44.6 0.3 copy.19
  44.9 0.9 fusion.5
  46.0 0.2 copy.16
  46.3 31.1 %all_to_all.16 = bf16[128,8,384]{2,1,0:T(8,128)(2,1)S(1)} all-to-all(bf16[128,8,384]{2,1,0:T(8,128)(2,1)S(1)} %pad_maximum_fusion), channel_id=1, replica_groups=mesh['sub'=128,'blk'=2] {'sub'}, dimensions={0} | all-to-all | bytes 1572864 | tf_op jit(solution)/shard_map/all_to_all | solution.py:304
  77.4 0.1 convert_reduce_fusion
  77.6 18.5 %all_to_all.17.mine_ref = f32[128,4,128]{2,1,0:T(4,128)S(1)} all-to-all(f32[128,4,128]{2,1,0:T(4,128)S(1)} %broadcast_in_dim.23), channel_id=1, replica_groups=mesh['sub'=128,'blk'=2] {'sub'}, dimensions={0} | all-to-all | bytes 524288 | tf_op jit(solution)/shard_map/all_to_all | solution.py:313
  96.1 3.0 %collective-permute-start.2 = (f32[128,4,128]{2,1,0:T(4,128)S(1)}, f32[128,4,128]{2,1,0:T(4,128)S(1)}, u32[]{:S(2)}, u32[]{:S(2)}) collective-permute-start(f32[128,4,128]{2,1,0:T(4,128)S(1)} %all_to_all.17.mine_ref), channel_id=1, source_target_pairs={{0,1},{1,0},{2,3},{3,2},{4,5},{5,4},{6,7},{7,6},{8,9},{9,8},{10,11... | collective-permute-start | bytes 786440 | tf_op jit(solution)/shard_map/ppermute | solution.py:321
  99.1 0.9 fusion
  100.2 0.1 collective-permute-done.2.other_ref
  100.3 49.6 %inverse.1.inverse_ref = f32[256,256]{1,0:T(8,128)S(1)} custom-call(f32[128,4,128]{2,1,0:T(4,128)S(1)} %all_to_all.17.mine_ref, f32[128,4,128]{2,1,0:T(4,128)S(1)} %collective-permute-done.2.other_ref), custom_call_target="tpu_custom_call" | custom-call | flops 3000000000 | bytes 1048576 | tf_op jit(solution)/shard_map/inverse/pallas_call | solution.py:248
  149.9 1.6 %rotate.1 = (f32[256,256]{1,0:T(8,128)}, f32[256,256]{1,0:T(8,128)}) custom-call(f32[256,256]{1,0:T(8,128)S(1)} %inverse.1.inverse_ref, f32[128,4,128]{2,1,0:T(4,128)S(1)} %all_to_all.17.mine_ref, f32[128,4,128]{2,1,0:T(4,128)S(1)} %collective-permute-done.2.other_ref, f32[256,256]{1,0:T(8,128)S(1)} %get-tuple-element.33.image_ref, ...), custom_call_target="tpu_custom_call" | custom-call | tf_op jit(solution)/shard_map/rotate/pallas_call | solution.py:258
  (22 shorter events, 0.7 us)
Async XLA Ops:
  0.6 1.0 copy-start
  0.6 37.0 %copy-start.3 = (s32[2]{0:T(128)S(1)}, s32[2]{0:T(128)}, u32[]{:S(2)}) copy-start(s32[2]{0:T(128)} %counts_ref) | copy-start | bytes 28
  2.1 38.8 %copy-start.2 = (bf16[2,512,1024]{2,1,0:T(8,128)(2,1)S(1)}, bf16[2,512,1024]{2,1,0:T(8,128)(2,1)}, u32[]{:S(2)}) copy-start(bf16[2,512,1024]{2,1,0:T(8,128)(2,1)} %mass_ref.1) | copy-start | bytes 6291460
  38.3 3.0 %copy-start.1 = (bf16[2,512,1024]{2,1,0:T(8,128)(2,1)S(1)}, bf16[2,512,1024]{2,1,0:T(8,128)(2,1)}, u32[]{:S(2)}) copy-start(bf16[2,512,1024]{2,1,0:T(8,128)(2,1)} %stiff_ref.1) | copy-start | bytes 6291460
  38.3 4.1 %collective-permute-start = (bf16[2,512,256]{2,1,0:T(8,128)(2,1)S(1)}, bf16[2,512,256]{2,1,0:T(8,128)(2,1)S(1)}, u32[]{:S(2)}, u32[]{:S(2)}) collective-permute-start(bf16[2,512,256]{2,1,0:T(8,128)(2,1)S(1)} %bitcast_select_fusion.mine_ref), channel_id=1, source_target_pairs={{0,1},{1,0},{2,3},{3,2},{4,5},{5,4},{6,7},{7,6},{8,9},{9,8},{10,11... | collective-permute-start | bytes 1572872 | tf_op jit(solution)/shard_map/ppermute | solution.py:298
  44.0 1.8 %collective-permute-start.1 = (f32[2,128,256]{2,1,0:T(8,128)S(1)}, f32[2,128,256]{2,1,0:T(8,128)S(1)}, u32[]{:S(2)}, u32[]{:S(2)}) collective-permute-start(f32[2,128,256]{2,1,0:T(8,128)S(1)} %get-tuple-element.28), channel_id=1, source_target_pairs={{0,1},{1,0},{2,3},{3,2},{4,5},{5,4},{6,7},{7,6},{8,9},{9,8},{10,11... | collective-permute-start | bytes 786440 | tf_op jit(solution)/shard_map/ppermute | solution.py:300
  96.1 4.2 %collective-permute-start.2 = (f32[128,4,128]{2,1,0:T(4,128)S(1)}, f32[128,4,128]{2,1,0:T(4,128)S(1)}, u32[]{:S(2)}, u32[]{:S(2)}) collective-permute-start(f32[128,4,128]{2,1,0:T(4,128)S(1)} %all_to_all.17.mine_ref), channel_id=1, source_target_pairs={{0,1},{1,0},{2,3},{3,2},{4,5},{5,4},{6,7},{7,6},{8,9},{9,8},{10,11... | collective-permute-start | bytes 786440 | tf_op jit(solution)/shard_map/ppermute | solution.py:321
  100.1 49.8 %collective-permute-start.3 = (f32[256,256]{1,0:T(8,128)S(1)}, f32[256,256]{1,0:T(8,128)S(1)}, u32[]{:S(2)}, u32[]{:S(2)}) collective-permute-start(f32[256,256]{1,0:T(8,128)S(1)} %get-tuple-element.32), channel_id=1, source_target_pairs={{0,1},{1,0},{2,3},{3,2},{4,5},{5,4},{6,7},{7,6},{8,9},{9,8},{10,11... | collective-permute-start | bytes 786440 | tf_op jit(solution)/shard_map/ppermute | solution.py:332

commit v11 on v10

--- a/solution.py
+++ b/solution.py
@@ -58,6 +58,16 @@
         )
         if turned_ref is not None:
             turned_ref[:, s * half : (s + 1) * half] = mine_ref[s].T
+
+
+def scatter_pieces(target_ref, plane_rows, place):
+    pieces, _, lanes = target_ref.shape
+    rows = pieces // 2
+    for r in range(2):
+        for part in range(2):
+            target_ref[part * rows : (part + 1) * rows, 2 * place + r, :] = plane_rows[
+                r * rows : (r + 1) * rows, part * lanes : (part + 1) * lanes
+            ]
 
 
 def far_kernel(
@@ -91,8 +101,8 @@
         parts = parts_ref[...].reshape(sub_dev * half, width)
         gram = jnp.dot(turned_ref[...], parts, preferred_element_type=jnp.float32)
         low, high = gram[: width // 2], gram[width // 2 :]
-        keep_ref[place] = jnp.where(first, low, high)
-        send_ref[place] = jnp.where(first, high, low)
+        scatter_pieces(keep_ref, jnp.where(first, low, high), place)
+        scatter_pieces(send_ref, jnp.where(first, high, low), place)
 
 
 def products(counts, mine, other, stiffness, mass):
@@ -119,7 +129,7 @@
         cost_estimate=cost,
         name="own_mass",
     )(mine, mass)
-    gram = jax.ShapeDtypeStruct((2, width // 2, width), jnp.float32)
+    gram = jax.ShapeDtypeStruct((width // 2, 4, width // 2), jnp.float32)
     return pl.pallas_call(
         far_kernel,
         out_shape=(jax.ShapeDtypeStruct(mine.shape, jnp.bfloat16), gram, gram),
@@ -266,12 +276,6 @@
     )(inverse, mine, other, image, extra)
 
 
-def to_pieces(planes):
-    n, rows, wide = planes.shape
-    pieces = planes.reshape(n, 2, rows // 2, 2, wide // 2).transpose(3, 2, 0, 1, 4)
-    return pieces.reshape(rows, 2 * n, wide // 2)
-
-
 def per_device(basis, stiffness, mass, owner_rows, counts):
     n_sub = lax.axis_size("sub")
     me_sub = lax.axis_index("sub")
@@ -298,7 +302,7 @@
     other = lax.ppermute(mine, "blk", SWAP)
     stiff_part, keep, send = products(counts, mine, other, stiffness, mass)
     grams = keep + lax.ppermute(send, "blk", SWAP)
-    terms = to_pieces(jnp.concatenate(two_terms(grams)))
+    terms = jnp.concatenate(two_terms(grams), axis=1)
     outgoing = stiff_part.reshape(cap_half, n_sub, width).transpose(1, 0, 2)
     outgoing = jnp.roll(outgoing, me_sub, axis=0)
     back = lax.all_to_all(

time: 152 us -> 152 us (level)
  no operation moved by 1% of the time
where the time goes in v11:
time: 152 us
  blocking collectives  85 us (56%)
  Pallas kernels  53.9 us (35%)
  starting transfers between devices  6.21 us (4%)
  other arithmetic  2.03 us (1%)
    pallas_call x1, Pallas kernels, ritz(): pl.pallas_call(inverse_kernel, out_shape=square, in_specs=[vmem] * 2, out...  49.6 us
    all_to_all x1, blocking collectives, per_device(): lax.all_to_all(sent.reshape(n_sub, cap_half, width), 'sub', split_axis=0,...  35.4 us
    all_to_all x1, blocking collectives, per_device(): lax.all_to_all(jnp.concatenate([outgoing, terms], axis=2), 'sub', split_a...  31.1 us
    all_to_all x1, blocking collectives, per_device(): lax.all_to_all(jnp.broadcast_to(total[None], (n_sub, 4, lanes)), 'sub', s...  18.5 us
  transfers between devices with their start and end apart: 4, of which 2 were waited for; matrix products, arithmetic and copies ran while one was open for 1% of the time, Pallas kernels for 33%

profile of v11, /device:TPU:1, one launch (start us, length us, event | category | flops | bytes accessed | tf_op | source)
XLA Modules:
  0.0 151.7 jit_solution(70330531866853248)
XLA Ops:
  0.7 0.7 constant_dynamic-slice_fusion.2
  1.4 0.1 copy.11
  1.6 0.5 fusion.2
  2.1 35.4 %all_to_all.15 = bf16[128,8,256]{2,1,0:T(8,128)(2,1)S(1)} all-to-all(bf16[128,8,256]{2,1,0:T(8,128)(2,1)S(1)} %bitcast.19), channel_id=1, replica_groups=mesh['sub'=128,'blk'=2] {'sub'}, dimensions={0} | all-to-all | bytes 1048576 | tf_op jit(solution)/shard_map/all_to_all | solution.py:293
  37.8 0.4 fusion.6
  38.1 0.2 bitcast_select_fusion.mine_ref
  38.3 2.6 %collective-permute-start = (bf16[2,512,256]{2,1,0:T(8,128)(2,1)S(1)}, bf16[2,512,256]{2,1,0:T(8,128)(2,1)S(1)}, u32[]{:S(2)}, u32[]{:S(2)}) collective-permute-start(bf16[2,512,256]{2,1,0:T(8,128)(2,1)S(1)} %bitcast_select_fusion.mine_ref), channel_id=1, source_target_pairs={{0,1},{1,0},{2,3},{3,2},{4,5},{5,4},{6,7},{7,6},{8,9},{9,8},{10,11... | collective-permute-start | bytes 1572872 | tf_op jit(solution)/shard_map/ppermute | solution.py:302
  40.9 0.5 own_mass.1.mass_own_ref
  41.4 0.5 own_stiff.1
  41.8 0.6 collective-permute-done.other_ref
  42.4 1.8 %far_half.1 = (bf16[2,512,256]{2,1,0:T(8,128)(2,1)S(1)}, f32[128,4,128]{2,1,0:T(4,128)S(1)}, f32[128,4,128]{2,1,0:T(4,128)S(1)}) custom-call(s32[2]{0:T(128)S(1)} %copy-done.3, f32[2,512,256]{2,1,0:T(8,128)S(1)} %get-tuple-element.24.stiff_own_ref, f32[2,512,256]{2,1,0:T(8,128)S(1)} %own_mass.1.mass_own_ref, ...), custom_call_target="tpu_custom_call" | custom-call | flops 810000000 | bytes 4194304 | tf_op jit(solution)/shard_map/far_half/pallas_call | solution.py:133
  44.3 0.5 collective-permute-start.1
  44.8 0.3 copy.16
  45.1 0.9 fusion.5
  46.1 0.1 reduce-precision_convert_fusion
  46.2 0.2 maximum_maximum_fusion
  46.4 31.1 %all_to_all.16 = bf16[128,8,384]{2,1,0:T(8,128)(2,1)S(1)} all-to-all(bf16[128,8,384]{2,1,0:T(8,128)(2,1)S(1)} %maximum_maximum_fusion), channel_id=1, replica_groups=mesh['sub'=128,'blk'=2] {'sub'}, dimensions={0} | all-to-all | bytes 1572864 | tf_op jit(solution)/shard_map/all_to_all | solution.py:308
  77.5 0.1 convert_reduce_fusion
  77.7 18.5 %all_to_all.17.mine_ref = f32[128,4,128]{2,1,0:T(4,128)S(1)} all-to-all(f32[128,4,128]{2,1,0:T(4,128)S(1)} %broadcast_in_dim.23), channel_id=1, replica_groups=mesh['sub'=128,'blk'=2] {'sub'}, dimensions={0} | all-to-all | bytes 524288 | tf_op jit(solution)/shard_map/all_to_all | solution.py:317
  96.2 3.0 %collective-permute-start.2 = (f32[128,4,128]{2,1,0:T(4,128)S(1)}, f32[128,4,128]{2,1,0:T(4,128)S(1)}, u32[]{:S(2)}, u32[]{:S(2)}) collective-permute-start(f32[128,4,128]{2,1,0:T(4,128)S(1)} %all_to_all.17.mine_ref), channel_id=1, source_target_pairs={{0,1},{1,0},{2,3},{3,2},{4,5},{5,4},{6,7},{7,6},{8,9},{9,8},{10,11... | collective-permute-start | bytes 786440 | tf_op jit(solution)/shard_map/ppermute | solution.py:325
  99.2 0.9 fusion
  100.2 0.1 collective-permute-done.2.other_ref
  100.4 49.6 %inverse.1.inverse_ref = f32[256,256]{1,0:T(8,128)S(1)} custom-call(f32[128,4,128]{2,1,0:T(4,128)S(1)} %all_to_all.17.mine_ref, f32[128,4,128]{2,1,0:T(4,128)S(1)} %collective-permute-done.2.other_ref), custom_call_target="tpu_custom_call" | custom-call | flops 3000000000 | bytes 1048576 | tf_op jit(solution)/shard_map/inverse/pallas_call | solution.py:258
  149.9 1.6 %rotate.1 = (f32[256,256]{1,0:T(8,128)}, f32[256,256]{1,0:T(8,128)}) custom-call(f32[256,256]{1,0:T(8,128)S(1)} %inverse.1.inverse_ref, f32[128,4,128]{2,1,0:T(4,128)S(1)} %all_to_all.17.mine_ref, f32[128,4,128]{2,1,0:T(4,128)S(1)} %collective-permute-done.2.other_ref, f32[256,256]{1,0:T(8,128)S(1)} %get-tuple-element.33.image_ref, ...), custom_call_target="tpu_custom_call" | custom-call | tf_op jit(solution)/shard_map/rotate/pallas_call | solution.py:268
  (18 shorter events, 0.5 us)
Async XLA Ops:
  0.6 1.0 copy-start
  0.6 37.0 %copy-start.3 = (s32[2]{0:T(128)S(1)}, s32[2]{0:T(128)}, u32[]{:S(2)}) copy-start(s32[2]{0:T(128)} %counts_ref) | copy-start | bytes 28
  2.1 38.8 %copy-start.2 = (bf16[2,512,1024]{2,1,0:T(8,128)(2,1)S(1)}, bf16[2,512,1024]{2,1,0:T(8,128)(2,1)}, u32[]{:S(2)}) copy-start(bf16[2,512,1024]{2,1,0:T(8,128)(2,1)} %mass_ref.1) | copy-start | bytes 6291460
  38.3 3.0 %copy-start.1 = (bf16[2,512,1024]{2,1,0:T(8,128)(2,1)S(1)}, bf16[2,512,1024]{2,1,0:T(8,128)(2,1)}, u32[]{:S(2)}) copy-start(bf16[2,512,1024]{2,1,0:T(8,128)(2,1)} %stiff_ref.1) | copy-start | bytes 6291460
  38.3 4.1 %collective-permute-start = (bf16[2,512,256]{2,1,0:T(8,128)(2,1)S(1)}, bf16[2,512,256]{2,1,0:T(8,128)(2,1)S(1)}, u32[]{:S(2)}, u32[]{:S(2)}) collective-permute-start(bf16[2,512,256]{2,1,0:T(8,128)(2,1)S(1)} %bitcast_select_fusion.mine_ref), channel_id=1, source_target_pairs={{0,1},{1,0},{2,3},{3,2},{4,5},{5,4},{6,7},{7,6},{8,9},{9,8},{10,11... | collective-permute-start | bytes 1572872 | tf_op jit(solution)/shard_map/ppermute | solution.py:302
  44.3 1.8 %collective-permute-start.1 = (f32[128,4,128]{2,1,0:T(4,128)S(1)}, f32[128,4,128]{2,1,0:T(4,128)S(1)}, u32[]{:S(2)}, u32[]{:S(2)}) collective-permute-start(f32[128,4,128]{2,1,0:T(4,128)S(1)} %get-tuple-element.28), channel_id=1, source_target_pairs={{0,1},{1,0},{2,3},{3,2},{4,5},{5,4},{6,7},{7,6},{8,9},{9,8},{10,11... | collective-permute-start | bytes 786440 | tf_op jit(solution)/shard_map/ppermute | solution.py:304
  96.2 4.2 %collective-permute-start.2 = (f32[128,4,128]{2,1,0:T(4,128)S(1)}, f32[128,4,128]{2,1,0:T(4,128)S(1)}, u32[]{:S(2)}, u32[]{:S(2)}) collective-permute-start(f32[128,4,128]{2,1,0:T(4,128)S(1)} %all_to_all.17.mine_ref), channel_id=1, source_target_pairs={{0,1},{1,0},{2,3},{3,2},{4,5},{5,4},{6,7},{7,6},{8,9},{9,8},{10,11... | collective-permute-start | bytes 786440 | tf_op jit(solution)/shard_map/ppermute | solution.py:325
  100.1 49.8 %collective-permute-start.3 = (f32[256,256]{1,0:T(8,128)S(1)}, f32[256,256]{1,0:T(8,128)S(1)}, u32[]{:S(2)}, u32[]{:S(2)}) collective-permute-start(f32[256,256]{1,0:T(8,128)S(1)} %get-tuple-element.32), channel_id=1, source_target_pairs={{0,1},{1,0},{2,3},{3,2},{4,5},{5,4},{6,7},{7,6},{8,9},{9,8},{10,11... | collective-permute-start | bytes 786440 | tf_op jit(solution)/shard_map/ppermute | solution.py:336
